TPU v7x, 32 devices: a whole 2x2x4 slice. The times are simulated.
32 devices in a mesh: section: 2 (over x), dp: 4 (over z), mp: 4 (over y, core).
Axes of the slice: x: 2, y: 2, z: 4, core: 2. Of those that a mesh axis runs over, the one named last changes fastest.
Arguments:
- image: bfloat16 [16, 576, 768], P('dp', 'mp'), may hold values from -6 to 6
- text: bfloat16 [16, 800, 768], P('dp', 'mp'), may hold values from -6 to 6
- lengths: int32 [16], P('dp'), may hold values from 5 to 800, as said below
- image_cot: bfloat16 [16, 576, 768], P('dp', 'mp'), may hold values from -6 to 6
- text_cot: bfloat16 [16, 800, 768], P('dp', 'mp'), may hold values from -6 to 6
- qkv_image: bfloat16 [2, 768, 3, 768], P('section', None, None, 'mp'), may hold values from -0.21875 to 0.21875
- out_image: bfloat16 [2, 768, 768], P('section', 'mp'), may hold values from -0.875 to 0.875
- qkv_text: bfloat16 [2, 768, 3, 768], P('section', None, None, 'mp'), may hold values from -0.21875 to 0.21875
- out_text: bfloat16 [2, 768, 768], P('section', 'mp'), may hold values from -0.875 to 0.875
- query_cross: bfloat16 [2, 768, 768], P('section', None, 'mp'), may hold values from -0.21875 to 0.21875
- kv_cross: bfloat16 [2, 768, 2, 768], P('section', None, None, 'mp'), may hold values from -0.21875 to 0.21875
- out_cross: bfloat16 [2, 768, 768], P('section', 'mp'), may hold values from -0.875 to 0.875
- up_proj: bfloat16 [2, 768, 3072], P('section', None, 'mp'), may hold values from -0.21875 to 0.21875
- down_proj: bfloat16 [2, 3072, 768], P('section', 'mp'), may hold values from -0.21875 to 0.21875
- norm_gain: float32 [2, 2, 768], P('section'), may hold values from 0.1 to 1.9
- norm_bias: float32 [2, 2, 768], P('section'), may hold values from -2.4 to 2.4
Outputs:
- image_out: bfloat16 [2, 16, 576, 768], P('section', 'dp', 'mp')
- text_out: bfloat16 [2, 16, 800, 768], P('section', 'dp', 'mp')
- image_grad: float32 [2, 16, 576, 768], P('section', 'dp', 'mp')
- text_grad: float32 [2, 16, 800, 768], P('section', 'dp', 'mp')
- qkv_image_grad: float32 [2, 768, 3, 768], P('section', 'dp', None, 'mp')
- out_image_grad: float32 [2, 768, 768], P('section', ('mp', 'dp'))
- qkv_text_grad: float32 [2, 768, 3, 768], P('section', 'dp', None, 'mp')
- out_text_grad: float32 [2, 768, 768], P('section', ('mp', 'dp'))
- query_cross_grad: float32 [2, 768, 768], P('section', 'dp', 'mp')
- kv_cross_grad: float32 [2, 768, 2, 768], P('section', 'dp', None, 'mp')
- out_cross_grad: float32 [2, 768, 768], P('section', ('mp', 'dp'))
- up_proj_grad: float32 [2, 768, 3072], P('section', 'dp', 'mp')
- down_proj_grad: float32 [2, 3072, 768], P('section', ('mp', 'dp'))
- norm_gain_grad: float32 [2, 2, 768], P('section', None, ('dp', 'mp'))
- norm_bias_grad: float32 [2, 2, 768], P('section', None, ('dp', 'mp'))
Inputs may be any that keep to these rules, and one draw needn't show every extreme that they name: `lengths`: the answer length of each sample; the longest equals 800 in every draw.
All inputs are finite; a program needn't handle non-finite values.
Results may differ from a plain program's by a relative error of at most 0.033.
Values may be sent and summed in bfloat16 or wider, within the bound.
No kernel may reach another device: no remote copies, remote signals or barrier semaphores. Data moves between devices by JAX's collectives and lax.ppermute only.
A program may use at most 448 MiB of HBM per device.

v0:
```python
import jax
import jax.numpy as jnp
from jax import lax
from jax.sharding import PartitionSpec as P

HEAD_DIM = 64
WIN = 12
PATCH_ROWS = 24
PATCH_COLS = 24


EPSILON = 1e-05
MASKED_SCORE = -1000000000.0


def shifted(array, axis, by):
    length = lax.axis_size(axis)
    pairs = [(i, i + by) for i in range(length) if 0 <= i + by < length]
    return lax.ppermute(array, axis, pairs)


def shortened(array):
    return jax.tree.map(lambda a: a.astype(jnp.bfloat16) if a.dtype == jnp.float32 else a, array)


def layer_norm(values, norm_gains, norm_biases):
    average = jnp.mean(values, axis=-1, keepdims=True)
    centered = values - average
    variance = jnp.mean(centered * centered, axis=-1, keepdims=True)
    return centered * lax.rsqrt(variance + EPSILON) * norm_gains + norm_biases


def to_windows(row_data, shift_by):
    channels = row_data.shape[-1]
    patch_grid = row_data.reshape(PATCH_ROWS, PATCH_COLS, channels)
    patch_grid = jnp.roll(jnp.roll(patch_grid, -shift_by, axis=0), -shift_by, axis=1)
    patch_grid = patch_grid.reshape(PATCH_ROWS // WIN, WIN, PATCH_COLS // WIN, WIN, channels)
    return patch_grid.transpose(0, 2, 1, 3, 4).reshape(-1, WIN * WIN, channels)


def from_windows(windowed, shift_by):
    channels = windowed.shape[-1]
    patch_grid = windowed.reshape(PATCH_ROWS // WIN, PATCH_COLS // WIN, WIN, WIN, channels)
    patch_grid = patch_grid.transpose(0, 2, 1, 3, 4).reshape(PATCH_ROWS, PATCH_COLS, channels)
    patch_grid = jnp.roll(jnp.roll(patch_grid, shift_by, axis=0), shift_by, axis=1)
    return patch_grid.reshape(PATCH_ROWS * PATCH_COLS, channels)


def window_allowed(shift_by):
    row_index = jnp.arange(PATCH_ROWS)
    col_index = jnp.arange(PATCH_COLS)
    row_region = (row_index >= PATCH_ROWS - WIN).astype(jnp.int32) + (
        row_index >= PATCH_ROWS - shift_by
    ).astype(jnp.int32)
    col_region = (col_index >= PATCH_COLS - WIN).astype(jnp.int32) + (
        col_index >= PATCH_COLS - shift_by
    ).astype(jnp.int32)
    region_ids = (row_region[:, None] * 3 + col_region[None, :]).reshape(PATCH_ROWS * PATCH_COLS, 1)
    window_ids = to_windows(region_ids, 0)[:, :, 0]
    return window_ids[:, :, None] == window_ids[:, None, :]


def text_allowed(length, answer):
    positions = jnp.arange(answer)
    return (positions[None, :] <= positions[:, None]) & (positions[None, :] < length)


def contract_rows(left_rows, right_rows):
    return lax.dot_general(
        left_rows, right_rows, (((0,), (0,)), ((), ())), preferred_element_type=jnp.float32
    )


def score_rows(query_rows, key_rows, allowed):
    scale_factor = HEAD_DIM ** (-0.5)
    scores = (
        jnp.einsum("bnhe,bmhe->bhnm", query_rows, key_rows, preferred_element_type=jnp.float32)
        * scale_factor
    )
    if allowed is not None:
        scores = jnp.where(allowed[:, None], scores, MASKED_SCORE)
    return scores


def attend_forward(query_rows, key_rows, value_rows, allowed):
    scores = score_rows(query_rows, key_rows, allowed)
    largest = jnp.max(scores, axis=-1, keepdims=True)
    log_total = largest + jnp.log(jnp.sum(jnp.exp(scores - largest), axis=-1, keepdims=True))
    weights = jnp.exp(scores - log_total).astype(jnp.bfloat16)
    result = jnp.einsum("bhnm,bmhe->bnhe", weights, value_rows, preferred_element_type=jnp.float32)
    return (result.astype(jnp.bfloat16), log_total)


def attend_backward(query_rows, key_rows, value_rows, allowed, log_total, result_grad):
    scale_factor = HEAD_DIM ** (-0.5)
    weights = jnp.exp(score_rows(query_rows, key_rows, allowed) - log_total)
    weight_grad = jnp.einsum(
        "bnhe,bmhe->bhnm", result_grad, value_rows, preferred_element_type=jnp.float32
    )
    value_grad = jnp.einsum(
        "bhnm,bnhe->bmhe",
        weights.astype(jnp.bfloat16),
        result_grad,
        preferred_element_type=jnp.float32,
    ).astype(jnp.bfloat16)
    score_grad = (
        weights * (weight_grad - jnp.sum(weight_grad * weights, axis=-1, keepdims=True))
    ).astype(jnp.bfloat16)
    query_grad = (
        jnp.einsum("bhnm,bmhe->bnhe", score_grad, key_rows, preferred_element_type=jnp.float32)
        * scale_factor
    ).astype(jnp.bfloat16)
    key_grad = (
        jnp.einsum("bhnm,bnhe->bmhe", score_grad, query_rows, preferred_element_type=jnp.float32)
        * scale_factor
    ).astype(jnp.bfloat16)
    return (query_grad, key_grad, value_grad)


def gather_rows(image_part, text_part):
    return (
        lax.all_gather(image_part, "mp", axis=0, tiled=True),
        lax.all_gather(text_part, "mp", axis=0, tiled=True),
    )


def sum_rows(image_part, text_part):
    return (
        lax.psum_scatter(
            image_part.astype(jnp.bfloat16), "mp", scatter_dimension=0, tiled=True
        ).astype(jnp.float32),
        lax.psum_scatter(
            text_part.astype(jnp.bfloat16), "mp", scatter_dimension=0, tiled=True
        ).astype(jnp.float32),
    )


def gather_grads(image_part, text_part):
    return (
        lax.all_gather(image_part, "mp", axis=0, tiled=True),
        lax.all_gather(text_part, "mp", axis=0, tiled=True),
    )


def sum_grads(image_part, text_part):
    return (
        lax.psum_scatter(
            image_part.astype(jnp.bfloat16), "mp", scatter_dimension=0, tiled=True
        ).astype(jnp.float32),
        lax.psum_scatter(
            text_part.astype(jnp.bfloat16), "mp", scatter_dimension=0, tiled=True
        ).astype(jnp.float32),
    )


def attention_forward(normed_image, normed_text, length, params, shift_by):
    qkv_image, out_image, qkv_text, out_text, query_cross, kv_cross, out_cross = params[:7]
    local_dim = out_image.shape[0]
    local_heads = local_dim // HEAD_DIM
    patch_count = normed_image.shape[0]
    answer = normed_text.shape[0]
    image_qkv = jnp.einsum(
        "rd,dtk->rtk", normed_image, qkv_image, preferred_element_type=jnp.float32
    ).astype(jnp.bfloat16)
    windowed = to_windows(image_qkv.reshape(patch_count, 3 * local_dim), shift_by)
    windowed = windowed.reshape(-1, WIN * WIN, 3, local_heads, HEAD_DIM)
    image_att, image_total = attend_forward(
        windowed[:, :, 0], windowed[:, :, 1], windowed[:, :, 2], window_allowed(shift_by)
    )
    image_att_rows = from_windows(image_att.reshape(-1, WIN * WIN, local_dim), shift_by)
    image_part = jnp.dot(image_att_rows, out_image, preferred_element_type=jnp.float32)
    text_qkv = jnp.einsum(
        "rd,dtk->rtk", normed_text, qkv_text, preferred_element_type=jnp.float32
    ).astype(jnp.bfloat16)
    text_qkv = text_qkv.reshape(1, answer, 3, local_heads, HEAD_DIM)
    self_att, self_total = attend_forward(
        text_qkv[:, :, 0], text_qkv[:, :, 1], text_qkv[:, :, 2], text_allowed(length, answer)[None]
    )
    cross_query = jnp.dot(normed_text, query_cross, preferred_element_type=jnp.float32).astype(
        jnp.bfloat16
    )
    cross_query = cross_query.reshape(1, answer, local_heads, HEAD_DIM)
    cross_kv = jnp.einsum(
        "rd,dtk->rtk", normed_image, kv_cross, preferred_element_type=jnp.float32
    ).astype(jnp.bfloat16)
    cross_kv = cross_kv.reshape(1, patch_count, 2, local_heads, HEAD_DIM)
    cross_att, cross_total = attend_forward(cross_query, cross_kv[:, :, 0], cross_kv[:, :, 1], None)
    self_rows = self_att.reshape(answer, local_dim)
    cross_rows = cross_att.reshape(answer, local_dim)
    text_part = jnp.dot(self_rows, out_text, preferred_element_type=jnp.float32) + jnp.dot(
        cross_rows, out_cross, preferred_element_type=jnp.float32
    )
    kept_state = (
        normed_image,
        normed_text,
        windowed,
        image_total,
        image_att_rows,
        text_qkv,
        self_total,
        self_rows,
        cross_query,
        cross_kv,
        cross_total,
        cross_rows,
    )
    return (image_part, text_part, kept_state)


def attention_backward(kept_state, image_grad, text_grad, length, params, shift_by):
    qkv_image, out_image, qkv_text, out_text, query_cross, kv_cross, out_cross = params[:7]
    (
        normed_image,
        normed_text,
        windowed,
        image_total,
        image_att_rows,
        text_qkv,
        self_total,
        self_rows,
        cross_query,
        cross_kv,
        cross_total,
        cross_rows,
    ) = kept_state
    local_dim = out_image.shape[0]
    local_heads = local_dim // HEAD_DIM
    patch_count = normed_image.shape[0]
    answer = normed_text.shape[0]
    image_rows_grad = jnp.einsum(
        "rd,kd->rk", image_grad, out_image, preferred_element_type=jnp.float32
    ).astype(jnp.bfloat16)
    window_grad = to_windows(image_rows_grad, shift_by).reshape(
        -1, WIN * WIN, local_heads, HEAD_DIM
    )
    image_q_grad, image_k_grad, image_v_grad = attend_backward(
        windowed[:, :, 0],
        windowed[:, :, 1],
        windowed[:, :, 2],
        window_allowed(shift_by),
        image_total,
        window_grad,
    )
    image_qkv_grad = jnp.stack((image_q_grad, image_k_grad, image_v_grad), axis=2).reshape(
        -1, WIN * WIN, 3 * local_dim
    )
    image_qkv_grad = from_windows(image_qkv_grad, shift_by).reshape(patch_count, 3, local_dim)
    normed_image_grad = jnp.einsum(
        "rtk,dtk->rd", image_qkv_grad, qkv_image, preferred_element_type=jnp.float32
    )
    self_grad = jnp.einsum(
        "rd,kd->rk", text_grad, out_text, preferred_element_type=jnp.float32
    ).astype(jnp.bfloat16)
    text_q_grad, text_k_grad, text_v_grad = attend_backward(
        text_qkv[:, :, 0],
        text_qkv[:, :, 1],
        text_qkv[:, :, 2],
        text_allowed(length, answer)[None],
        self_total,
        self_grad.reshape(1, answer, local_heads, HEAD_DIM),
    )
    text_qkv_grad = jnp.stack((text_q_grad, text_k_grad, text_v_grad), axis=2).reshape(
        answer, 3, local_dim
    )
    normed_text_grad = jnp.einsum(
        "rtk,dtk->rd", text_qkv_grad, qkv_text, preferred_element_type=jnp.float32
    )
    cross_grad = jnp.einsum(
        "rd,kd->rk", text_grad, out_cross, preferred_element_type=jnp.float32
    ).astype(jnp.bfloat16)
    cross_q_grad, cross_k_grad, cross_v_grad = attend_backward(
        cross_query,
        cross_kv[:, :, 0],
        cross_kv[:, :, 1],
        None,
        cross_total,
        cross_grad.reshape(1, answer, local_heads, HEAD_DIM),
    )
    cross_q_rows = cross_q_grad.reshape(answer, local_dim)
    normed_text_grad = normed_text_grad + jnp.einsum(
        "rk,dk->rd", cross_q_rows, query_cross, preferred_element_type=jnp.float32
    )
    cross_kv_grad = jnp.stack((cross_k_grad, cross_v_grad), axis=2).reshape(
        patch_count, 2, local_dim
    )
    normed_image_grad = normed_image_grad + jnp.einsum(
        "rtk,dtk->rd", cross_kv_grad, kv_cross, preferred_element_type=jnp.float32
    )
    weight_pairs = (
        (normed_image, image_qkv_grad),
        (image_att_rows, image_grad),
        (normed_text, text_qkv_grad),
        (self_rows, text_grad),
        (normed_text, cross_q_rows),
        (normed_image, cross_kv_grad),
        (cross_rows, text_grad),
    )
    return (weight_pairs, normed_image_grad, normed_text_grad)


def mlp_forward(normed_rows, up_proj, down_proj):
    hidden_pre = jnp.dot(normed_rows, up_proj, preferred_element_type=jnp.float32)
    hidden_act = jax.nn.gelu(hidden_pre).astype(jnp.bfloat16)
    return (
        jnp.dot(hidden_act, down_proj, preferred_element_type=jnp.float32),
        (normed_rows, hidden_pre, hidden_act),
    )


def mlp_backward(kept_state, branch_grad, up_proj, down_proj):
    normed_rows, hidden_pre, hidden_act = kept_state
    act_grad = jnp.einsum("rd,kd->rk", branch_grad, down_proj, preferred_element_type=jnp.float32)
    pre_grad = jax.vjp(jax.nn.gelu, hidden_pre)[1](act_grad)[0].astype(jnp.bfloat16)
    normed_grad = jnp.einsum("rk,dk->rd", pre_grad, up_proj, preferred_element_type=jnp.float32)
    return ((normed_rows, pre_grad), (hidden_act, branch_grad), normed_grad)


def layer_forward(image_rows, text_rows, length, params, shift_by):
    norm_gains, norm_biases = (params[9], params[10])
    first_image = layer_norm(image_rows, norm_gains[0], norm_biases[0]).astype(jnp.bfloat16)
    first_text = layer_norm(text_rows, norm_gains[0], norm_biases[0]).astype(jnp.bfloat16)
    whole_image, whole_text = gather_rows(first_image, first_text)
    image_part, text_part, attn_state = attention_forward(
        whole_image, whole_text, length, params, shift_by
    )
    image_branch, text_branch = sum_rows(image_part, text_part)
    mid_image = image_rows + image_branch
    mid_text = text_rows + text_branch
    second_image = layer_norm(mid_image, norm_gains[1], norm_biases[1]).astype(jnp.bfloat16)
    second_text = layer_norm(mid_text, norm_gains[1], norm_biases[1]).astype(jnp.bfloat16)
    whole_second_image, whole_second_text = gather_rows(second_image, second_text)
    patch_count = whole_second_image.shape[0]
    mlp_part, mlp_state = mlp_forward(
        jnp.concatenate((whole_second_image, whole_second_text), axis=0), params[7], params[8]
    )
    image_mlp, text_mlp = sum_rows(mlp_part[:patch_count], mlp_part[patch_count:])
    kept_state = (image_rows, text_rows, mid_image, mid_text, attn_state, mlp_state)
    return (mid_image + image_mlp, mid_text + text_mlp, kept_state)


def layer_backward(kept_state, image_grad, text_grad, length, params, shift_by):
    image_rows, text_rows, mid_image, mid_text, attn_state, mlp_state = kept_state
    norm_gains, norm_biases = (params[9], params[10])
    shard_patches = image_grad.shape[0]
    whole_image_grad, whole_text_grad = gather_grads(
        image_grad.astype(jnp.bfloat16), text_grad.astype(jnp.bfloat16)
    )
    patch_count = whole_image_grad.shape[0]
    up_pair, down_pair, normed_grad = mlp_backward(
        mlp_state,
        jnp.concatenate((whole_image_grad, whole_text_grad), axis=0),
        params[7],
        params[8],
    )
    second_image_grad, second_text_grad = sum_grads(
        normed_grad[:patch_count], normed_grad[patch_count:]
    )
    mid_rows = jnp.concatenate((mid_image, mid_text), axis=0)
    norm_pull = jax.vjp(layer_norm, mid_rows, norm_gains[1], norm_biases[1])[1]
    mid_grad, gain_two, bias_two = norm_pull(
        jnp.concatenate((second_image_grad, second_text_grad), axis=0)
    )
    mid_grad = mid_grad + jnp.concatenate((image_grad, text_grad), axis=0)
    mid_image_grad = mid_grad[:shard_patches]
    mid_text_grad = mid_grad[shard_patches:]
    whole_mid_image, whole_mid_text = gather_grads(
        mid_image_grad.astype(jnp.bfloat16), mid_text_grad.astype(jnp.bfloat16)
    )
    attn_pairs, normed_image_grad, normed_text_grad = attention_backward(
        attn_state, whole_mid_image, whole_mid_text, length, params, shift_by
    )
    first_image_grad, first_text_grad = sum_grads(normed_image_grad, normed_text_grad)
    in_rows = jnp.concatenate((image_rows, text_rows), axis=0)
    norm_pull = jax.vjp(layer_norm, in_rows, norm_gains[0], norm_biases[0])[1]
    in_grad, gain_one, bias_one = norm_pull(
        jnp.concatenate((first_image_grad, first_text_grad), axis=0)
    )
    in_grad = in_grad + mid_grad
    weight_pairs = attn_pairs + (up_pair, down_pair)
    return (
        in_grad[:shard_patches],
        in_grad[shard_patches:],
        weight_pairs,
        jnp.stack((gain_one, gain_two)),
        jnp.stack((bias_one, bias_two)),
    )


def shards(
    image,
    text,
    lengths,
    image_cot,
    text_cot,
    qkv_image,
    out_image,
    qkv_text,
    out_text,
    query_cross,
    kv_cross,
    out_cross,
    up_proj,
    down_proj,
    norm_gain,
    norm_bias,
):
    section_index = lax.axis_index("section")
    micro_count = image.shape[0]
    answer_shard = text.shape[1]
    text_start = lax.axis_index("mp") * answer_shard
    params = (
        qkv_image[0],
        out_image[0],
        qkv_text[0],
        out_text[0],
        query_cross[0],
        kv_cross[0],
        out_cross[0],
        up_proj[0],
        down_proj[0],
        norm_gain[0],
        norm_bias[0],
    )
    shift_by = section_index * (WIN // 2)
    is_first = section_index == 0
    received_image = jnp.zeros(image.shape[1:], jnp.bfloat16)
    received_text = jnp.zeros(text.shape[1:], jnp.bfloat16)
    kept_list = []
    length_list = []
    sent_list = []
    for tick_index in range(micro_count + 1):
        source = min(tick_index, micro_count - 1)
        length = lengths[jnp.clip(tick_index - section_index, 0, micro_count - 1)]
        in_image = jnp.where(is_first, image[source], received_image).astype(jnp.float32)
        in_text = jnp.where(is_first, text[source], received_text).astype(jnp.float32)
        result_image, result_text, kept_state = layer_forward(
            in_image, in_text, length, params, shift_by
        )
        kept_list.append(kept_state)
        length_list.append(length)
        sent_image = result_image.astype(jnp.bfloat16)
        sent_text = result_text.astype(jnp.bfloat16)
        sent_list.append((sent_image, sent_text))
        received_image, received_text = shifted((sent_image, sent_text), "section", 1)
    back_image = jnp.zeros(image.shape[1:], jnp.bfloat16)
    back_text = jnp.zeros(text.shape[1:], jnp.bfloat16)
    accumulated = None
    gain_total = jnp.zeros(norm_gain.shape[1:], jnp.float32)
    bias_total = jnp.zeros(norm_bias.shape[1:], jnp.float32)
    grad_list = []
    for tick_index in range(micro_count + 1):
        cot_index = max(micro_count - 1 - tick_index, 0)
        batch_index = micro_count - tick_index - section_index
        valid_flag = ((batch_index >= 0) & (batch_index < micro_count)).astype(jnp.float32)
        length = length_list[micro_count - tick_index]
        keep_rows = (text_start + jnp.arange(answer_shard) < length).astype(jnp.float32)[:, None]
        top_image = image_cot[cot_index].astype(jnp.float32)
        top_text = text_cot[cot_index].astype(jnp.float32) * keep_rows
        grad_image = jnp.where(is_first, back_image.astype(jnp.float32), top_image)
        grad_text = jnp.where(is_first, back_text.astype(jnp.float32), top_text)
        kept_state = kept_list[micro_count - tick_index]
        image_in_grad, text_in_grad, weight_pairs, gain_grads, bias_grads = layer_backward(
            kept_state, grad_image, grad_text, length, params, shift_by
        )
        weight_grads = tuple(
            (
                contract_rows(left_rows, right_rows) * valid_flag
                for left_rows, right_rows in weight_pairs
            )
        )
        if accumulated is None:
            accumulated = weight_grads
        else:
            accumulated = tuple(
                (earlier + current for earlier, current in zip(accumulated, weight_grads))
            )
        gain_total = gain_total + gain_grads * valid_flag
        bias_total = bias_total + bias_grads * valid_flag
        grad_list.append((image_in_grad, text_in_grad))
        back_image, back_text = shifted(
            (image_in_grad.astype(jnp.bfloat16), text_in_grad.astype(jnp.bfloat16)), "section", -1
        )
    accumulated = jax.tree.map(
        lambda part: part.astype(jnp.float32),
        lax.psum_scatter(shortened(accumulated), "dp", scatter_dimension=0, tiled=True),
    )
    gain_share, bias_share = (
        lax.psum_scatter(gain_total, ("dp", "mp"), scatter_dimension=1, tiled=True),
        lax.psum_scatter(bias_total, ("dp", "mp"), scatter_dimension=1, tiled=True),
    )
    is_second = section_index == 1
    image_result = jnp.stack(
        [
            jnp.where(is_first, sent_list[batch][0], sent_list[batch + 1][0])
            for batch in range(micro_count)
        ]
    )
    text_result = jnp.stack(
        [
            jnp.where(is_first, sent_list[batch][1], sent_list[batch + 1][1])
            for batch in range(micro_count)
        ]
    )
    image_grads = jnp.stack(
        [
            jnp.where(
                is_second, grad_list[micro_count - 1 - batch][0], grad_list[micro_count - batch][0]
            )
            for batch in range(micro_count)
        ]
    )
    text_grads = jnp.stack(
        [
            jnp.where(
                is_second, grad_list[micro_count - 1 - batch][1], grad_list[micro_count - batch][1]
            )
            for batch in range(micro_count)
        ]
    )
    return (
        image_result[None],
        text_result[None],
        image_grads[None],
        text_grads[None],
        accumulated[0][None],
        accumulated[1][None],
        accumulated[2][None],
        accumulated[3][None],
        accumulated[4][None],
        accumulated[5][None],
        accumulated[6][None],
        accumulated[7][None],
        accumulated[8][None],
        gain_share[None],
        bias_share[None],
    )


def solution(mesh):
    return jax.shard_map(
        shards,
        mesh=mesh,
        in_specs=(
            P("dp", "mp", None),
            P("dp", "mp", None),
            P("dp"),
            P("dp", "mp", None),
            P("dp", "mp", None),
            P("section", None, None, "mp"),
            P("section", "mp", None),
            P("section", None, None, "mp"),
            P("section", "mp", None),
            P("section", None, "mp"),
            P("section", None, None, "mp"),
            P("section", "mp", None),
            P("section", None, "mp"),
            P("section", "mp", None),
            P("section", None, None),
            P("section", None, None),
        ),
        out_specs=(
            P("section", "dp", "mp", None),
            P("section", "dp", "mp", None),
            P("section", "dp", "mp", None),
            P("section", "dp", "mp", None),
            P("section", "dp", None, "mp"),
            P("section", ("mp", "dp"), None),
            P("section", "dp", None, "mp"),
            P("section", ("mp", "dp"), None),
            P("section", "dp", "mp"),
            P("section", "dp", None, "mp"),
            P("section", ("mp", "dp"), None),
            P("section", "dp", "mp"),
            P("section", ("mp", "dp"), None),
            P("section", None, ("dp", "mp")),
            P("section", None, ("dp", "mp")),
        ),
        check_vma=False,
    )
```

profile of v0, /device:TPU:0, one launch (start us, length us, event | category | flops | bytes accessed | tf_op | source)
XLA Modules:
  0.0 2399.3 jit_solution(1724709545325349545)
XLA Ops:
  82.4 24.3 %reduce-scatter.56.cloned.1.call-done = bf16[144,768]{1,0:T(8,128)(2,1)} async-done(((bf16[576,768]{1,0:T(8,128)(2,1)}), bf16[144,768]{1,0:T(8,128)(2,1)}) %reduce-scatter.56.cloned.1.call-update) | async-done | bytes 221200 | tf_op jit(solution)/shard_map/reduce_scatter | solution.py:129
  139.8 23.9 reduce-scatter.64.cloned.1.call-done
  169.5 21.3 reduce-scatter.60.cloned.1.call-done
  334.3 24.2 %reduce-scatter.72.cloned.1.call-done = bf16[200,768]{1,0:T(8,128)(2,1)} async-done(((bf16[800,768]{1,0:T(8,128)(2,1)}), bf16[200,768]{1,0:T(8,128)(2,1)}) %reduce-scatter.72.cloned.1.call-update) | async-done | bytes 307216 | tf_op jit(solution)/shard_map/reduce_scatter | solution.py:132
  364.4 21.1 reduce-scatter.68.cloned.1.call-done
  530.2 24.2 %reduce-scatter.80.cloned.1.call-done = bf16[200,768]{1,0:T(8,128)(2,1)} async-done(((bf16[800,768]{1,0:T(8,128)(2,1)}), bf16[200,768]{1,0:T(8,128)(2,1)}) %reduce-scatter.80.cloned.1.call-update) | async-done | bytes 307216 | tf_op jit(solution)/shard_map/reduce_scatter | solution.py:132
  560.5 20.9 reduce-scatter.76.cloned.1.call-done
  734.3 24.2 %reduce-scatter.88.cloned.1.call-done = bf16[200,768]{1,0:T(8,128)(2,1)} async-done(((bf16[800,768]{1,0:T(8,128)(2,1)}), bf16[200,768]{1,0:T(8,128)(2,1)}) %reduce-scatter.88.cloned.1.call-update) | async-done | bytes 307216 | tf_op jit(solution)/shard_map/reduce_scatter | solution.py:132
  764.4 21.2 reduce-scatter.84.cloned.1.call-done
  968.8 27.7 %reduce-scatter.98.cloned.1.call-done = bf16[200,768]{1,0:T(8,128)(2,1)} async-done(((bf16[800,768]{1,0:T(8,128)(2,1)}), bf16[200,768]{1,0:T(8,128)(2,1)}) %reduce-scatter.98.cloned.1.call-update) | async-done | bytes 307216 | tf_op jit(solution)/shard_map/reduce_scatter | solution.py:150
  1094.7 27.7 %reduce-scatter.102.cloned.1.call-done = bf16[200,768]{1,0:T(8,128)(2,1)} async-done(((bf16[800,768]{1,0:T(8,128)(2,1)}), bf16[200,768]{1,0:T(8,128)(2,1)}) %reduce-scatter.102.cloned.1.call-update) | async-done | bytes 307216 | tf_op jit(solution)/shard_map/reduce_scatter | solution.py:150
  1179.2 21.0 reduce-scatter.104.cloned.1.call-done
  1201.9 27.5 %reduce-scatter.106.cloned.1.call-done = bf16[200,768]{1,0:T(8,128)(2,1)} async-done(((bf16[800,768]{1,0:T(8,128)(2,1)}), bf16[200,768]{1,0:T(8,128)(2,1)}) %reduce-scatter.106.cloned.1.call-update) | async-done | bytes 307216 | tf_op jit(solution)/shard_map/reduce_scatter | solution.py:150
  1322.8 27.6 %reduce-scatter.110.cloned.1.call-done = bf16[200,768]{1,0:T(8,128)(2,1)} async-done(((bf16[800,768]{1,0:T(8,128)(2,1)}), bf16[200,768]{1,0:T(8,128)(2,1)}) %reduce-scatter.110.cloned.1.call-update) | async-done | bytes 307216 | tf_op jit(solution)/shard_map/reduce_scatter | solution.py:150
  1407.2 21.0 reduce-scatter.112.cloned.1.call-done
  1429.9 27.5 %reduce-scatter.114.cloned.1.call-done = bf16[200,768]{1,0:T(8,128)(2,1)} async-done(((bf16[800,768]{1,0:T(8,128)(2,1)}), bf16[200,768]{1,0:T(8,128)(2,1)}) %reduce-scatter.114.cloned.1.call-update) | async-done | bytes 307216 | tf_op jit(solution)/shard_map/reduce_scatter | solution.py:150
  1550.9 27.5 %reduce-scatter.118.cloned.1.call-done = bf16[200,768]{1,0:T(8,128)(2,1)} async-done(((bf16[800,768]{1,0:T(8,128)(2,1)}), bf16[200,768]{1,0:T(8,128)(2,1)}) %reduce-scatter.118.cloned.1.call-update) | async-done | bytes 307216 | tf_op jit(solution)/shard_map/reduce_scatter | solution.py:150
  1698.6 27.5 %reduce-scatter.122.cloned.1.call-done = bf16[200,768]{1,0:T(8,128)(2,1)} async-done(((bf16[800,768]{1,0:T(8,128)(2,1)}), bf16[200,768]{1,0:T(8,128)(2,1)}) %reduce-scatter.122.cloned.1.call-update) | async-done | bytes 307216 | tf_op jit(solution)/shard_map/reduce_scatter | solution.py:150
  2160.5 22.3 reduce-scatter.146.cloned.1.call-done
  2184.8 23.7 reduce-scatter.132.cloned.1.call-done
  2210.5 30.1 %reduce-scatter.140.cloned.1.call-done = bf16[192,3,192]{2,0,1:T(8,128)(2,1)} async-done(((bf16[768,3,192]{2,0,1:T(8,128)(2,1)}), bf16[192,3,192]{2,0,1:T(8,128)(2,1)}) %reduce-scatter.140.cloned.1.call-update) | async-done | bytes 221200 | tf_op jit(solution)/shard_map/reduce_scatter | solution.py:485
  2242.4 26.1 %reduce-scatter.134.cloned.1.call-done = bf16[200,768]{1,0:T(8,128)(2,1)} async-done(((bf16[800,768]{1,0:T(8,128)(2,1)}), bf16[200,768]{1,0:T(8,128)(2,1)}) %reduce-scatter.134.cloned.1.call-update) | async-done | bytes 307216 | tf_op jit(solution)/shard_map/reduce_scatter | solution.py:150
  2282.7 50.3 %reduce-scatter.154.cloned.1.call-done = f32[48,2]{1,0:T(8,128)} async-done(((f32[768,2]{1,0:T(8,128)}), f32[48,2]{1,0:T(8,128)}) %reduce-scatter.154.cloned.1.call-update) | async-done | bytes 400
  2334.4 56.8 %reduce-scatter.156.cloned.1.call-done = f32[48,2]{1,0:T(8,128)} async-done(((f32[768,2]{1,0:T(8,128)}), f32[48,2]{1,0:T(8,128)}) %reduce-scatter.156.cloned.1.call-update) | async-done | bytes 400
  (2166 shorter events, 1727.2 us)
Async XLA Ops:
  590.5 84.5 %reduce-scatter.82.cloned.1.call-start = ((), (), s32[]{:S(2)}) async-start(), calls=%async_computation.71 | async-start | bytes 1536000 | tf_op jit(solution)/shard_map/reduce_scatter | solution.py:132
  882.1 84.9 %reduce-scatter.96.cloned.1.call-start = ((), (), s32[]{:S(2)}) async-start(), calls=%async_computation.82 | async-start | bytes 1105920 | tf_op jit(solution)/shard_map/reduce_scatter | solution.py:147
  945.1 105.6 %all-gather.43.cloned.1.call-start = ((), (), s32[]{:S(2)}) async-start(), calls=%async_computation.84 | async-start | bytes 1536000 | tf_op jit(solution)/shard_map/all_gather | solution.py:141
  1003.1 89.8 %reduce-scatter.100.cloned.1.call-start = ((), (), s32[]{:S(2)}) async-start(), calls=%async_computation.85 | async-start | bytes 1105920 | tf_op jit(solution)/shard_map/reduce_scatter | solution.py:147
  1178.6 100.3 %all-gather.47.cloned.1.call-start = ((), (), s32[]{:S(2)}) async-start(), calls=%async_computation.90 | async-start | bytes 1536000 | tf_op jit(solution)/shard_map/all_gather | solution.py:141
  1234.9 86.1 %reduce-scatter.108.cloned.1.call-start = ((), (), s32[]{:S(2)}) async-start(), calls=%async_computation.91 | async-start | bytes 1105920 | tf_op jit(solution)/shard_map/reduce_scatter | solution.py:147
  1406.7 100.3 %all-gather.51.cloned.1.call-start = ((), (), s32[]{:S(2)}) async-start(), calls=%async_computation.96 | async-start | bytes 1536000 | tf_op jit(solution)/shard_map/all_gather | solution.py:141
  1463.0 86.2 %reduce-scatter.116.cloned.1.call-start = ((), (), s32[]{:S(2)}) async-start(), calls=%async_computation.97 | async-start | bytes 1105920 | tf_op jit(solution)/shard_map/reduce_scatter | solution.py:147
  1610.6 86.3 %reduce-scatter.120.cloned.1.call-start = ((), (), s32[]{:S(2)}) async-start(), calls=%async_computation.100 | async-start | bytes 1105920 | tf_op jit(solution)/shard_map/reduce_scatter | solution.py:147
  1641.0 85.1 %reduce-scatter.122.cloned.1.call-start = ((), (), s32[]{:S(2)}) async-start(), calls=%async_computation.101 | async-start | bytes 1536000 | tf_op jit(solution)/shard_map/reduce_scatter | solution.py:150
  1646.6 129.2 %all-gather.55.cloned.1.call-start = ((), (), s32[]{:S(2)}) async-start(), calls=%async_computation.102 | async-start | bytes 1536000 | tf_op jit(solution)/shard_map/all_gather | solution.py:141
  1731.8 104.1 %reduce-scatter.124.cloned.1.call-start = ((), (), s32[]{:S(2)}) async-start(), calls=%async_computation.103 | async-start | bytes 1105920 | tf_op jit(solution)/shard_map/reduce_scatter | solution.py:147
  1921.7 134.8 %all-gather.59.cloned.1.call-start = ((), (), s32[]{:S(2)}) async-start(), calls=%async_computation.108 | async-start | bytes 1536000 | tf_op jit(solution)/shard_map/all_gather | solution.py:141
  1965.5 170.6 %reduce-scatter.152.cloned.1.call-start = ((), (), s32[]{:S(2)}) async-start(), calls=%async_computation.119 | async-start | bytes 1474560 | tf_op jit(solution)/shard_map/reduce_scatter | solution.py:485
  1981.0 156.9 %reduce-scatter.150.cloned.1.call-start = ((), (), s32[]{:S(2)}) async-start(), calls=%async_computation.118 | async-start | bytes 1474560 | tf_op jit(solution)/shard_map/reduce_scatter | solution.py:485
  1997.7 142.1 %reduce-scatter.138.cloned.1.call-start = ((), (), s32[]{:S(2)}) async-start(), calls=%async_computation.112 | async-start | bytes 368640 | tf_op jit(solution)/shard_map/reduce_scatter | solution.py:485
  2041.1 100.3 %reduce-scatter.136.cloned.1.call-start = ((), (), s32[]{:S(2)}) async-start(), calls=%async_computation.111 | async-start | bytes 1474560 | tf_op jit(solution)/shard_map/reduce_scatter | solution.py:485
  2047.7 95.5 %reduce-scatter.148.cloned.1.call-start = ((), (), s32[]{:S(2)}) async-start(), calls=%async_computation.117 | async-start | bytes 368640 | tf_op jit(solution)/shard_map/reduce_scatter | solution.py:485
  2088.4 94.4 %reduce-scatter.146.cloned.1.call-start = ((), (), s32[]{:S(2)}) async-start(), calls=%async_computation.116 | async-start | bytes 983040 | tf_op jit(solution)/shard_map/reduce_scatter | solution.py:485
  2095.3 113.2 %reduce-scatter.132.cloned.1.call-start = ((), (), s32[]{:S(2)}) async-start(), calls=%async_computation.109 | async-start | bytes 1105920 | tf_op jit(solution)/shard_map/reduce_scatter | solution.py:147
  2110.8 129.9 %reduce-scatter.140.cloned.1.call-start = ((), (), s32[]{:S(2)}) async-start(), calls=%async_computation.113 | async-start | bytes 1474560 | tf_op jit(solution)/shard_map/reduce_scatter | solution.py:485
  2128.1 140.5 %reduce-scatter.134.cloned.1.call-start = ((), (), s32[]{:S(2)}) async-start(), calls=%async_computation.110 | async-start | bytes 1536000 | tf_op jit(solution)/shard_map/reduce_scatter | solution.py:150
  2135.9 197.1 %reduce-scatter.154.cloned.1.call-start = ((), (), s32[]{:S(2)}) async-start(), calls=%async_computation.120 | async-start | bytes 417792
  2277.3 113.8 %reduce-scatter.156.cloned.1.call-start = ((), (), s32[]{:S(2)}) async-start(), calls=%async_computation.121 | async-start | bytes 417792
  (601 other events, 6702.1 us)
Sparse Core Ops, SparseCore 0:
  53.0 26.3 reduce-scatter.57
  137.6 26.0 reduce-scatter.63
  237.8 28.0 reduce-scatter.65
  332.1 26.3 reduce-scatter.71
  433.7 28.0 reduce-scatter.73
  528.0 26.3 reduce-scatter.79
  629.6 28.0 reduce-scatter.81
  732.1 26.3 reduce-scatter.87
  833.4 27.8 reduce-scatter.89
  970.4 26.0 reduce-scatter.97
  1096.3 26.0 reduce-scatter.101
  1203.3 25.9 reduce-scatter.105
  1324.4 25.9 reduce-scatter.109
  1431.4 25.9 reduce-scatter.113
  1644.4 26.0 reduce-scatter.93
  1700.1 26.0 reduce-scatter.121
  1821.6 25.9 reduce-scatter.125
  1933.8 25.9 reduce-scatter.129
  1985.5 29.1 reduce-scatter.151
  2017.1 27.8 reduce-scatter.149
  2068.8 27.4 reduce-scatter.135
  2211.4 29.1 reduce-scatter.139
  2277.4 55.5 reduce-scatter.153
  2336.5 54.5 reduce-scatter.155
  (47 shorter events, 992.1 us)
where the time goes:
time: 2420 us; the launch traced here: 2400 us
  waiting for transfers between devices  920 us (38%)
  matrix products  501 us (21%)
  local copies, waits for them, and re-layouts  395 us (16%)
  other arithmetic  316 us (13%)
  blocking collectives  198 us (8%)
  starting transfers between devices  47.6 us (2%)
    reduce_scatter x10, waiting for transfers between devices, sum_grads(): lax.psum_scatter(text_part.astype(jnp.bfloat16), 'mp', scatter_dimension=...  247 us
    reduce_scatter x10, waiting for transfers between devices, sum_rows(): lax.psum_scatter(image_part.astype(jnp.bfloat16), 'mp', scatter_dimension...  184 us
    dot_general x45, matrix products, contract_rows(): lax.dot_general(left_rows, right_rows, (((0,), (0,)), ((), ())), preferre...  134 us
    unnamed x1104, local copies, waits for them, and re-layouts  121 us
    reduce_scatter x10, waiting for transfers between devices, sum_grads(): lax.psum_scatter(image_part.astype(jnp.bfloat16), 'mp', scatter_dimension...  112 us
    unnamed x73, waiting for transfers between devices  108 us
    all_gather x10, blocking collectives, gather_rows(): lax.all_gather(image_part, 'mp', axis=0, tiled=True)  105 us
    reduce_scatter x10, waiting for transfers between devices, sum_rows(): lax.psum_scatter(text_part.astype(jnp.bfloat16), 'mp', scatter_dimension=...  104 us
  transfers between devices with their start and end apart: 87, of which 59 were waited for; matrix products, arithmetic and copies ran while one was open for 35% of the time, Pallas kernels for 0%

commit v1 on v0

v1 whole, which is shorter than its diff:
```python
import functools

import jax
import jax.numpy as jnp
from jax import lax
from jax.experimental import pallas as pl
from jax.experimental.pallas import tpu as pltpu
from jax.sharding import PartitionSpec as P

HEAD_DIM = 64
WIN = 12
PATCH_ROWS = 24
PATCH_COLS = 24
SHIFT = WIN // 2

EPSILON = 1e-05
MASKED_SCORE = -1000000000.0
SCALE = HEAD_DIM**-0.5
GELU_C = 0.7978845608028654
GELU_A = 0.044715

VMEM_MIB = 56
FF_BLOCK = 256
SKEW = 2

F32 = jnp.float32
BF16 = jnp.bfloat16

FLIPS = (0, 2, 1, 3)
AT_SLOT, AT_BLOCK, AT_SECTION, AT_MP, AT_LENGTH, AT_VALID = 0, 4, 8, 9, 16, 32


def dot(left, right):
    return lax.dot_general(left, right, (((1,), (0,)), ((), ())), preferred_element_type=F32)


def dot_nt(left, right):
    return lax.dot_general(left, right, (((1,), (1,)), ((), ())), preferred_element_type=F32)


def dot_tn(left, right):
    return lax.dot_general(left, right, (((0,), (0,)), ((), ())), preferred_element_type=F32)


def head_mask(head, width, scale):
    lane = lax.broadcasted_iota(jnp.int32, (1, width), 1)
    inside = (lane >= head * HEAD_DIM) & (lane < (head + 1) * HEAD_DIM)
    return jnp.where(inside, F32(scale), F32(0.0)).astype(BF16)


def normalized(values):
    average = jnp.mean(values, axis=-1, keepdims=True)
    centered = values - average
    variance = jnp.mean(centered * centered, axis=-1, keepdims=True)
    inverse = lax.rsqrt(variance + EPSILON)
    return centered * inverse, inverse


def norm_pull(grad, values, gain):
    unit, inverse = normalized(values)
    scaled = grad * gain
    first = jnp.mean(scaled, axis=-1, keepdims=True)
    second = jnp.mean(scaled * unit, axis=-1, keepdims=True)
    pulled = inverse * (scaled - first - unit * second)
    gain_sum = jnp.sum(grad * unit, axis=0, keepdims=True)
    bias_sum = jnp.sum(grad, axis=0, keepdims=True)
    return pulled, gain_sum, bias_sum


SMEM_SPEC = pl.BlockSpec(memory_space=pltpu.SMEM)
ANY_SPEC = pl.BlockSpec(memory_space=pl.ANY)


def whole(*extent):
    zeros = (0,) * len(extent)
    return pl.BlockSpec(extent, lambda *at: zeros, pipeline_mode=pl.Buffered(1))


def params(mib=VMEM_MIB):
    return pltpu.CompilerParams(vmem_limit_bytes=mib << 20)


def cost(flops, moved, exps=0):
    return pl.CostEstimate(flops=int(flops), bytes_accessed=int(moved), transcendentals=int(exps))


def shape_of(extent, dtype):
    return jax.ShapeDtypeStruct(extent, dtype)


def entry_kernel(tick, info, image, text, got_image, got_text, gain, bias, xi, xt, hi, ht):
    first = info[AT_SECTION] == 0
    for own, got, rows, normed in ((image, got_image, xi, hi), (text, got_text, xt, ht)):
        values = jnp.where(first, own[0].astype(F32), got[...].astype(F32))
        rows[...] = values.astype(BF16)
        unit, _ = normalized(values)
        normed[...] = (unit * gain[0:1, :] + bias[0:1, :]).astype(BF16)


def entry(tick, info, source, image, text, got_image, got_text, gain, bias):
    ni, d = got_image.shape
    nt = got_text.shape[0]
    return pl.pallas_call(
        entry_kernel,
        grid=(1,),
        out_shape=(
            shape_of((ni, d), BF16),
            shape_of((nt, d), BF16),
            shape_of((ni, d), BF16),
            shape_of((nt, d), BF16),
        ),
        in_specs=[
            SMEM_SPEC,
            SMEM_SPEC,
            pl.BlockSpec((1, ni, d), lambda i: (source, 0, 0)),
            pl.BlockSpec((1, nt, d), lambda i: (source, 0, 0)),
            whole(ni, d),
            whole(nt, d),
            whole(*gain.shape),
            whole(*bias.shape),
        ],
        out_specs=(whole(ni, d), whole(nt, d), whole(ni, d), whole(nt, d)),
        compiler_params=params(),
        cost_estimate=cost(10 * (ni + nt) * d, 8 * (ni + nt) * d),
        name="entry_norm",
    )(tick, info, image, text, got_image, got_text, gain, bias)


def image_forward_kernel(
    info, p0, p1, p2, p3, w, wo, gidc, gidr, hx, qkv, ot, tt, r0, r1, r2, r3, o_rows, v_tall
):
    shard = p0.shape[0]
    band = ot.shape[2]
    width = wo.shape[0]
    heads = width // HEAD_DIM
    offs = [pl.multiple_of(info[AT_SLOT + i] * shard, 16) for i in range(4)]
    for off, piece in zip(offs, (p0, p1, p2, p3)):
        rows = piece[...]
        hx[pl.ds(off, shard), :] = rows
        for j in range(5):
            qkv[j, pl.ds(off, shard), :] = dot(rows, w[j]).astype(BF16)
    for b in range(ot.shape[0]):
        span = slice(b * band, (b + 1) * band)
        bias = jnp.where(gidc[span, :] == gidr[0:1, span], F32(0.0), F32(MASKED_SCORE))
        v_tall[...] = qkv[4, span, :].astype(F32).T.astype(BF16)

        def one_head(head, carry):
            query = qkv[2, span, :] * head_mask(head, width, SCALE)
            scores = dot_nt(qkv[3, span, :], query) + bias
            largest = jnp.max(scores, axis=0, keepdims=True)
            weights = jnp.exp(scores - largest)
            total = jnp.sum(weights, axis=0, keepdims=True)
            tt[b * heads + head] = largest + jnp.log(total)
            at = pl.multiple_of(head * HEAD_DIM, HEAD_DIM)
            mixed = dot(v_tall[pl.ds(at, HEAD_DIM), :], weights.astype(BF16))
            ot[b, pl.ds(at, HEAD_DIM), :] = mixed * (1.0 / total)
            return carry

        lax.fori_loop(0, heads, one_head, 0)
        o_rows[span, :] = ot[b].T.astype(BF16)
    for off, piece in zip(offs, (r0, r1, r2, r3)):
        piece[...] = dot(o_rows[pl.ds(off, shard), :], wo[...]).astype(BF16)


def image_forward(info, pieces, w, wo, gidc, gidr):
    shard, d = pieces[0].shape
    rows = 4 * shard
    width = wo.shape[0]
    band = rows // 2
    heads = width // HEAD_DIM
    return pl.pallas_call(
        image_forward_kernel,
        out_shape=(
            shape_of((rows, d), BF16),
            shape_of((5, rows, width), BF16),
            shape_of((2, width, band), F32),
            shape_of((2 * heads, 1, band), F32),
        )
        + (shape_of((shard, d), BF16),) * 4,
        grid=(1,),
        in_specs=[SMEM_SPEC]
        + [whole(shard, d)] * 4
        + [whole(*a.shape) for a in (w, wo, gidc, gidr)],
        out_specs=(
            whole(rows, d),
            whole(5, rows, width),
            whole(2, width, band),
            whole(2 * heads, 1, band),
        )
        + (whole(shard, d),) * 4,
        scratch_shapes=[
            pltpu.VMEM((rows, width), BF16),
            pltpu.VMEM((width, band), BF16),
        ],
        compiler_params=params(),
        cost_estimate=cost(
            2 * rows * d * width * 6 + 8 * heads * band * band * 256,
            2 * rows * d * 3 + 12 * rows * width + 12 * d * width,
            2 * heads * band * band,
        ),
        name="image_forward",
    )(info, *pieces, w, wo, gidc, gidr)


def store_chunks(grads, chunks, w_parts, wo_parts):
    width, d = w_parts[0].shape
    rows, at = d // chunks, d // chunks
    for j, part in enumerate(w_parts):
        turned = part.T.astype(BF16)
        for z in range(chunks):
            grads[z, 0:rows, j * width : (j + 1) * width] = turned[z * rows : (z + 1) * rows, :]
    for part in wo_parts:
        rows = width // chunks
        narrow = part.astype(BF16)
        for z in range(chunks):
            grads[z, at : at + rows, 0:d] = narrow[z * rows : (z + 1) * rows, :]
            if grads.shape[2] > d:
                grads[z, at : at + rows, d:] = jnp.zeros((rows, grads.shape[2] - d), BF16)
        at += rows


def image_backward_kernel(
    first, last, tick, info, p0, p1, p2, p3, w, wo, gidc, gidr, hx, qkv, ot, tt, dkv, *refs
):
    olds, refs = ([], refs) if first else (refs[:2], refs[2:])
    (r0, r1, r2, r3), refs = refs[:4], refs[4:]
    news, refs = (refs[:1], refs[1:]) if last else (refs[:2], refs[2:])
    da_rows, do_rows, d_rows, dq_tall, k_tall, do_tall, dk_sum, dv_sum = refs
    shard = p0.shape[0]
    band = ot.shape[2]
    width = wo.shape[0]
    heads = width // HEAD_DIM
    valid = info[AT_VALID + tick[0]].astype(F32)
    offs = [pl.multiple_of(info[AT_SLOT + i] * shard, 16) for i in range(4)]
    for off, piece in zip(offs, (p0, p1, p2, p3)):
        rows = piece[...]
        da_rows[pl.ds(off, shard), :] = rows
        do_rows[pl.ds(off, shard), :] = dot_nt(rows, wo[...]).astype(BF16)
    total_wo = jnp.zeros(wo.shape, F32)
    for b in range(ot.shape[0]):
        span = slice(b * band, (b + 1) * band)
        total_wo = total_wo + dot(ot[b].astype(BF16), da_rows[span, :])
        bias = jnp.where(gidc[span, :] == gidr[0:1, span], F32(0.0), F32(MASKED_SCORE))
        k_tall[...] = qkv[3, span, :].astype(F32).T.astype(BF16)
        do_tall[...] = do_rows[span, :].astype(F32).T
        dk_sum[...] = jnp.zeros_like(dk_sum)
        dv_sum[...] = jnp.zeros_like(dv_sum)

        def one_head(head, carry):
            at = pl.multiple_of(head * HEAD_DIM, HEAD_DIM)
            query = qkv[2, span, :] * head_mask(head, width, SCALE)
            grad = do_rows[span, :] * head_mask(head, width, 1.0)
            scores = dot_nt(qkv[3, span, :], query) + bias
            weights = jnp.exp(scores - tt[b * heads + head])
            pulled = dot_nt(qkv[4, span, :], grad)
            mixed = ot[b, pl.ds(at, HEAD_DIM), :]
            delta = jnp.sum(do_tall[pl.ds(at, HEAD_DIM), :] * mixed, axis=0, keepdims=True)
            score_grad = (weights * (pulled - delta)).astype(BF16)
            dv_sum[...] += dot(weights.astype(BF16), grad)
            dk_sum[...] += dot(score_grad, query)
            dq_tall[pl.ds(at, HEAD_DIM), :] = dot(k_tall[pl.ds(at, HEAD_DIM), :], score_grad) * SCALE
            return carry

        lax.fori_loop(0, heads, one_head, 0)
        d_rows[0, span, :] = dq_tall[...].T.astype(BF16)
        d_rows[1, span, :] = dk_sum[...].astype(BF16)
        d_rows[2, span, :] = dv_sum[...].astype(BF16)
    for off, piece in zip(offs, (r0, r1, r2, r3)):
        part = dot_nt(dkv[0, pl.ds(off, shard), :], w[0]) + dot_nt(dkv[1, pl.ds(off, shard), :], w[1])
        for j in range(3):
            part = part + dot_nt(d_rows[j, pl.ds(off, shard), :], w[2 + j])
        piece[...] = part.astype(BF16)
    w_parts = [dot_tn(dkv[j] if j < 2 else d_rows[j - 2], hx[...]) * valid for j in range(5)]
    wo_part = total_wo * valid
    if not first:
        w_parts = [olds[0][j] + part for j, part in enumerate(w_parts)]
        wo_part = olds[1][...] + wo_part
    if last:
        store_chunks(news[0], news[0].shape[0], w_parts, [wo_part])
    else:
        for j, part in enumerate(w_parts):
            news[0][j] = part
        news[1][...] = wo_part


def image_backward(tick, info, pieces, w, wo, gidc, gidr, hx, qkv, ot, tt, dkv, accs, chunks):
    first, last = not accs, chunks > 0
    shard, d = pieces[0].shape
    rows = 4 * shard
    width = wo.shape[0]
    band = rows // 2
    heads = width // HEAD_DIM
    if last:
        news = (shape_of((chunks, (d + width) // chunks, max(5 * width, d)), BF16),)
    else:
        news = (shape_of((5, width, d), F32), shape_of((width, d), F32))
    arrays = (w, wo, gidc, gidr, hx, qkv, ot, tt, dkv) + tuple(accs)
    out = pl.pallas_call(
        functools.partial(image_backward_kernel, first, last),
        grid=(1,),
        out_shape=(shape_of((shard, d), BF16),) * 4 + news,
        in_specs=[SMEM_SPEC] * 2 + [whole(shard, d)] * 4 + [whole(*a.shape) for a in arrays],
        out_specs=(whole(shard, d),) * 4 + tuple(whole(*a.shape) for a in news),
        input_output_aliases={} if first or last else {15: 4, 16: 5},
        scratch_shapes=[
            pltpu.VMEM((rows, d), BF16),
            pltpu.VMEM((rows, width), BF16),
            pltpu.VMEM((3, rows, width), BF16),
            pltpu.VMEM((width, band), F32),
            pltpu.VMEM((width, band), BF16),
            pltpu.VMEM((width, band), F32),
            pltpu.VMEM((band, width), F32),
            pltpu.VMEM((band, width), F32),
        ],
        compiler_params=params(),
        cost_estimate=cost(
            2 * rows * d * width * 12 + 20 * heads * band * band * 256,
            2 * rows * d * 3 + 20 * rows * width + 60 * d * width,
            2 * heads * band * band,
        ),
        name="image_backward",
    )(tick, info, *pieces, *arrays)
    return out[:4], out[4:]


QUERY_BLOCK = 256


def query_blocks(rows):
    return [(at, min(QUERY_BLOCK, rows - at)) for at in range(0, rows, QUERY_BLOCK)]


def text_forward_kernel(
    tick, info, p0, p1, p2, p3, w, wo, kv, hy, qkv, ot, tt, r0, r1, r2, r3, stage, o_rows, v_tall
):
    shard, d = p0.shape
    rows = 4 * shard
    patches = kv.shape[1]
    width = wo.shape[1]
    heads = width // HEAD_DIM
    last_key = info[AT_LENGTH + tick[0]] - 1
    offs = [pl.multiple_of(info[AT_BLOCK + i] * shard, 8) for i in range(4)]
    for off, piece in zip(offs, (p0, p1, p2, p3)):
        stage[pl.ds(off, shard), :] = piece[...].astype(F32)
    hy[...] = stage[...].astype(BF16)
    for j in range(4):
        qkv[j] = dot(hy[...], w[j]).astype(BF16)
    for kind in range(2):
        span = rows if kind == 0 else patches
        values = qkv[2] if kind == 0 else kv[1]
        v_tall[:, 0:span] = values.astype(F32).T.astype(BF16)

        def one_head(head, carry):
            at = pl.multiple_of(head * HEAD_DIM, HEAD_DIM)
            out_at = pl.multiple_of(kind * width + head * HEAD_DIM, HEAD_DIM)
            mask = head_mask(head, width, SCALE)
            for start, size in query_blocks(rows):
                seen = start + size if kind == 0 else patches
                query = qkv[0 if kind == 0 else 3, start : start + size, :] * mask
                keys = qkv[1, 0:seen, :] if kind == 0 else kv[0]
                scores = dot_nt(keys, query)
                if kind == 0:
                    key_at = lax.broadcasted_iota(jnp.int32, (seen, size), 0)
                    query_at = lax.broadcasted_iota(jnp.int32, (1, size), 1) + start
                    limit = jnp.minimum(query_at, last_key)
                    scores = jnp.where(key_at <= limit, scores, F32(MASKED_SCORE))
                largest = jnp.max(scores, axis=0, keepdims=True)
                weights = jnp.exp(scores - largest)
                total = jnp.sum(weights, axis=0, keepdims=True)
                tt[kind * heads + head, :, start : start + size] = largest + jnp.log(total)
                mixed = dot(v_tall[pl.ds(at, HEAD_DIM), 0:seen], weights.astype(BF16))
                mixed = mixed * (1.0 / total)
                ot[pl.ds(out_at, HEAD_DIM), start : start + size] = mixed
            return carry

        lax.fori_loop(0, heads, one_head, 0)
    o_rows[...] = ot[...].T
    for off, piece in zip(offs, (r0, r1, r2, r3)):
        mixed = o_rows[pl.ds(off, shard), :].astype(BF16)
        piece[...] = (dot(mixed[:, 0:width], wo[0]) + dot(mixed[:, width:], wo[1])).astype(BF16)


def text_forward(tick, info, pieces, w, wo, kv):
    shard, d = pieces[0].shape
    rows = 4 * shard
    width = wo.shape[1]
    heads = width // HEAD_DIM
    patches = kv.shape[1]
    return pl.pallas_call(
        text_forward_kernel,
        grid=(1,),
        out_shape=(
            shape_of((rows, d), BF16),
            shape_of((4, rows, width), BF16),
            shape_of((2 * width, rows), F32),
            shape_of((2 * heads, 1, rows), F32),
        )
        + (shape_of((shard, d), BF16),) * 4,
        in_specs=[SMEM_SPEC] * 2
        + [whole(shard, d)] * 4
        + [whole(*w.shape), whole(*wo.shape), whole(2, patches, width)],
        out_specs=(whole(rows, d), whole(4, rows, width), whole(2 * width, rows), whole(2 * heads, 1, rows))
        + (whole(shard, d),) * 4,
        scratch_shapes=[
            pltpu.VMEM((rows, d), F32),
            pltpu.VMEM((rows, 2 * width), F32),
            pltpu.VMEM((width, rows), BF16),
        ],
        compiler_params=params(),
        cost_estimate=cost(
            2 * rows * d * width * 6 + 4 * heads * rows * (rows * 0.6 + patches) * 256,
            2 * rows * d * 3 + 12 * rows * width + 12 * d * width,
            heads * rows * (rows * 0.6 + patches),
        ),
        name="text_forward",
    )(tick, info, *pieces, w, wo, kv)


def text_backward_kernel(first, last, tick, info, p0, p1, p2, p3, w, wo, kv, hy, qkv, ot, tt, *refs):
    olds, refs = ([], refs) if first else (refs[:2], refs[2:])
    (r0, r1, r2, r3, dkv), refs = refs[:5], refs[5:]
    news, refs = (refs[:1], refs[1:]) if last else (refs[:2], refs[2:])
    stage, da_rows, do_rows, dq_tall, k_tall, do_tall, dk_sum, dv_sum, d_rows = refs
    shard, d = p0.shape
    rows = 4 * shard
    patches = kv.shape[1]
    width = wo.shape[1]
    heads = width // HEAD_DIM
    valid = info[AT_VALID + tick[0]].astype(F32)
    last_key = info[AT_LENGTH + tick[0]] - 1
    offs = [pl.multiple_of(info[AT_BLOCK + i] * shard, 8) for i in range(4)]
    for off, piece in zip(offs, (p0, p1, p2, p3)):
        stage[pl.ds(off, shard), :] = piece[...].astype(F32)
    da_rows[...] = stage[...].astype(BF16)
    wo_parts = []
    for kind in range(2):
        span = rows if kind == 0 else patches
        grads = dot_nt(da_rows[...], wo[kind]).astype(BF16)
        do_rows[...] = grads
        do_tall[...] = grads.astype(F32).T
        wo_parts.append(dot(ot[kind * width : (kind + 1) * width, :].astype(BF16), da_rows[...]) * valid)
        whole_keys = qkv[1] if kind == 0 else kv[0]
        k_tall[:, 0:span] = whole_keys.astype(F32).T.astype(BF16)
        dk_sum[...] = jnp.zeros_like(dk_sum)
        dv_sum[...] = jnp.zeros_like(dv_sum)

        def one_head(head, carry):
            at = pl.multiple_of(head * HEAD_DIM, HEAD_DIM)
            out_at = pl.multiple_of(kind * width + head * HEAD_DIM, HEAD_DIM)
            query_mask = head_mask(head, width, SCALE)
            grad_mask = head_mask(head, width, 1.0)
            for start, size in query_blocks(rows):
                seen = start + size if kind == 0 else patches
                block = slice(start, start + size)
                query = qkv[0 if kind == 0 else 3, block, :] * query_mask
                grad = do_rows[block, :] * grad_mask
                keys = qkv[1, 0:seen, :] if kind == 0 else kv[0]
                values = qkv[2, 0:seen, :] if kind == 0 else kv[1]
                scores = dot_nt(keys, query)
                if kind == 0:
                    key_at = lax.broadcasted_iota(jnp.int32, (seen, size), 0)
                    query_at = lax.broadcasted_iota(jnp.int32, (1, size), 1) + start
                    limit = jnp.minimum(query_at, last_key)
                    scores = jnp.where(key_at <= limit, scores, F32(MASKED_SCORE))
                weights = jnp.exp(scores - tt[kind * heads + head, :, block])
                pulled = dot_nt(values, grad)
                mixed = ot[pl.ds(out_at, HEAD_DIM), block]
                delta = jnp.sum(do_tall[pl.ds(at, HEAD_DIM), block] * mixed, axis=0, keepdims=True)
                score_grad = (weights * (pulled - delta)).astype(BF16)
                dv_sum[0:seen, :] += dot(weights.astype(BF16), grad)
                dk_sum[0:seen, :] += dot(score_grad, query)
                dq_tall[pl.ds(at, HEAD_DIM), block] = (
                    dot(k_tall[pl.ds(at, HEAD_DIM), 0:seen], score_grad) * SCALE
                )
            return carry

        lax.fori_loop(0, heads, one_head, 0)
        if kind == 0:
            d_rows[0] = dq_tall[...].T.astype(BF16)
            d_rows[1] = dk_sum[...].astype(BF16)
            d_rows[2] = dv_sum[...].astype(BF16)
        else:
            d_rows[3] = dq_tall[...].T.astype(BF16)
            dkv[0] = dk_sum[0:patches, :].astype(BF16)
            dkv[1] = dv_sum[0:patches, :].astype(BF16)
    part = dot_nt(d_rows[0], w[0])
    for j in range(1, 4):
        part = part + dot_nt(d_rows[j], w[j])
    stage[...] = part
    for off, piece in zip(offs, (r0, r1, r2, r3)):
        piece[...] = stage[pl.ds(off, shard), :].astype(BF16)
    w_parts = [dot_tn(d_rows[j], hy[...]) * valid for j in range(4)]
    if not first:
        w_parts = [olds[0][j] + part for j, part in enumerate(w_parts)]
        wo_parts = [olds[1][j] + part for j, part in enumerate(wo_parts)]
    if last:
        store_chunks(news[0], news[0].shape[0], w_parts, wo_parts)
    else:
        for j, part in enumerate(w_parts):
            news[0][j] = part
        for j, part in enumerate(wo_parts):
            news[1][j] = part


def text_backward(tick, info, pieces, w, wo, kv, hy, qkv, ot, tt, accs, chunks):
    first, last = not accs, chunks > 0
    shard, d = pieces[0].shape
    rows = 4 * shard
    width = wo.shape[1]
    heads = width // HEAD_DIM
    patches = kv.shape[1]
    if last:
        news = (shape_of((chunks, (d + 2 * width) // chunks, max(4 * width, d)), BF16),)
    else:
        news = (shape_of((4, width, d), F32), shape_of((2, width, d), F32))
    arrays = (hy, qkv, ot, tt) + tuple(accs)
    out = pl.pallas_call(
        functools.partial(text_backward_kernel, first, last),
        grid=(1,),
        out_shape=(shape_of((shard, d), BF16),) * 4 + (shape_of((2, patches, width), BF16),) + news,
        in_specs=[SMEM_SPEC] * 2
        + [whole(shard, d)] * 4
        + [whole(*w.shape), whole(*wo.shape), whole(2, patches, width)]
        + [whole(*a.shape) for a in arrays],
        out_specs=(whole(shard, d),) * 4
        + (whole(2, patches, width),)
        + tuple(whole(*a.shape) for a in news),
        input_output_aliases={} if first or last else {13: 5, 14: 6},
        scratch_shapes=[
            pltpu.VMEM((rows, d), F32),
            pltpu.VMEM((rows, d), BF16),
            pltpu.VMEM((rows, width), BF16),
            pltpu.VMEM((width, rows), F32),
            pltpu.VMEM((width, rows), BF16),
            pltpu.VMEM((width, rows), F32),
            pltpu.VMEM((rows, width), F32),
            pltpu.VMEM((rows, width), F32),
            pltpu.VMEM((4, rows, width), BF16),
        ],
        compiler_params=params(),
        cost_estimate=cost(
            2 * rows * d * width * 12 + 10 * heads * rows * (rows * 0.6 + patches) * 256,
            2 * rows * d * 3 + 20 * rows * width + 60 * d * width,
            heads * rows * (rows * 0.6 + patches),
        ),
        name="text_backward",
    )(tick, info, *pieces, w, wo, kv, *arrays)
    return out[:4], out[4], out[5:]


def ff_forward_kernel(stacked, xi, ai, bi, ci, xt, at, bt, ct, gain, bias, up, down, *refs):
    refs = refs[2:] if stacked else refs
    mid, h2_tall, g, gp, zi, zt, h2, acc = refs
    step = pl.program_id(0)
    ni = xi.shape[0]

    @pl.when(step == 0)
    def _():
        for x, a, b, c, span in (
            (xi, ai, bi, ci, slice(0, ni)),
            (xt, at, bt, ct, slice(ni, mid.shape[0])),
        ):
            branch = a[...].astype(F32) + b[...].astype(F32) + c[...].astype(F32)
            values = x[...].astype(F32) + branch
            mid[span, :] = values
            acc[span, :] = values
        unit, _ = normalized(mid[...])
        rows = unit * gain[1:2, :] + bias[1:2, :]
        h2[...] = rows.astype(BF16)
        h2_tall[0] = rows.T.astype(BF16)

    hidden = up.shape[2]
    total = acc[...]
    for at_unit in range(0, hidden, FF_BLOCK):
        block = slice(at_unit, at_unit + FF_BLOCK)
        u = dot(h2[...], up[0, :, block])
        square = u * u
        bent = jnp.tanh(u * (GELU_C + (GELU_C * GELU_A) * square))
        half = 0.5 * (1.0 + bent)
        act = (u * half).astype(BF16)
        g[0, :, block] = act
        slope = half + (0.5 * u) * (1.0 - bent * bent) * (GELU_C + (3.0 * GELU_C * GELU_A) * square)
        gp[:, block] = slope.astype(BF16)
        total = total + dot(act, down[0, block, :])
    acc[...] = total

    @pl.when(step == pl.num_programs(0) - 1)
    def _():
        zi[...] = acc[0:ni, :].astype(BF16)
        zt[...] = acc[ni:, :].astype(BF16)


def ff_forward(t, ticks, stacks, xi, image_parts, xt, text_parts, gain, bias, up, down):
    ni, d = xi.shape
    nt = xt.shape[0]
    n = ni + nt
    blocks, _, hidden = up.shape
    stacked = len(stacks) > 0
    return pl.pallas_call(
        functools.partial(ff_forward_kernel, stacked),
        grid=(blocks,),
        out_shape=(
            shape_of((n, d), F32),
            shape_of((ticks, d, n), BF16),
            shape_of((ticks, n, blocks * hidden), BF16),
            shape_of((n, blocks * hidden), BF16),
            shape_of((ni, d), BF16),
            shape_of((nt, d), BF16),
        ),
        in_specs=[whole(ni, d)] * 4
        + [whole(nt, d)] * 4
        + [whole(*gain.shape), whole(*bias.shape)]
        + [
            pl.BlockSpec((1, d, hidden), lambda i: (i, 0, 0)),
            pl.BlockSpec((1, hidden, d), lambda i: (i, 0, 0)),
        ]
        + [ANY_SPEC] * len(stacks),
        out_specs=(
            whole(n, d),
            pl.BlockSpec((1, d, n), lambda i: (t, 0, 0)),
            pl.BlockSpec((1, n, hidden), lambda i: (t, 0, i)),
            pl.BlockSpec((n, hidden), lambda i: (0, i)),
            whole(ni, d),
            whole(nt, d),
        ),
        input_output_aliases={12: 1, 13: 2} if stacked else {},
        scratch_shapes=[pltpu.VMEM((n, d), BF16), pltpu.VMEM((n, d), F32)],
        compiler_params=params(),
        cost_estimate=cost(
            4 * n * d * hidden * blocks,
            4 * d * hidden * blocks + 4 * n * hidden * blocks + 16 * n * d,
            n * hidden * blocks,
        ),
        name="ff_forward",
    )(xi, *image_parts, xt, *text_parts, gain, bias, up, down, *stacks)


def ff_backward_kernel(
    stacked, tick, info, coti, cott, backi, backt, gp, mid, gain, up, down, *refs
):
    refs = refs[2:] if stacked else refs
    dm_tall, du, dmid, dai, dat, sums, rows, dm, acc = refs
    step = pl.program_id(0)
    ni = backi.shape[0]
    nt = backt.shape[0]
    valid = info[AT_VALID + tick[0]].astype(F32)

    @pl.when(step == 0)
    def _():
        first = info[AT_SECTION] == 0
        place = lax.broadcasted_iota(jnp.int32, (nt, 1), 0) + info[AT_MP] * nt
        kept = (place < info[AT_LENGTH + tick[0]]).astype(F32)
        rows[0:ni, :] = jnp.where(first, backi[...].astype(F32), coti[0].astype(F32)) * valid
        rows[ni:, :] = jnp.where(first, backt[...].astype(F32), cott[0].astype(F32) * kept) * valid
        dm[...] = rows[...].astype(BF16)
        dm_tall[0] = rows[...].T.astype(BF16)
        acc[...] = jnp.zeros_like(acc)

    hidden = up.shape[2]
    total = acc[...]
    for at_unit in range(0, hidden, FF_BLOCK):
        block = slice(at_unit, at_unit + FF_BLOCK)
        act_grad = dot_nt(dm[...], down[0, block, :])
        pre_grad = (gp[:, block].astype(F32) * act_grad).astype(BF16)
        du[0, :, block] = pre_grad
        total = total + dot_nt(pre_grad, up[0, :, block])
    acc[...] = total

    @pl.when(step == pl.num_programs(0) - 1)
    def _():
        pulled, gain_sum, bias_sum = norm_pull(acc[...], mid[...], gain[1:2, :])
        total = rows[...] + pulled
        dmid[...] = total
        dai[...] = total[0:ni, :].astype(BF16)
        dat[...] = total[ni:, :].astype(BF16)
        sums[0:1, :] = gain_sum
        sums[1:2, :] = bias_sum


def ff_backward(
    tick, info, source, t, ticks, stacks, coti, cott, backi, backt, gp, mid, gain, up, down
):
    ni, d = backi.shape
    nt = backt.shape[0]
    n = ni + nt
    blocks, _, hidden = up.shape
    stacked = len(stacks) > 0
    return pl.pallas_call(
        functools.partial(ff_backward_kernel, stacked),
        grid=(blocks,),
        out_shape=(
            shape_of((ticks, d, n), BF16),
            shape_of((ticks, n, blocks * hidden), BF16),
            shape_of((n, d), F32),
            shape_of((ni, d), BF16),
            shape_of((nt, d), BF16),
            shape_of((2, d), F32),
        ),
        in_specs=[
            SMEM_SPEC,
            SMEM_SPEC,
            pl.BlockSpec((1, ni, d), lambda i: (source, 0, 0)),
            pl.BlockSpec((1, nt, d), lambda i: (source, 0, 0)),
            whole(ni, d),
            whole(nt, d),
            pl.BlockSpec((n, hidden), lambda i: (0, i)),
            whole(n, d),
            whole(*gain.shape),
            pl.BlockSpec((1, d, hidden), lambda i: (i, 0, 0)),
            pl.BlockSpec((1, hidden, d), lambda i: (i, 0, 0)),
        ]
        + [ANY_SPEC] * len(stacks),
        out_specs=(
            pl.BlockSpec((1, d, n), lambda i: (t, 0, 0)),
            pl.BlockSpec((1, n, hidden), lambda i: (t, 0, i)),
            whole(n, d),
            whole(ni, d),
            whole(nt, d),
            whole(2, d),
        ),
        input_output_aliases={11: 0, 12: 1} if stacked else {},
        scratch_shapes=[
            pltpu.VMEM((n, d), F32),
            pltpu.VMEM((n, d), BF16),
            pltpu.VMEM((n, d), F32),
        ],
        compiler_params=params(),
        cost_estimate=cost(
            4 * n * d * hidden * blocks,
            4 * d * hidden * blocks + 4 * n * hidden * blocks + 16 * n * d,
        ),
        name="ff_backward",
    )(tick, info, coti, cott, backi, backt, gp, mid, gain, up, down, *stacks)


def ff_weights_kernel(h2_tall, dm_tall, du, g, one, two, up_sum, down_sum):
    piece, t = pl.program_id(0), pl.program_id(1)
    up_part = dot(h2_tall[t], du[0])
    down_part = dot(dm_tall[t], g[0])

    @pl.when(t == 0)
    def _():
        up_sum[...] = up_part
        down_sum[...] = down_part

    @pl.when(t > 0)
    def _():
        up_sum[...] += up_part
        down_sum[...] += down_part

    for index, out in enumerate((one, two)):

        @pl.when((t == pl.num_programs(1) - 1) & (piece == index))
        def _():
            chunks, rows = out.shape[0], out.shape[1] // 2
            turned = down_sum[...].T
            for z in range(chunks):
                span = slice(z * rows, (z + 1) * rows)
                out[z, 0:rows, :] = up_sum[span, :].astype(BF16)
                out[z, rows:, :] = turned[span, :].astype(BF16)


def ff_weights(pieces, h2_tall, dm_tall, du, g, chunks):
    ticks, d, n = h2_tall.shape
    hidden = du.shape[2] // 4
    one, two = pieces
    part = (chunks, 2 * d // chunks, hidden)
    column = lambda i: one + (two - one) * i
    return pl.pallas_call(
        ff_weights_kernel,
        grid=(2, ticks),
        out_shape=(shape_of(part, BF16),) * 2,
        in_specs=[
            whole(ticks, d, n),
            whole(ticks, d, n),
            pl.BlockSpec((1, n, hidden), lambda i, t: (t, 0, column(i))),
            pl.BlockSpec((1, n, hidden), lambda i, t: (t, 0, column(i))),
        ],
        out_specs=(whole(*part), whole(*part)),
        scratch_shapes=[pltpu.VMEM((d, hidden), F32), pltpu.VMEM((hidden, d), F32)],
        compiler_params=params(),
        cost_estimate=cost(
            8 * ticks * n * d * hidden, 4 * ticks * d * n + 8 * ticks * n * hidden + 8 * d * hidden
        ),
        name="ff_weights",
    )(h2_tall, dm_tall, du, g)


def close_kernel(
    tick, info, xi, ai, bi, ci, xt, at, bt, ct, dmid, gain, gi, gt, backi, backt, sums
):
    ni = xi.shape[0]
    n = dmid.shape[0]
    gain_total = jnp.zeros((1, xi.shape[1]), F32)
    bias_total = jnp.zeros((1, xi.shape[1]), F32)
    for x, a, b, c, span, out, back in (
        (xi, ai, bi, ci, slice(0, ni), gi, backi),
        (xt, at, bt, ct, slice(ni, n), gt, backt),
    ):
        grad = a[...].astype(F32) + b[...].astype(F32) + c[...].astype(F32)
        pulled, gain_sum, bias_sum = norm_pull(grad, x[...].astype(F32), gain[0:1, :])
        total = dmid[span, :] + pulled
        out[...] = total
        back[...] = total.astype(BF16)
        gain_total = gain_total + gain_sum
        bias_total = bias_total + bias_sum
    valid = info[AT_VALID + tick[0]].astype(F32)
    sums[0:1, :] = gain_total * valid
    sums[1:2, :] = bias_total * valid


def close(tick, info, xi, image_parts, xt, text_parts, dmid, gain):
    ni, d = xi.shape
    nt = xt.shape[0]
    return pl.pallas_call(
        close_kernel,
        out_shape=(
            shape_of((ni, d), F32),
            shape_of((nt, d), F32),
            shape_of((ni, d), BF16),
            shape_of((nt, d), BF16),
            shape_of((2, d), F32),
        ),
        grid=(1,),
        in_specs=[SMEM_SPEC] * 2
        + [whole(ni, d)] * 4
        + [whole(nt, d)] * 4
        + [whole(*dmid.shape), whole(*gain.shape)],
        out_specs=(whole(ni, d), whole(nt, d), whole(ni, d), whole(nt, d), whole(2, d)),
        compiler_params=params(),
        cost_estimate=cost(20 * (ni + nt) * d, 18 * (ni + nt) * d),
        name="input_grad",
    )(tick, info, xi, *image_parts, xt, *text_parts, dmid, gain)


def over_y(array):
    return lax.ppermute(array, "mp", [(m, m ^ 2) for m in range(4)])


def over_core(array):
    return lax.ppermute(array, "mp", [(m, m ^ 1) for m in range(4)])


def gathered(own):
    across = over_y(own)
    return (own, across, over_core(own), over_core(across))


def scattered(r0, r1, r2, r3):
    across = (r1.astype(F32) + over_core(r3).astype(F32)).astype(BF16)
    return (r0, over_core(r2), over_y(across))


def shifted(array, by):
    length = lax.axis_size("section")
    return lax.ppermute(array, "section", [(i, i + by) for i in range(length) if 0 <= i + by < length])


def shards(
    image, text, lengths, image_cot, text_cot, qkv_image, out_image, qkv_text, out_text,
    query_cross, kv_cross, out_cross, up_proj, down_proj, norm_gain, norm_bias,
):
    section = lax.axis_index("section")
    me = lax.axis_index("mp")
    groups = lax.axis_size("dp")
    micro = image.shape[0]
    ticks = micro + SKEW
    ni, d = image.shape[1:]
    nt = text.shape[1]
    gain, bias = norm_gain[0], norm_bias[0]
    wo_image = out_image[0]
    wo_text = jnp.stack((out_text[0], out_cross[0]))
    w_image = jnp.concatenate((kv_cross[0].transpose(1, 0, 2), qkv_image[0].transpose(1, 0, 2)), axis=0)
    w_text = jnp.concatenate((qkv_text[0].transpose(1, 0, 2), query_cross[0][None]), axis=0)
    width = wo_image.shape[0]

    flips = jnp.array(FLIPS, jnp.int32)
    turn = jnp.arange(ticks) - section * SKEW
    valid = ((turn >= 0) & (turn < micro)).astype(jnp.int32)
    info = jnp.concatenate(
        (
            ((me ^ flips) - section) % 4,
            me ^ flips,
            jnp.stack((section, me)).astype(jnp.int32),
            jnp.zeros((AT_LENGTH - 10,), jnp.int32),
            lengths[jnp.clip(turn, 0, micro - 1)],
            jnp.zeros((AT_VALID - AT_LENGTH - ticks,), jnp.int32),
            valid,
        )
    ).astype(jnp.int32)
    place = jnp.arange(4 * ni)
    turned = (place % PATCH_COLS - section * SHIFT) % PATCH_COLS
    edge = PATCH_ROWS - section * SHIFT
    row_region = (place // PATCH_COLS >= PATCH_ROWS - WIN).astype(jnp.int32) + (
        place // PATCH_COLS >= edge
    ).astype(jnp.int32)
    col_region = (turned >= PATCH_COLS - WIN).astype(jnp.int32) + (turned >= edge).astype(jnp.int32)
    region = row_region * 3 + col_region
    gidc = region[:, None]
    gidr = region[None, :]

    tick_at = [jnp.full((1,), t, jnp.int32) for t in range(ticks)]
    none_image = jnp.zeros((ni, d), BF16)
    none_text = jnp.zeros((nt, d), BF16)
    kept = []
    sent = []
    relayed = []
    up = down = None
    stacks = ()
    for t in range(ticks):
        got_image, got_text = relayed[t - SKEW] if t >= SKEW else (none_image, none_text)
        xi, xt, hi, ht = entry(
            tick_at[t], info, min(t, micro - 1), image, text, got_image, got_text, gain, bias
        )
        image_pieces = gathered(hi)
        text_pieces = gathered(ht)
        if up is None:
            up_own, down_own, _ = lax.optimization_barrier((up_proj[0], down_proj[0], text_pieces[1]))
            up = jnp.stack(gathered(up_own))
            down = jnp.stack(gathered(down_own))
        hx, qkvi, oti, tti, *image_parts = image_forward(info, image_pieces, w_image, wo_image, gidc, gidr)
        hy, qkvt, ott, ttt, *text_parts = text_forward(tick_at[t], info, text_pieces, w_text, wo_text, qkvi)
        mid, h2_tall, g, gp, zi, zt = ff_forward(
            t, ticks, stacks, xi, scattered(*image_parts), xt, scattered(*text_parts),
            gain, bias, up, down,
        )
        stacks = (h2_tall, g)
        kept.append((xi, xt, hx, qkvi, oti, tti, hy, qkvt, ott, ttt, mid, gp))
        sent.append((zi, zt))
        if t + SKEW < ticks:
            relayed.append((shifted(zi, 1), shifted(zt, 1)))

    accs_image = accs_text = back_stacks = ()
    sums_one = sums_two = jnp.zeros((2, d), F32)
    grads = []
    relayed = []
    for k in range(ticks):
        t = ticks - 1 - k
        last = groups if k == ticks - 1 else 0
        xi, xt, hx, qkvi, oti, tti, hy, qkvt, ott, ttt, mid, gp = kept[t]
        back_image, back_text = relayed[k - SKEW] if k >= SKEW else (none_image, none_text)
        dm_tall, du, dmid, dai, dat, sums = ff_backward(
            tick_at[t], info, max(t - SKEW, 0), t, ticks, back_stacks, image_cot, text_cot,
            back_image, back_text, gp, mid, gain, up, down,
        )
        back_stacks = (dm_tall, du)
        sums_two = sums_two + sums
        text_pieces = gathered(dat)
        image_pieces = gathered(dai)
        if last:
            far, y_part = ff_weights((3, 1), stacks[0], dm_tall, du, stacks[1], groups)
            near, core_part = ff_weights((0, 2), stacks[0], dm_tall, du, stacks[1], groups)
            ff_parts = scattered(near, y_part, core_part, far)
        text_parts, dkv, accs_text = text_backward(
            tick_at[t], info, text_pieces, w_text, wo_text, qkvi, hy, qkvt, ott, ttt, accs_text, last
        )
        image_parts, accs_image = image_backward(
            tick_at[t], info, image_pieces, w_image, wo_image, gidc, gidr, hx, qkvi, oti, tti,
            dkv, accs_image, last,
        )
        gi, gt, back_image, back_text, sums = close(
            tick_at[t], info, xi, scattered(*image_parts), xt, scattered(*text_parts), dmid, gain
        )
        sums_one = sums_one + sums
        grads.append((gi, gt))
        if k + SKEW < ticks:
            relayed.append((shifted(back_image, -1), shifted(back_text, -1)))

    def over_dp(array):
        return lax.psum_scatter(array, "dp", scatter_dimension=0, tiled=True)[0].astype(F32)

    a, b, c = ff_parts
    ff_grad = over_dp((a.astype(F32) + b.astype(F32) + c.astype(F32)).astype(BF16))
    text_grad = over_dp(accs_text[0])
    image_grad = over_dp(accs_image[0])
    rows, wo_rows = d // groups, width // groups
    up_grad, down_grad = ff_grad[:rows], ff_grad[rows:]
    gain_grad, bias_grad = (
        lax.psum_scatter(
            jnp.stack((sums_one[i], sums_two[i])), ("dp", "mp"), scatter_dimension=1, tiled=True
        )
        for i in range(2)
    )
    head = section == 0
    image_result, text_result = (
        jnp.stack([jnp.where(head, sent[b][i], sent[b + SKEW][i]) for b in range(micro)])
        for i in range(2)
    )
    by_tick = grads[::-1]
    image_grads, text_grads = (
        jnp.stack([jnp.where(head, by_tick[b][i], by_tick[b + SKEW][i]) for b in range(micro)])
        for i in range(2)
    )
    return (
        image_result[None],
        text_result[None],
        image_grads[None],
        text_grads[None],
        image_grad[:rows, 2 * width :].reshape(1, rows, 3, width),
        image_grad[rows:, :d][None],
        text_grad[:rows, : 3 * width].reshape(1, rows, 3, width),
        text_grad[rows : rows + wo_rows, :d][None],
        text_grad[:rows, 3 * width :][None],
        image_grad[:rows, : 2 * width].reshape(1, rows, 2, width),
        text_grad[rows + wo_rows :, :d][None],
        up_grad[None],
        down_grad[None],
        gain_grad[None],
        bias_grad[None],
    )


def solution(mesh):
    return jax.shard_map(
        shards,
        mesh=mesh,
        in_specs=(
            P("dp", "mp", None),
            P("dp", "mp", None),
            P("dp"),
            P("dp", "mp", None),
            P("dp", "mp", None),
            P("section", None, None, "mp"),
            P("section", "mp", None),
            P("section", None, None, "mp"),
            P("section", "mp", None),
            P("section", None, "mp"),
            P("section", None, None, "mp"),
            P("section", "mp", None),
            P("section", None, "mp"),
            P("section", "mp", None),
            P("section", None, None),
            P("section", None, None),
        ),
        out_specs=(
            P("section", "dp", "mp", None),
            P("section", "dp", "mp", None),
            P("section", "dp", "mp", None),
            P("section", "dp", "mp", None),
            P("section", "dp", None, "mp"),
            P("section", ("mp", "dp"), None),
            P("section", "dp", None, "mp"),
            P("section", ("mp", "dp"), None),
            P("section", "dp", "mp"),
            P("section", "dp", None, "mp"),
            P("section", ("mp", "dp"), None),
            P("section", "dp", "mp"),
            P("section", ("mp", "dp"), None),
            P("section", None, ("dp", "mp")),
            P("section", None, ("dp", "mp")),
        ),
        check_vma=False,
    )
```

time: 2420 us -> 1180 us (0.49)
  Pallas kernels: 0 us -> 619 us
  waiting for transfers between devices: 920 us -> 341 us
  matrix products: 501 us -> 0 us
  local copies, waits for them, and re-layouts: 395 us -> 53.1 us
  other arithmetic: 316 us -> 32.4 us
  blocking collectives: 198 us -> 0 us
  starting transfers between devices: 47.6 us -> 104 us
    pallas_call x0 -> x50, Pallas kernels: none -> 619 us  [the longest x6 130 us: text_backward(): pl.pallas_call(functools.partial(text_backward_kernel, first, last), grid...]
    reduce_scatter x49 -> x3, waiting for transfers between devices: 712 us -> 108 us  [over_dp(): lax.psum_scatter(array, 'dp', scatter_dimension=0, tiled=True)[0]]
    dot_general x210 -> x0, matrix products: 473 us -> none  [the longest x45 134 us: contract_rows(): lax.dot_general(left_rows, right_rows, (((0,), (0,)), ((), ())), preferre...]
    all_gather x20 -> x0, blocking collectives: 198 us -> none  [the longest x10 105 us: gather_rows(): lax.all_gather(image_part, 'mp', axis=0, tiled=True)]
    ppermute x16 -> x169, waiting for transfers between devices: 59.9 us -> 233 us  [the longest x51 164 us: over_y(): return lax.ppermute(array, 'mp', [(m, m ^ 2) for m in range(4)])]
    convert_element_type x97 -> x29, other arithmetic: 131 us -> 13.4 us  [the longest x25 8.7 us: scattered(): across = (r1.astype(F32) + over_core(r3).astype(F32)).astype(BF16)]
    another operation x45 -> x3, local copies, waits for them, and re-layouts: 116 us -> 0.02 us  [the longest x1 0.02 us: shards(): wo_text = jnp.stack((out_text[0], out_cross[0]))]
    unnamed x73 -> x7, waiting for transfers between devices: 108 us -> 0.75 us
  transfers between devices with their start and end apart: 87 -> 174, of which waited for: 59 -> 31; matrix products, arithmetic and copies ran while one was open for 35% -> 4% of each run, Pallas kernels for 0% -> 46%
where the time goes in v1:
time: 1180 us; the launch traced here: 1170 us
  Pallas kernels  619 us (52%)
  waiting for transfers between devices  341 us (29%)
  starting transfers between devices  104 us (9%)
  local copies, waits for them, and re-layouts  53.1 us (4%)
  other arithmetic  32.4 us (3%)
  between operations  16.5 us (1%)
    ppermute x51, waiting for transfers between devices, over_y(): return lax.ppermute(array, 'mp', [(m, m ^ 2) for m in range(4)])  164 us
    pallas_call x6, Pallas kernels, text_backward(): pl.pallas_call(functools.partial(text_backward_kernel, first, last), grid...  130 us
    reduce_scatter x3, waiting for transfers between devices, over_dp(): lax.psum_scatter(array, 'dp', scatter_dimension=0, tiled=True)[0]  108 us
    pallas_call x6, Pallas kernels, text_forward(): pl.pallas_call(text_forward_kernel, grid=(1,), out_shape=(shape_of((rows,...  106 us
    pallas_call x6, Pallas kernels, image_backward(): pl.pallas_call(functools.partial(image_backward_kernel, first, last), gri...  84.6 us
    pallas_call x6, Pallas kernels, ff_forward(): pl.pallas_call(functools.partial(ff_forward_kernel, stacked), grid=(block...  82 us
    pallas_call x6, Pallas kernels, ff_backward(): pl.pallas_call(functools.partial(ff_backward_kernel, stacked), grid=(bloc...  71.5 us
    ppermute x16, waiting for transfers between devices, shifted(): lax.ppermute(array, 'section', [(i, i + by) for i in range(length) if 0 <...  62.4 us
  transfers between devices with their start and end apart: 174, of which 31 were waited for; matrix products, arithmetic and copies ran while one was open for 4% of the time, Pallas kernels for 46%

profile of v1, /device:TPU:0, one launch (start us, length us, event | category | flops | bytes accessed | tf_op | source)
XLA Modules:
  0.0 1166.9 jit_solution(11039671537040278756)
XLA Ops:
  62.4 17.8 %text_forward.8 = (bf16[800,768]{1,0:T(8,128)(2,1)}, bf16[4,800,192]{2,1,0:T(8,128)(2,1)}, f32[384,800]{1,0:T(8,128)}, f32[6,1,800]{2,1,0:T(1,128)}, bf16[200,76...) custom-call(s32[1]{0:T(128)} %constant.74.clone.1.tick, ...), custom_call_target="tpu_custom_call" | custom-call | flops 4010803200 | bytes 7299072 | tf_op jit(solution)/shard_map/text_forward/pallas_call | solution.py:389
  81.3 17.5 %text_forward.6 = (bf16[800,768]{1,0:T(8,128)(2,1)}, bf16[4,800,192]{2,1,0:T(8,128)(2,1)}, f32[384,800]{1,0:T(8,128)}, f32[6,1,800]{2,1,0:T(1,128)}, bf16[200,76...) custom-call(s32[1]{0:T(128)} %constant.36.clone.1.tick, ...), custom_call_target="tpu_custom_call" | custom-call | flops 4010803200 | bytes 7299072 | tf_op jit(solution)/shard_map/text_forward/pallas_call | solution.py:389
  143.5 23.5 %ff_forward.7 = (f32[344,768]{1,0:T(8,128)}, bf16[6,768,344]{2,1,0:T(8,128)(2,1)}, bf16[6,344,3072]{2,1,0:T(8,128)(2,1)}, bf16[344,3072]{1,0:T(8,128)(2,1)}, bf1...) custom-call(bf16[144,768]{1,0:T(8,128)(2,1)} %get-tuple-element.345.xi, ...), custom_call_target="tpu_custom_call", output_to_operand_aliasing={{1}: (12, {}), {2}: (13, {})} | custom-call | flops 3246391296 | bytes 17891328 | tf_op jit(solution)/shard_map/ff_forward/pallas_call | solution.py:599
  231.1 17.5 %text_forward.7 = (bf16[800,768]{1,0:T(8,128)(2,1)}, bf16[4,800,192]{2,1,0:T(8,128)(2,1)}, f32[384,800]{1,0:T(8,128)}, f32[6,1,800]{2,1,0:T(1,128)}, bf16[200,76...) custom-call(s32[1]{0:T(128)} %constant.73.clone.1.tick, ...), custom_call_target="tpu_custom_call" | custom-call | flops 4010803200 | bytes 7299072 | tf_op jit(solution)/shard_map/text_forward/pallas_call | solution.py:389
  249.8 17.9 %text_forward.9 = (bf16[800,768]{1,0:T(8,128)(2,1)}, bf16[4,800,192]{2,1,0:T(8,128)(2,1)}, f32[384,800]{1,0:T(8,128)}, f32[6,1,800]{2,1,0:T(1,128)}, bf16[200,76...) custom-call(s32[1]{0:T(128)} %constant.75.clone.1.tick, ...), custom_call_target="tpu_custom_call" | custom-call | flops 4010803200 | bytes 7299072 | tf_op jit(solution)/shard_map/text_forward/pallas_call | solution.py:389
  377.0 17.5 %text_forward.10 = (bf16[800,768]{1,0:T(8,128)(2,1)}, bf16[4,800,192]{2,1,0:T(8,128)(2,1)}, f32[384,800]{1,0:T(8,128)}, f32[6,1,800]{2,1,0:T(1,128)}, bf16[200,7...) custom-call(s32[1]{0:T(128)} %constant.76.clone.1.tick, ...), custom_call_target="tpu_custom_call" | custom-call | flops 4010803200 | bytes 7299072 | tf_op jit(solution)/shard_map/text_forward/pallas_call | solution.py:389
  395.7 17.9 %text_forward.11 = (bf16[800,768]{1,0:T(8,128)(2,1)}, bf16[4,800,192]{2,1,0:T(8,128)(2,1)}, f32[384,800]{1,0:T(8,128)}, f32[6,1,800]{2,1,0:T(1,128)}, bf16[200,7...) custom-call(s32[1]{0:T(128)} %constant.77.clone.1.tick, ...), custom_call_target="tpu_custom_call" | custom-call | flops 4010803200 | bytes 7299072 | tf_op jit(solution)/shard_map/text_forward/pallas_call | solution.py:389
  494.7 20.9 %text_backward.6 = (bf16[200,768]{1,0:T(8,128)(2,1)}, bf16[200,768]{1,0:T(8,128)(2,1)}, bf16[200,768]{1,0:T(8,128)(2,1)}, bf16[200,768]{1,0:T(8,128)(2,1)}, bf16...) custom-call(s32[1]{0:T(128)} %constant.77.clone.1.tick, s32[38]{0:T(128)} %concatenate.9.info, ...), custom_call_target="tpu_custom_call" | custom-call | flops 9319219200 | bytes 15605760 | tf_op jit(solution)/shard_map/text_backward/pallas_call | solution.py:517
  531.6 22.1 %text_backward.7 = (bf16[200,768]{1,0:T(8,128)(2,1)}, bf16[200,768]{1,0:T(8,128)(2,1)}, bf16[200,768]{1,0:T(8,128)(2,1)}, bf16[200,768]{1,0:T(8,128)(2,1)}, bf16...) custom-call(s32[1]{0:T(128)} %constant.76.clone.1.tick, ...), custom_call_target="tpu_custom_call", output_to_operand_aliasing={{5}: (13, {}), {6}: (14, {})} | custom-call | flops 9319219200 | bytes 15605760 | tf_op jit(solution)/shard_map/text_backward/pallas_call | solution.py:517
  556.9 14.2 %image_backward.7 = (bf16[144,768]{1,0:T(8,128)(2,1)}, bf16[144,768]{1,0:T(8,128)(2,1)}, bf16[144,768]{1,0:T(8,128)(2,1)}, bf16[144,768]{1,0:T(8,128)(2,1)}, f32[5,192,768]{2,1,0:T(8,128)}, /*index=5*/f32[192,768]{1,0:T(8,128)}) custom-call(s32[1]{0:T(128)} %constant.76.clone.1.tick, ...), custom_call_target="tpu_custom_call", output_to_operand_aliasing={{4}: (15, {}), {5}: (16, {})} | custom-call | flops 3312451584 | bytes 13713408 | tf_op jit(solution)/shard_map/image_backward/pallas_call | solution.py:298
  643.8 21.8 %text_backward.8 = (bf16[200,768]{1,0:T(8,128)(2,1)}, bf16[200,768]{1,0:T(8,128)(2,1)}, bf16[200,768]{1,0:T(8,128)(2,1)}, bf16[200,768]{1,0:T(8,128)(2,1)}, bf16...) custom-call(s32[1]{0:T(128)} %constant.75.clone.1.tick, ...), custom_call_target="tpu_custom_call", output_to_operand_aliasing={{5}: (13, {}), {6}: (14, {})} | custom-call | flops 9319219200 | bytes 15605760 | tf_op jit(solution)/shard_map/text_backward/pallas_call | solution.py:517
  667.0 14.4 %image_backward.8 = (bf16[144,768]{1,0:T(8,128)(2,1)}, bf16[144,768]{1,0:T(8,128)(2,1)}, bf16[144,768]{1,0:T(8,128)(2,1)}, bf16[144,768]{1,0:T(8,128)(2,1)}, f32[5,192,768]{2,1,0:T(8,128)}, /*index=5*/f32[192,768]{1,0:T(8,128)}) custom-call(s32[1]{0:T(128)} %constant.75.clone.1.tick, ...), custom_call_target="tpu_custom_call", output_to_operand_aliasing={{4}: (15, {}), {5}: (16, {})} | custom-call | flops 3312451584 | bytes 13713408 | tf_op jit(solution)/shard_map/image_backward/pallas_call | solution.py:298
  682.8 22.0 %text_backward.9 = (bf16[200,768]{1,0:T(8,128)(2,1)}, bf16[200,768]{1,0:T(8,128)(2,1)}, bf16[200,768]{1,0:T(8,128)(2,1)}, bf16[200,768]{1,0:T(8,128)(2,1)}, bf16...) custom-call(s32[1]{0:T(128)} %constant.73.clone.1.tick, ...), custom_call_target="tpu_custom_call", output_to_operand_aliasing={{5}: (13, {}), {6}: (14, {})} | custom-call | flops 9319219200 | bytes 15605760 | tf_op jit(solution)/shard_map/text_backward/pallas_call | solution.py:517
  706.0 14.3 %image_backward.9 = (bf16[144,768]{1,0:T(8,128)(2,1)}, bf16[144,768]{1,0:T(8,128)(2,1)}, bf16[144,768]{1,0:T(8,128)(2,1)}, bf16[144,768]{1,0:T(8,128)(2,1)}, f32[5,192,768]{2,1,0:T(8,128)}, /*index=5*/f32[192,768]{1,0:T(8,128)}) custom-call(s32[1]{0:T(128)} %constant.73.clone.1.tick, ...), custom_call_target="tpu_custom_call", output_to_operand_aliasing={{4}: (15, {}), {5}: (16, {})} | custom-call | flops 3312451584 | bytes 13713408 | tf_op jit(solution)/shard_map/image_backward/pallas_call | solution.py:298
  800.2 21.8 %text_backward.10 = (bf16[200,768]{1,0:T(8,128)(2,1)}, bf16[200,768]{1,0:T(8,128)(2,1)}, bf16[200,768]{1,0:T(8,128)(2,1)}, bf16[200,768]{1,0:T(8,128)(2,1)}, bf1...) custom-call(s32[1]{0:T(128)} %constant.74.clone.1.tick, ...), custom_call_target="tpu_custom_call", output_to_operand_aliasing={{5}: (13, {}), {6}: (14, {})} | custom-call | flops 9319219200 | bytes 15605760 | tf_op jit(solution)/shard_map/text_backward/pallas_call | solution.py:517
  823.5 14.4 %image_backward.10 = (bf16[144,768]{1,0:T(8,128)(2,1)}, bf16[144,768]{1,0:T(8,128)(2,1)}, bf16[144,768]{1,0:T(8,128)(2,1)}, bf16[144,768]{1,0:T(8,128)(2,1)}, f3...) custom-call(s32[1]{0:T(128)} %constant.74.clone.1.tick, ...), custom_call_target="tpu_custom_call", output_to_operand_aliasing={{4}: (15, {}), {5}: (16, {})} | custom-call | flops 3312451584 | bytes 13713408 | tf_op jit(solution)/shard_map/image_backward/pallas_call | solution.py:298
  839.1 21.6 %text_backward.11 = (bf16[200,768]{1,0:T(8,128)(2,1)}, bf16[200,768]{1,0:T(8,128)(2,1)}, bf16[200,768]{1,0:T(8,128)(2,1)}, bf16[200,768]{1,0:T(8,128)(2,1)}, bf1...) custom-call(s32[1]{0:T(128)} %constant.36.clone.1.tick, s32[38]{0:T(128)} %concatenate.9.info, ...), custom_call_target="tpu_custom_call" | custom-call | flops 9319219200 | bytes 15605760 | tf_op jit(solution)/shard_map/text_backward/pallas_call | solution.py:517
  862.0 14.2 %image_backward.11 = (bf16[144,768]{1,0:T(8,128)(2,1)}, bf16[144,768]{1,0:T(8,128)(2,1)}, bf16[144,768]{1,0:T(8,128)(2,1)}, bf16[144,768]{1,0:T(8,128)(2,1)}, bf16[4,240,960]{2,1,0:T(8,128)(2,1)}) custom-call(s32[1]{0:T(128)} %constant.36.clone.1.tick, s32[38]{0:T(128)} %concatenate.9.info, bf16[144,768]{1,0:T(8,128)(2,1)} %get-tuple-element.535.p0, ...), custom_call_target="tpu_custom_call" | custom-call | flops 3312451584 | bytes 13713408 | tf_op jit(solution)/shard_map/image_backward/pallas_call | solution.py:298
  911.9 28.7 %ff_weights.3 = (bf16[4,384,768]{2,1,0:T(8,128)(2,1)}, bf16[4,384,768]{2,1,0:T(8,128)(2,1)}) custom-call(bf16[6,768,344]{2,1,0:T(8,128)(2,1)} %get-tuple-element.595.h2_tall, bf16[6,768,344]{2,1,0:T(8,128)(2,1)} %get-tuple-element.596.dm_tall, bf16[6,344,3072]{2,1,0:T(8,128)(2,1)} %get-tuple-element.597.du, bf16[6,344,3072]{2,1,0:T(8,128)(2,1)} %get-tuple-element.598.g), custom_call_target="tpu_custom_call" | custom-call | flops 9739173888 | bytes 23740416 | tf_op jit(solution)/shard_map/ff_weights/pallas_call | solution.py:769
  940.7 28.7 %ff_weights.2 = (bf16[4,384,768]{2,1,0:T(8,128)(2,1)}, bf16[4,384,768]{2,1,0:T(8,128)(2,1)}) custom-call(bf16[6,768,344]{2,1,0:T(8,128)(2,1)} %get-tuple-element.595.h2_tall, bf16[6,768,344]{2,1,0:T(8,128)(2,1)} %get-tuple-element.596.dm_tall, bf16[6,344,3072]{2,1,0:T(8,128)(2,1)} %get-tuple-element.597.du, bf16[6,344,3072]{2,1,0:T(8,128)(2,1)} %get-tuple-element.598.g), custom_call_target="tpu_custom_call" | custom-call | flops 9739173888 | bytes 23740416 | tf_op jit(solution)/shard_map/ff_weights/pallas_call | solution.py:769
  974.2 52.6 %collective-permute-done.168 = bf16[4,384,768]{2,1,0:T(8,128)(2,1)S(1)} collective-permute-done((bf16[4,384,768]{2,1,0:T(8,128)(2,1)S(1)}, bf16[4,384,768]{2,1,0:T(8,128)(2,1)S(1)}, u32[]{:S(2)}, u32[]{:S(2)}) %collective-permute-start.168) | collective-permute-done | bytes 2359328 | tf_op jit(solution)/shard_map/ppermute | solution.py:837
  1041.9 23.5 %reduce-scatter.12.cloned.1.call-done = bf16[1,288,768]{2,1,0:T(8,128)(2,1)} async-done(((bf16[4,288,768]{2,1,0:T(8,128)(2,1)}), bf16[1,288,768]{2,1,0:T(8,128)(2,1)}) %reduce-scatter.12.cloned.1.call-update) | async-done | bytes 442384 | tf_op jit(solution)/shard_map/reduce_scatter | solution.py:970
  1069.4 38.9 %reduce-scatter.10.cloned.1.call-done = bf16[1,240,960]{2,1,0:T(8,128)(2,1)} async-done(((bf16[4,240,960]{2,1,0:T(8,128)(2,1)}), bf16[1,240,960]{2,1,0:T(8,128)(2,1)}) %reduce-scatter.10.cloned.1.call-update) | async-done | bytes 460816 | tf_op jit(solution)/shard_map/reduce_scatter | solution.py:970
  1112.4 45.3 %reduce-scatter.14.cloned.1.call-done = bf16[1,384,768]{2,1,0:T(8,128)(2,1)} async-done(((bf16[4,384,768]{2,1,0:T(8,128)(2,1)}), bf16[1,384,768]{2,1,0:T(8,128)(2,1)}) %reduce-scatter.14.cloned.1.call-update) | async-done | bytes 589840 | tf_op jit(solution)/shard_map/reduce_scatter | solution.py:970
  (932 shorter events, 601.7 us)
Async XLA Ops:
  7.2 1031.9 %reduce-scatter.16.cloned.1.call-start = ((), (), s32[]{:S(2)}) async-start(), calls=%async_computation.8 | async-start | bytes 417792
  25.9 55.0 %collective-permute-start.12 = (bf16[768,768]{1,0:T(8,128)(2,1)}, bf16[768,768]{1,0:T(8,128)(2,1)}, u32[]{:S(2)}, u32[]{:S(2)}) collective-permute-start(bf16[768,768]{1,0:T(8,128)(2,1)} %bitcast.16), channel_id=1, source_target_pairs={{0,2},{1,3},{2,0},{3,1},{4,6},{5,7},{6,4},{7,5},{8,10},{9,11},{10,... | collective-permute-start | bytes 3538952 | tf_op jit(solution)/shard_map/ppermute | solution.py:837
  40.6 58.5 %collective-permute-start.15 = (bf16[768,768]{1,0:T(8,128)(2,1)S(1)}, bf16[768,768]{1,0:T(8,128)(2,1)S(1)}, u32[]{:S(2)}, u32[]{:S(2)}) collective-permute-start(bf16[768,768]{1,0:T(8,128)(2,1)S(1)} %bitcast.114), channel_id=1, source_target_pairs={{0,2},{1,3},{2,0},{3,1},{4,6},{5,7},{6,4},{7,5},{8,10},{9,11},{10,... | collective-permute-start | bytes 3538952 | tf_op jit(solution)/shard_map/ppermute | solution.py:837
  221.3 50.0 %collective-permute-start.50 = (bf16[144,768]{1,0:T(8,128)(2,1)}, bf16[144,768]{1,0:T(8,128)(2,1)S(1)}, u32[]{:S(2)}, u32[]{:S(2)}) collective-permute-start(bf16[144,768]{1,0:T(8,128)(2,1)} %get-tuple-element.370), channel_id=1, source_target_pairs={{0,1},{1,0},{2,3},{3,2},{4,5},{5,4},{6,7},{7,6},{8,9},{9,8},{10,11... | collective-permute-start | bytes 663560 | tf_op jit(solution)/shard_map/ppermute | solution.py:841
  230.2 43.0 %collective-permute-start.23 = (bf16[144,768]{1,0:T(8,128)(2,1)}, bf16[144,768]{1,0:T(8,128)(2,1)S(1)}, u32[]{:S(2)}, u32[]{:S(2)}) collective-permute-start(bf16[144,768]{1,0:T(8,128)(2,1)} %get-tuple-element.335), channel_id=1, source_target_pairs={{0,1},{1,0},{2,3},{3,2},{4,5},{5,4},{6,7},{7,6},{8,9},{9,8},{10,11... | collective-permute-start | bytes 663560 | tf_op jit(solution)/shard_map/ppermute | solution.py:841
  367.2 51.4 %collective-permute-start.78 = (bf16[144,768]{1,0:T(8,128)(2,1)}, bf16[144,768]{1,0:T(8,128)(2,1)S(1)}, u32[]{:S(2)}, u32[]{:S(2)}) collective-permute-start(bf16[144,768]{1,0:T(8,128)(2,1)} %get-tuple-element.404), channel_id=1, source_target_pairs={{0,1},{1,0},{2,3},{3,2},{4,5},{5,4},{6,7},{7,6},{8,9},{9,8},{10,11... | collective-permute-start | bytes 663560 | tf_op jit(solution)/shard_map/ppermute | solution.py:841
  376.1 43.0 %collective-permute-start.63 = (bf16[144,768]{1,0:T(8,128)(2,1)}, bf16[144,768]{1,0:T(8,128)(2,1)S(1)}, u32[]{:S(2)}, u32[]{:S(2)}) collective-permute-start(bf16[144,768]{1,0:T(8,128)(2,1)} %get-tuple-element.385), channel_id=1, source_target_pairs={{0,1},{1,0},{2,3},{3,2},{4,5},{5,4},{6,7},{7,6},{8,9},{9,8},{10,11... | collective-permute-start | bytes 663560 | tf_op jit(solution)/shard_map/ppermute | solution.py:841
  515.8 40.5 %collective-permute-start.88 = (bf16[144,768]{1,0:T(8,128)(2,1)S(1)}, bf16[144,768]{1,0:T(8,128)(2,1)S(1)}, u32[]{:S(2)}, u32[]{:S(2)}) collective-permute-start(bf16[144,768]{1,0:T(8,128)(2,1)S(1)} %collective-permute-done.86.p1), channel_id=1, source_target_pairs={{0,1},{1,0},{2,3},{3,2},{4,5},{5,4},{6,7},{7,6},{8,9},{9,8},{10,11... | collective-permute-start | bytes 663560 | tf_op jit(solution)/shard_map/ppermute | solution.py:841
  530.2 40.9 %collective-permute-start.106 = (bf16[144,768]{1,0:T(8,128)(2,1)}, bf16[144,768]{1,0:T(8,128)(2,1)S(1)}, u32[]{:S(2)}, u32[]{:S(2)}) collective-permute-start(bf16[144,768]{1,0:T(8,128)(2,1)} %get-tuple-element.461), channel_id=1, source_target_pairs={{0,1},{1,0},{2,3},{3,2},{4,5},{5,4},{6,7},{7,6},{8,9},{9,8},{10,11... | collective-permute-start | bytes 663560 | tf_op jit(solution)/shard_map/ppermute | solution.py:841
  642.2 39.7 %collective-permute-start.118 = (bf16[200,768]{1,0:T(8,128)(2,1)}, bf16[200,768]{1,0:T(8,128)(2,1)S(1)}, u32[]{:S(2)}, u32[]{:S(2)}) collective-permute-start(bf16[200,768]{1,0:T(8,128)(2,1)} %get-tuple-element.481.p0), channel_id=1, source_target_pairs={{0,1},{1,0},{2,3},{3,2},{4,5},{5,4},{6,7},{7,6},{8,9},{9,8},{10,11... | collective-permute-start | bytes 921608 | tf_op jit(solution)/shard_map/ppermute | solution.py:841
  665.7 39.1 %collective-permute-start.115 = (bf16[144,768]{1,0:T(8,128)(2,1)S(1)}, bf16[144,768]{1,0:T(8,128)(2,1)S(1)}, u32[]{:S(2)}, u32[]{:S(2)}) collective-permute-start(bf16[144,768]{1,0:T(8,128)(2,1)S(1)} %copy-done.192), channel_id=1, source_target_pairs={{0,1},{1,0},{2,3},{3,2},{4,5},{5,4},{6,7},{7,6},{8,9},{9,8},{10,11... | collective-permute-start | bytes 663560 | tf_op jit(solution)/shard_map/ppermute | solution.py:841
  665.8 39.5 %collective-permute-start.116 = (bf16[144,768]{1,0:T(8,128)(2,1)S(1)}, bf16[144,768]{1,0:T(8,128)(2,1)S(1)}, u32[]{:S(2)}, u32[]{:S(2)}) collective-permute-start(bf16[144,768]{1,0:T(8,128)(2,1)S(1)} %collective-permute-done.114.p1), channel_id=1, source_target_pairs={{0,1},{1,0},{2,3},{3,2},{4,5},{5,4},{6,7},{7,6},{8,9},{9,8},{10,11... | collective-permute-start | bytes 663560 | tf_op jit(solution)/shard_map/ppermute | solution.py:841
  681.4 42.3 %collective-permute-start.134 = (bf16[144,768]{1,0:T(8,128)(2,1)}, bf16[144,768]{1,0:T(8,128)(2,1)S(1)}, u32[]{:S(2)}, u32[]{:S(2)}) collective-permute-start(bf16[144,768]{1,0:T(8,128)(2,1)} %get-tuple-element.519), channel_id=1, source_target_pairs={{0,1},{1,0},{2,3},{3,2},{4,5},{5,4},{6,7},{7,6},{8,9},{9,8},{10,11... | collective-permute-start | bytes 663560 | tf_op jit(solution)/shard_map/ppermute | solution.py:841
  681.9 39.0 %collective-permute-start.135 = (bf16[144,768]{1,0:T(8,128)(2,1)}, bf16[144,768]{1,0:T(8,128)(2,1)S(1)}, u32[]{:S(2)}, u32[]{:S(2)}) collective-permute-start(bf16[144,768]{1,0:T(8,128)(2,1)} %get-tuple-element.521), channel_id=1, source_target_pairs={{0,1},{1,0},{2,3},{3,2},{4,5},{5,4},{6,7},{7,6},{8,9},{9,8},{10,11... | collective-permute-start | bytes 663560 | tf_op jit(solution)/shard_map/ppermute | solution.py:841
  682.0 41.8 %collective-permute-start.137 = (bf16[200,768]{1,0:T(8,128)(2,1)S(1)}, bf16[200,768]{1,0:T(8,128)(2,1)S(1)}, u32[]{:S(2)}, u32[]{:S(2)}) collective-permute-start(bf16[200,768]{1,0:T(8,128)(2,1)S(1)} %copy-done.134), channel_id=1, source_target_pairs={{0,1},{1,0},{2,3},{3,2},{4,5},{5,4},{6,7},{7,6},{8,9},{9,8},{10,11... | collective-permute-start | bytes 921608 | tf_op jit(solution)/shard_map/ppermute | solution.py:841
  773.5 48.5 %collective-permute-start.152 = (bf16[144,768]{1,0:T(8,128)(2,1)}, bf16[144,768]{1,0:T(8,128)(2,1)S(1)}, u32[]{:S(2)}, u32[]{:S(2)}) collective-permute-start(bf16[144,768]{1,0:T(8,128)(2,1)} %get-tuple-element.554.p0), channel_id=1, source_target_pairs={{0,1},{1,0},{2,3},{3,2},{4,5},{5,4},{6,7},{7,6},{8,9},{9,8},{10,11... | collective-permute-start | bytes 663560 | tf_op jit(solution)/shard_map/ppermute | solution.py:841
  798.6 62.1 %collective-permute-start.143 = (bf16[144,768]{1,0:T(8,128)(2,1)}, bf16[144,768]{1,0:T(8,128)(2,1)S(1)}, u32[]{:S(2)}, u32[]{:S(2)}) collective-permute-start(bf16[144,768]{1,0:T(8,128)(2,1)} %get-tuple-element.535.p0), channel_id=1, source_target_pairs={{0,1},{1,0},{2,3},{3,2},{4,5},{5,4},{6,7},{7,6},{8,9},{9,8},{10,11... | collective-permute-start | bytes 663560 | tf_op jit(solution)/shard_map/ppermute | solution.py:841
  837.8 41.8 %collective-permute-start.160 = (bf16[144,768]{1,0:T(8,128)(2,1)}, bf16[144,768]{1,0:T(8,128)(2,1)S(1)}, u32[]{:S(2)}, u32[]{:S(2)}) collective-permute-start(bf16[144,768]{1,0:T(8,128)(2,1)} %get-tuple-element.575), channel_id=1, source_target_pairs={{0,1},{1,0},{2,3},{3,2},{4,5},{5,4},{6,7},{7,6},{8,9},{9,8},{10,11... | collective-permute-start | bytes 663560 | tf_op jit(solution)/shard_map/ppermute | solution.py:841
  838.4 43.4 %collective-permute-start.163 = (bf16[200,768]{1,0:T(8,128)(2,1)S(1)}, bf16[200,768]{1,0:T(8,128)(2,1)S(1)}, u32[]{:S(2)}, u32[]{:S(2)}) collective-permute-start(bf16[200,768]{1,0:T(8,128)(2,1)S(1)} %copy-done.132), channel_id=1, source_target_pairs={{0,1},{1,0},{2,3},{3,2},{4,5},{5,4},{6,7},{7,6},{8,9},{9,8},{10,11... | collective-permute-start | bytes 921608 | tf_op jit(solution)/shard_map/ppermute | solution.py:841
  910.1 130.4 %reduce-scatter.18.cloned.1.call-start = ((), (), s32[]{:S(2)}) async-start(), calls=%async_computation.9 | async-start | bytes 417792
  911.1 154.3 %reduce-scatter.12.cloned.1.call-start = ((), (), s32[]{:S(2)}) async-start(), calls=%async_computation.6 | async-start | bytes 2211840 | tf_op jit(solution)/shard_map/reduce_scatter | solution.py:970
  911.8 196.4 %reduce-scatter.10.cloned.1.call-start = ((), (), s32[]{:S(2)}) async-start(), calls=%async_computation.5 | async-start | bytes 2457600 | tf_op jit(solution)/shard_map/reduce_scatter | solution.py:970
  940.6 217.1 %reduce-scatter.14.cloned.1.call-start = ((), (), s32[]{:S(2)}) async-start(), calls=%async_computation.7 | async-start | bytes 2949120 | tf_op jit(solution)/shard_map/reduce_scatter | solution.py:970
  972.3 54.6 %collective-permute-start.168 = (bf16[4,384,768]{2,1,0:T(8,128)(2,1)S(1)}, bf16[4,384,768]{2,1,0:T(8,128)(2,1)S(1)}, u32[]{:S(2)}, u32[]{:S(2)}) collective-permute-start(bf16[4,384,768]{2,1,0:T(8,128)(2,1)S(1)} %add_convert_fusion.1), channel_id=1, source_target_pairs={{0,2},{1,3},{2,0},{3,1},{4,6},{5,7},{6,4},{7,5},{8,10},{9,11},{10,... | collective-permute-start | bytes 7077896 | tf_op jit(solution)/shard_map/ppermute | solution.py:837
  (386 other events, 4575.3 us)
Sparse Core Ops, SparseCore 0:
  910.2 55.7 reduce-scatter.15
  970.5 55.0 reduce-scatter.17
  1027.9 37.4 reduce-scatter.11
  1067.6 40.5 reduce-scatter.9
  1110.5 47.2 reduce-scatter.13

commit v2 on v1

v2 whole, which is shorter than its diff:
```python
import functools

import jax
import jax.numpy as jnp
from jax import lax
from jax.experimental import pallas as pl
from jax.experimental.pallas import tpu as pltpu
from jax.sharding import PartitionSpec as P

HEAD_DIM = 64
WIN = 12
PATCH_ROWS = 24
PATCH_COLS = 24
SHIFT = WIN // 2

EPSILON = 1e-05
MASKED_SCORE = -1000000000.0
SCALE = HEAD_DIM**-0.5
GELU_C = 0.7978845608028654
GELU_A = 0.044715

VMEM_MIB = 56
SKEW = 2
SELF_BLOCK = 256
CROSS_BLOCK = 1024

F32 = jnp.float32
BF16 = jnp.bfloat16

FLIPS = (0, 2, 1, 3)
AT_SLOT, AT_BLOCK, AT_SECTION, AT_MP, AT_LENGTH, AT_VALID, AT_STACK = 0, 4, 8, 9, 16, 32, 48


def dot(left, right):
    return lax.dot_general(left, right, (((1,), (0,)), ((), ())), preferred_element_type=F32)


def dot_nt(left, right):
    return lax.dot_general(left, right, (((1,), (1,)), ((), ())), preferred_element_type=F32)


def dot_tn(left, right):
    return lax.dot_general(left, right, (((0,), (0,)), ((), ())), preferred_element_type=F32)


def head_mask(head, width, scale):
    lane = lax.broadcasted_iota(jnp.int32, (1, width), 1)
    inside = (lane >= head * HEAD_DIM) & (lane < (head + 1) * HEAD_DIM)
    return jnp.where(inside, F32(scale), F32(0.0)).astype(BF16)


def normalized(values):
    average = jnp.mean(values, axis=-1, keepdims=True)
    centered = values - average
    variance = jnp.mean(centered * centered, axis=-1, keepdims=True)
    inverse = lax.rsqrt(variance + EPSILON)
    return centered * inverse, inverse


def norm_pull(grad, values, gain):
    unit, inverse = normalized(values)
    scaled = grad * gain
    first = jnp.mean(scaled, axis=-1, keepdims=True)
    second = jnp.mean(scaled * unit, axis=-1, keepdims=True)
    pulled = inverse * (scaled - first - unit * second)
    gain_sum = jnp.sum(grad * unit, axis=0, keepdims=True)
    bias_sum = jnp.sum(grad, axis=0, keepdims=True)
    return pulled, gain_sum, bias_sum


SMEM_SPEC = pl.BlockSpec(memory_space=pltpu.SMEM)
ANY_SPEC = pl.BlockSpec(memory_space=pl.ANY)


def whole(*extent):
    zeros = (0,) * len(extent)
    return pl.BlockSpec(extent, lambda *at: zeros, pipeline_mode=pl.Buffered(1))


def params():
    return pltpu.CompilerParams(vmem_limit_bytes=VMEM_MIB << 20)


def cost(flops, moved, exps=0):
    return pl.CostEstimate(flops=int(flops), bytes_accessed=int(moved), transcendentals=int(exps))


def shape_of(extent, dtype):
    return jax.ShapeDtypeStruct(extent, dtype)


class Copies:
    def __init__(self, sems):
        self.sems = sems
        self.used = 0
        self.going = []

    def start(self, source, target):
        copy = pltpu.make_async_copy(source, target, self.sems.at[self.used])
        self.used += 1
        copy.start()
        self.going.append(copy)
        return copy

    def wait(self, *copies):
        for copy in copies:
            copy.wait()
            self.going = [other for other in self.going if other is not copy]

    def finish(self):
        for copy in self.going:
            copy.wait()
        self.going = []


def run(kernel, name, estimate, scalars, arrays, outs, scratch, sems, aliases=()):
    lead = len(scalars)
    return pl.pallas_call(
        kernel,
        out_shape=tuple(outs),
        in_specs=[SMEM_SPEC] * lead + [ANY_SPEC] * len(arrays),
        out_specs=(ANY_SPEC,) * len(outs),
        scratch_shapes=list(scratch) + [pltpu.SemaphoreType.DMA((sems,))],
        input_output_aliases={lead + a: b for a, b in aliases},
        compiler_params=params(),
        cost_estimate=estimate,
        name=name,
    )(*scalars, *arrays)


def entry_kernel(source, tick, info, image, text, got, gain, bias, x, h, own, got_v, norm, xv, hv, sems):
    copies = Copies(sems)
    ni = image.shape[1]
    loads = [
        copies.start(image.at[source], own.at[0:ni]),
        copies.start(text.at[source], own.at[ni:]),
        copies.start(got, got_v),
        copies.start(gain, norm.at[0]),
        copies.start(bias, norm.at[1]),
    ]
    copies.wait(*loads)
    first = info[AT_SECTION] == 0
    values = jnp.where(first, own[...].astype(F32), got_v[...].astype(F32))
    xv[...] = values.astype(BF16)
    unit, _ = normalized(values)
    hv[...] = (unit * norm[0, 0:1, :] + norm[1, 0:1, :]).astype(BF16)
    copies.start(hv, h)
    copies.start(xv, x)
    copies.finish()


def entry(tick, info, source, image, text, got, gain, bias):
    n, d = got.shape
    return run(
        functools.partial(entry_kernel, source),
        "entry_norm",
        cost(10 * n * d, 8 * n * d),
        (tick, info),
        (image, text, got, gain, bias),
        (shape_of((n, d), BF16),) * 2,
        [pltpu.VMEM((n, d), BF16), pltpu.VMEM((n, d), BF16), pltpu.VMEM((2, 2, d), F32)]
        + [pltpu.VMEM((n, d), BF16)] * 2,
        7,
    )


def image_forward_kernel(
    tick, info, p0, p1, p2, p3, w, wo, gidc, gidr, *refs
):
    refs = refs[-(8 + 12) :]
    r0, r1, r23, qkv, ot, tt, hx, o = refs[:8]
    hx_v, w_v, wo_v, gidc_v, gidr_v, qkv_v, ot_v, tt_v, o_v, part, v_tall, sems = refs[8:]
    copies = Copies(sems)
    rows, d = hx_v.shape
    shard = rows // 4
    band = ot_v.shape[2]
    width = wo_v.shape[0]
    heads = width // HEAD_DIM
    slot = info[AT_STACK + tick[0]]
    offs = [pl.multiple_of(info[AT_SLOT + i] * shard, 16) for i in range(4)]
    loads = [
        copies.start(piece.at[0:shard], hx_v.at[pl.ds(off, shard)])
        for off, piece in zip(offs, (p0, p1, p2, p3))
    ] + [copies.start(w, w_v)]
    more = [copies.start(a, b) for a, b in ((gidc, gidc_v), (gidr, gidr_v), (wo, wo_v))]
    copies.wait(*loads)
    projected = dot(hx_v[...], w_v[...])
    for j in range(5):
        qkv_v[j] = projected[:, j * width : (j + 1) * width].astype(BF16)
    copies.start(hx_v, hx.at[slot])
    copies.start(qkv_v, qkv)
    copies.wait(*more)
    for b in range(2):
        span = slice(b * band, (b + 1) * band)
        bias = jnp.where(gidc_v[span, :] == gidr_v[0:1, span], F32(0.0), F32(MASKED_SCORE))
        v_tall[...] = qkv_v[4, span, :].astype(F32).T.astype(BF16)
        for head in range(heads):
            query = qkv_v[2, span, :] * head_mask(head, width, SCALE)
            scores = dot_nt(qkv_v[3, span, :], query) + bias
            largest = jnp.max(scores, axis=0, keepdims=True)
            weights = jnp.exp(scores - largest)
            total = jnp.sum(weights, axis=0, keepdims=True)
            tt_v[b * heads + head] = largest + jnp.log(total)
            at = head * HEAD_DIM
            mixed = dot(v_tall[at : at + HEAD_DIM, :], weights.astype(BF16))
            ot_v[b, at : at + HEAD_DIM, :] = mixed * (1.0 / total)
        o_v[span, :] = ot_v[b].T.astype(BF16)
    copies.start(ot_v, ot)
    copies.start(tt_v, tt)
    copies.start(o_v, o.at[slot])
    part[...] = dot(o_v[...], wo_v[...]).astype(BF16)
    for off, piece in zip(offs, (r0, r1, r23.at[0], r23.at[1])):
        copies.start(part.at[pl.ds(off, shard)], piece.at[0:shard])
    copies.finish()


def image_forward(tick, info, shard, micro, pieces, w, wo, gidc, gidr, stacks):
    n, d = pieces[0].shape
    rows = 4 * shard
    width = wo.shape[0]
    band = rows // 2
    heads = width // HEAD_DIM
    return run(
        image_forward_kernel,
        "image_forward",
        cost(
            2 * rows * d * width * 6 + 8 * heads * band * band * 256,
            2 * rows * d * 3 + 12 * rows * width + 12 * d * width,
            2 * heads * band * band,
        ),
        (tick, info),
        (*pieces, w, wo, gidc, gidr, *stacks),
        (
            shape_of((n, d), BF16),
            shape_of((n, d), BF16),
            shape_of((2, n, d), BF16),
            shape_of((5, rows, width), BF16),
            shape_of((2, width, band), F32),
            shape_of((2 * heads, 1, band), F32),
            shape_of((micro + 1, rows, d), BF16),
            shape_of((micro + 1, rows, width), BF16),
        ),
        [
            pltpu.VMEM((rows, d), BF16),
            pltpu.VMEM(w.shape, BF16),
            pltpu.VMEM(wo.shape, BF16),
            pltpu.VMEM(gidc.shape, jnp.int32),
            pltpu.VMEM(gidr.shape, jnp.int32),
            pltpu.VMEM((5, rows, width), BF16),
            pltpu.VMEM((2, width, band), F32),
            pltpu.VMEM((2 * heads, 1, band), F32),
            pltpu.VMEM((rows, width), BF16),
            pltpu.VMEM((rows, d), BF16),
            pltpu.VMEM((width, band), BF16),
        ],
        18,
        ((8, 6), (9, 7)) if stacks else (),
    )


def image_backward_kernel(tick, info, p0, p1, p2, p3, w, wo, gidc, gidr, qkv, ot, tt, dkv, *refs):
    refs = refs[-(5 + 18) :]
    r0, r1, r23, da, dd = refs[:5]
    (
        da_v, w_v, wo_v, gidc_v, gidr_v, qkv_v, ot_v, tt_v, dkv_v, do_v, d_v, part,
        dq_tall, k_tall, do_tall, dk_sum, dv_sum, sems,
    ) = refs[5:]
    copies = Copies(sems)
    rows, d = da_v.shape
    shard = rows // 4
    band = ot_v.shape[2]
    width = wo_v.shape[0]
    heads = width // HEAD_DIM
    slot = info[AT_STACK + tick[0]]
    offs = [pl.multiple_of(info[AT_SLOT + i] * shard, 16) for i in range(4)]
    loads = [
        copies.start(piece.at[0:shard], da_v.at[pl.ds(off, shard)])
        for off, piece in zip(offs, (p0, p1, p2, p3))
    ] + [copies.start(wo, wo_v)]
    more = [
        copies.start(a, b)
        for a, b in ((qkv, qkv_v), (gidc, gidc_v), (gidr, gidr_v), (tt, tt_v), (ot, ot_v))
    ]
    rest = [copies.start(a, b) for a, b in ((dkv, dkv_v), (w, w_v))]
    copies.wait(*loads)
    copies.start(da_v, da.at[slot])
    do_v[...] = dot_nt(da_v[...], wo_v[...]).astype(BF16)
    copies.wait(*more)
    for b in range(2):
        span = slice(b * band, (b + 1) * band)
        bias = jnp.where(gidc_v[span, :] == gidr_v[0:1, span], F32(0.0), F32(MASKED_SCORE))
        k_tall[...] = qkv_v[3, span, :].astype(F32).T.astype(BF16)
        do_tall[...] = do_v[span, :].astype(F32).T
        dk_sum[...] = jnp.zeros_like(dk_sum)
        dv_sum[...] = jnp.zeros_like(dv_sum)
        for head in range(heads):
            at = head * HEAD_DIM
            own = slice(at, at + HEAD_DIM)
            query = qkv_v[2, span, :] * head_mask(head, width, SCALE)
            grad = do_v[span, :] * head_mask(head, width, 1.0)
            scores = dot_nt(qkv_v[3, span, :], query) + bias
            weights = jnp.exp(scores - tt_v[b * heads + head])
            pulled = dot_nt(qkv_v[4, span, :], grad)
            delta = jnp.sum(do_tall[own, :] * ot_v[b, own, :], axis=0, keepdims=True)
            score_grad = (weights * (pulled - delta)).astype(BF16)
            dv_sum[...] += dot(weights.astype(BF16), grad)
            dk_sum[...] += dot(score_grad, query)
            dq_tall[own, :] = dot(k_tall[own, :], score_grad) * SCALE
        d_v[span, 2 * width : 3 * width] = dq_tall[...].T.astype(BF16)
        d_v[span, 3 * width : 4 * width] = dk_sum[...].astype(BF16)
        d_v[span, 4 * width :] = dv_sum[...].astype(BF16)
    copies.wait(*rest)
    d_v[:, 0:width] = dkv_v[0]
    d_v[:, width : 2 * width] = dkv_v[1]
    copies.start(d_v, dd.at[slot])
    part[...] = dot_nt(d_v[...], w_v[...]).astype(BF16)
    for off, piece in zip(offs, (r0, r1, r23.at[0], r23.at[1])):
        copies.start(part.at[pl.ds(off, shard)], piece.at[0:shard])
    copies.finish()


def image_backward(tick, info, shard, micro, pieces, w, wo, gidc, gidr, qkv, ot, tt, dkv, parts, stacks):
    n, d = pieces[0].shape
    rows = 4 * shard
    width = wo.shape[0]
    band = rows // 2
    heads = width // HEAD_DIM
    return run(
        image_backward_kernel,
        "image_backward",
        cost(
            2 * rows * d * width * 6 + 20 * heads * band * band * 256,
            2 * rows * d * 3 + 20 * rows * width + 12 * d * width,
            2 * heads * band * band,
        ),
        (tick, info),
        (*pieces, w, wo, gidc, gidr, qkv, ot, tt, dkv, *parts, *stacks),
        (
            shape_of((n, d), BF16),
            shape_of((n, d), BF16),
            shape_of((2, n, d), BF16),
            shape_of((micro + 1, rows, d), BF16),
            shape_of((micro + 1, rows, 5 * width), BF16),
        ),
        [
            pltpu.VMEM((rows, d), BF16),
            pltpu.VMEM(w.shape, BF16),
            pltpu.VMEM(wo.shape, BF16),
            pltpu.VMEM(gidc.shape, jnp.int32),
            pltpu.VMEM(gidr.shape, jnp.int32),
            pltpu.VMEM((5, rows, width), BF16),
            pltpu.VMEM((2, width, band), F32),
            pltpu.VMEM((2 * heads, 1, band), F32),
            pltpu.VMEM((2, rows, width), BF16),
            pltpu.VMEM((rows, width), BF16),
            pltpu.VMEM((rows, 5 * width), BF16),
            pltpu.VMEM((rows, d), BF16),
            pltpu.VMEM((width, band), F32),
            pltpu.VMEM((width, band), BF16),
            pltpu.VMEM((width, band), F32),
            pltpu.VMEM((band, width), F32),
            pltpu.VMEM((band, width), F32),
        ],
        18,
        ((12, 0), (13, 1), (14, 2)) + (((15, 3), (16, 4)) if stacks else ()),
    )


def query_blocks(rows, size):
    return [(at, min(size, rows - at)) for at in range(0, rows, size)]


def causal(scores, start, last_key):
    key_at = lax.broadcasted_iota(jnp.int32, scores.shape, 0)
    query_at = lax.broadcasted_iota(jnp.int32, (1, scores.shape[1]), 1) + start
    return jnp.where(key_at <= jnp.minimum(query_at, last_key), scores, F32(MASKED_SCORE))


def text_forward_kernel(skip, tick, info, p0, p1, p2, p3, w, wo, kv, *refs):
    refs = refs[-(8 + 11) :]
    r0, r1, r23, qkv, ot, tt, hy, o = refs[:8]
    hy_v, w_v, wo_v, kv_v, qkv_v, ot_v, tt_v, o_v, part, piece_v, sems = refs[8:]
    copies = Copies(sems)
    rows, d = hy_v.shape
    shard = rows // 4
    patches = kv_v.shape[1]
    width = kv_v.shape[2]
    heads = width // HEAD_DIM
    slot = info[AT_STACK + tick[0]]
    last_key = info[AT_LENGTH + tick[0]] - 1
    offs = [pl.multiple_of(info[AT_BLOCK + i] * shard, 8) for i in range(4)]
    loads = [
        copies.start(piece.at[skip:], piece_v.at[i]) for i, piece in enumerate((p0, p1, p2, p3))
    ] + [copies.start(w, w_v)]
    more = [copies.start(kv.at[0:2], kv_v)]
    rest = [copies.start(wo, wo_v)]
    copies.wait(*loads)
    for i, off in enumerate(offs):
        part[pl.ds(off, shard), :] = piece_v[i].astype(F32)
    hy_v[...] = part[...].astype(BF16)
    projected = dot(hy_v[...], w_v[...])
    for j in range(4):
        qkv_v[j] = projected[:, j * width : (j + 1) * width].astype(BF16)
    copies.start(hy_v, hy.at[slot])
    copies.start(qkv_v, qkv)
    copies.wait(*more)
    for kind in range(2):
        values = qkv_v[2] if kind == 0 else kv_v[1]
        v_tall = values.astype(F32).T.astype(BF16)
        for start, size in query_blocks(rows, CROSS_BLOCK if kind else SELF_BLOCK):
            seen = start + size if kind == 0 else patches
            for head in range(heads):
                at = head * HEAD_DIM
                mask = head_mask(head, width, SCALE)
                query = qkv_v[3 if kind else 0, start : start + size, :] * mask
                keys = kv_v[0] if kind else qkv_v[1, 0:seen, :]
                scores = dot_nt(keys, query)
                if kind == 0:
                    scores = causal(scores, start, last_key)
                largest = jnp.max(scores, axis=0, keepdims=True)
                weights = jnp.exp(scores - largest)
                total = jnp.sum(weights, axis=0, keepdims=True)
                tt_v[kind * heads + head, :, start : start + size] = largest + jnp.log(total)
                mixed = dot(v_tall[at : at + HEAD_DIM, 0:seen], weights.astype(BF16))
                out_at = kind * width + at
                ot_v[out_at : out_at + HEAD_DIM, start : start + size] = mixed * (1.0 / total)
    copies.start(ot_v, ot)
    copies.start(tt_v, tt)
    o_v[...] = ot_v[...].T.astype(BF16)
    copies.start(o_v, o.at[slot])
    copies.wait(*rest)
    part[...] = dot(o_v[...], wo_v[...])
    for i, (off, piece) in enumerate(zip(offs, (r0, r1, r23.at[0], r23.at[1]))):
        piece_v[i] = part[pl.ds(off, shard), :].astype(BF16)
        copies.start(piece_v.at[i], piece.at[skip:])
    copies.finish()


def text_forward(tick, info, shard, micro, pieces, w, wo, kv, parts, stacks):
    n, d = pieces[0].shape
    rows = 4 * shard
    patches, width = kv.shape[1:]
    heads = width // HEAD_DIM
    return run(
        functools.partial(text_forward_kernel, n - shard),
        "text_forward",
        cost(
            2 * rows * d * width * 6 + 4 * heads * rows * (rows * 0.6 + patches) * 256,
            2 * rows * d * 3 + 12 * rows * width + 12 * d * width,
            heads * rows * (rows * 0.6 + patches),
        ),
        (tick, info),
        (*pieces, w, wo, kv, *parts, *stacks),
        (
            shape_of((n, d), BF16),
            shape_of((n, d), BF16),
            shape_of((2, n, d), BF16),
            shape_of((4, rows, width), BF16),
            shape_of((2 * width, rows), F32),
            shape_of((2 * heads, 1, rows), F32),
            shape_of((micro + 1, rows, d), BF16),
            shape_of((micro + 1, rows, 2 * width), BF16),
        ),
        [
            pltpu.VMEM((rows, d), BF16),
            pltpu.VMEM(w.shape, BF16),
            pltpu.VMEM(wo.shape, BF16),
            pltpu.VMEM((2, patches, width), BF16),
            pltpu.VMEM((4, rows, width), BF16),
            pltpu.VMEM((2 * width, rows), F32),
            pltpu.VMEM((2 * heads, 1, rows), F32),
            pltpu.VMEM((rows, 2 * width), BF16),
            pltpu.VMEM((rows, d), F32),
            pltpu.VMEM((4, shard, d), BF16),
        ],
        16,
        ((7, 0), (8, 1), (9, 2)) + (((10, 6), (11, 7)) if stacks else ()),
    )


def text_backward_kernel(skip, tick, info, p0, p1, p2, p3, w, wo, kv, qkv, ot, tt, *refs):
    refs = refs[-(6 + 18) :]
    r0, r1, r23, dkv, da, dd = refs[:6]
    (
        da_v, w_v, wo_v, kv_v, qkv_v, ot_v, tt_v, do_v, d_v, dkv_v, part, piece_v,
        dq_tall, k_tall, do_tall, dk_sum, dv_sum, sems,
    ) = refs[6:]
    copies = Copies(sems)
    rows, d = da_v.shape
    shard = rows // 4
    patches, width = kv_v.shape[1:]
    heads = width // HEAD_DIM
    slot = info[AT_STACK + tick[0]]
    last_key = info[AT_LENGTH + tick[0]] - 1
    offs = [pl.multiple_of(info[AT_BLOCK + i] * shard, 8) for i in range(4)]
    loads = [
        copies.start(piece.at[skip:], piece_v.at[i]) for i, piece in enumerate((p0, p1, p2, p3))
    ] + [copies.start(wo, wo_v)]
    more = [copies.start(a, b) for a, b in ((qkv, qkv_v), (tt, tt_v), (ot, ot_v), (kv.at[0:2], kv_v))]
    rest = [copies.start(w, w_v)]
    copies.wait(*loads)
    for i, off in enumerate(offs):
        part[pl.ds(off, shard), :] = piece_v[i].astype(F32)
    da_v[...] = part[...].astype(BF16)
    copies.start(da_v, da.at[slot])
    grads = dot_nt(da_v[...], wo_v[...])
    do_v[...] = grads.astype(BF16)
    do_tall[...] = grads.astype(BF16).astype(F32).T
    copies.wait(*more)
    for kind in range(2):
        span = patches if kind else rows
        whole_keys = kv_v[0] if kind else qkv_v[1]
        k_tall[:, 0:span] = whole_keys.astype(F32).T.astype(BF16)
        dk_sum[...] = jnp.zeros_like(dk_sum)
        dv_sum[...] = jnp.zeros_like(dv_sum)
        for start, size in query_blocks(rows, CROSS_BLOCK if kind else SELF_BLOCK):
            seen = start + size if kind == 0 else patches
            block = slice(start, start + size)
            keys = kv_v[0] if kind else qkv_v[1, 0:seen, :]
            values = kv_v[1] if kind else qkv_v[2, 0:seen, :]
            for head in range(heads):
                at = head * HEAD_DIM
                own = slice(at, at + HEAD_DIM)
                out_own = slice(kind * width + at, kind * width + at + HEAD_DIM)
                query = qkv_v[3 if kind else 0, block, :] * head_mask(head, width, SCALE)
                grad = do_v[block, kind * width : (kind + 1) * width] * head_mask(head, width, 1.0)
                scores = dot_nt(keys, query)
                if kind == 0:
                    scores = causal(scores, start, last_key)
                weights = jnp.exp(scores - tt_v[kind * heads + head, :, block])
                pulled = dot_nt(values, grad)
                delta = jnp.sum(do_tall[out_own, block] * ot_v[out_own, block], axis=0, keepdims=True)
                score_grad = (weights * (pulled - delta)).astype(BF16)
                dv_sum[0:seen, :] += dot(weights.astype(BF16), grad)
                dk_sum[0:seen, :] += dot(score_grad, query)
                dq_tall[own, block] = dot(k_tall[own, 0:seen], score_grad) * SCALE
        if kind == 0:
            d_v[:, 0:width] = dq_tall[...].T.astype(BF16)
            d_v[:, width : 2 * width] = dk_sum[...].astype(BF16)
            d_v[:, 2 * width : 3 * width] = dv_sum[...].astype(BF16)
        else:
            d_v[:, 3 * width :] = dq_tall[...].T.astype(BF16)
            dkv_v[0] = dk_sum[0:patches, :].astype(BF16)
            dkv_v[1] = dv_sum[0:patches, :].astype(BF16)
    copies.start(dkv_v, dkv)
    copies.start(d_v, dd.at[slot])
    copies.wait(*rest)
    part[...] = dot_nt(d_v[...], w_v[...])
    for i, (off, piece) in enumerate(zip(offs, (r0, r1, r23.at[0], r23.at[1]))):
        piece_v[i] = part[pl.ds(off, shard), :].astype(BF16)
        copies.start(piece_v.at[i], piece.at[skip:])
    copies.finish()


def text_backward(tick, info, shard, micro, pieces, w, wo, kv, qkv, ot, tt, stacks):
    n, d = pieces[0].shape
    rows = 4 * shard
    patches, width = kv.shape[1:]
    heads = width // HEAD_DIM
    return run(
        functools.partial(text_backward_kernel, n - shard),
        "text_backward",
        cost(
            2 * rows * d * width * 6 + 10 * heads * rows * (rows * 0.6 + patches) * 256,
            2 * rows * d * 3 + 20 * rows * width + 12 * d * width,
            heads * rows * (rows * 0.6 + patches),
        ),
        (tick, info),
        (*pieces, w, wo, kv, qkv, ot, tt, *stacks),
        (
            shape_of((n, d), BF16),
            shape_of((n, d), BF16),
            shape_of((2, n, d), BF16),
            shape_of((2, patches, width), BF16),
            shape_of((micro + 1, rows, d), BF16),
            shape_of((micro + 1, rows, 4 * width), BF16),
        ),
        [
            pltpu.VMEM((rows, d), BF16),
            pltpu.VMEM(w.shape, BF16),
            pltpu.VMEM(wo.shape, BF16),
            pltpu.VMEM((2, patches, width), BF16),
            pltpu.VMEM((4, rows, width), BF16),
            pltpu.VMEM((2 * width, rows), F32),
            pltpu.VMEM((2 * heads, 1, rows), F32),
            pltpu.VMEM((rows, 2 * width), BF16),
            pltpu.VMEM((rows, 4 * width), BF16),
            pltpu.VMEM((2, patches, width), BF16),
            pltpu.VMEM((rows, d), F32),
            pltpu.VMEM((4, shard, d), BF16),
            pltpu.VMEM((width, rows), F32),
            pltpu.VMEM((width, rows), BF16),
            pltpu.VMEM((2 * width, rows), F32),
            pltpu.VMEM((rows, width), F32),
            pltpu.VMEM((rows, width), F32),
        ],
        18,
        ((10, 4), (11, 5)) if stacks else (),
    )


def attention_weights_kernel(h, dd, o, da, out, w_sum, wo_sum):
    step = pl.program_id(0)
    w_part = dot_tn(h[0], dd[0])
    wo_part = dot_tn(o[0], da[0])

    @pl.when(step == 0)
    def _():
        w_sum[...] = w_part
        wo_sum[...] = wo_part

    @pl.when(step > 0)
    def _():
        w_sum[...] += w_part
        wo_sum[...] += wo_part

    @pl.when(step == pl.num_programs(0) - 1)
    def _():
        chunks = out.shape[0]
        d, columns = w_sum.shape
        rows, wide = d // chunks, wo_sum.shape[1]
        at = rows
        for z in range(chunks):
            out[z, 0:rows, :] = w_sum[z * rows : (z + 1) * rows, :].astype(BF16)
        narrow = d // 4 // chunks
        for part in range(wo_sum.shape[0] // (d // 4)):
            for z in range(chunks):
                top = part * (d // 4) + z * narrow
                out[z, at : at + narrow, 0:wide] = wo_sum[top : top + narrow, :].astype(BF16)
                if columns > wide:
                    out[z, at : at + narrow, wide:] = jnp.zeros((narrow, columns - wide), BF16)
            at += narrow


def attention_weights(h, dd, o, da, chunks, name):
    slots, rows, d = h.shape
    columns, wide = dd.shape[2], o.shape[2]
    out = (chunks, (d + wide) // chunks, columns)
    slot = lambda a: pl.BlockSpec((1, *a.shape[1:]), lambda i: (i, 0, 0))
    return pl.pallas_call(
        attention_weights_kernel,
        grid=(slots - 1,),
        out_shape=shape_of(out, BF16),
        in_specs=[slot(a) for a in (h, dd, o, da)],
        out_specs=whole(*out),
        scratch_shapes=[pltpu.VMEM((d, columns), F32), pltpu.VMEM((wide, d), F32)],
        compiler_params=params(),
        cost_estimate=cost(
            2 * slots * rows * d * (columns + wide), 2 * slots * rows * (2 * d + columns + wide)
        ),
        name=name,
    )(h, dd, o, da)


def ff_forward_kernel(ni, tick, info, x, a, b, c, gain, bias, u0, u1, u2, u3, d0, d1, d2, d3, *refs):
    refs = refs[-(7 + 11) :]
    mid, gp, z, h2, g, image_out, text_out = refs[:7]
    x_v, abc, norm, up, down, mid_v, h2_v, g_v, gp_v, z_v, sems = refs[7:]
    copies = Copies(sems)
    n, d = x_v.shape
    hidden = up.shape[2]
    slot = info[AT_STACK + tick[0]]
    at_row = pl.multiple_of(slot * n, 8)
    loads = [
        copies.start(s, t)
        for s, t in (
            (x, x_v),
            (a, abc.at[0]),
            (b.at[0], abc.at[1]),
            (c, abc.at[2]),
            (gain, norm.at[0]),
            (bias, norm.at[1]),
        )
    ]
    weights = [
        (copies.start(u, up.at[i]), copies.start(w, down.at[i]))
        for i, (u, w) in enumerate(zip((u0, u1, u2, u3), (d0, d1, d2, d3)))
    ]
    copies.wait(*loads)
    values = x_v[...].astype(F32) + (
        abc[0].astype(F32) + abc[1].astype(F32) + abc[2].astype(F32)
    )
    mid_v[...] = values
    unit, _ = normalized(values)
    h2_v[...] = (unit * norm[0, 1:2, :] + norm[1, 1:2, :]).astype(BF16)
    copies.start(mid_v, mid)
    copies.start(h2_v, h2.at[pl.ds(at_row, n)])

    def ascend(i):
        copies.wait(weights[i][0])
        return dot(h2_v[...], up[i])

    def bend(i, u):
        square = u * u
        bent = jnp.tanh(u * (GELU_C + (GELU_C * GELU_A) * square))
        half = 0.5 * (1.0 + bent)
        g_v[i] = (u * half).astype(BF16)
        slope = half + (0.5 * u) * (1.0 - bent * bent) * (GELU_C + (3.0 * GELU_C * GELU_A) * square)
        gp_v[i] = slope.astype(BF16)
        columns = slice(i * hidden, (i + 1) * hidden)
        copies.start(g_v.at[i], g.at[pl.ds(at_row, n), columns])
        copies.start(gp_v.at[i], gp.at[:, columns])

    total = mid_v[...]
    u = ascend(0)
    for i in range(4):
        bend(i, u)
        copies.wait(weights[i][1])
        total = total + dot(g_v[i], down[i])
        u = ascend(i + 1) if i < 3 else None
    z_v[...] = total.astype(BF16)
    copies.start(z_v, z)
    copies.finish()

    @pl.when(info[AT_VALID + tick[0]] > 0)
    def _():
        image_copy = pltpu.make_async_copy(z_v.at[0:ni], image_out.at[slot], sems.at[0])
        text_copy = pltpu.make_async_copy(z_v.at[ni:], text_out.at[slot], sems.at[1])
        image_copy.start()
        text_copy.start()
        image_copy.wait()
        text_copy.wait()


def ff_forward(tick, info, ni, micro, x, parts, gain, bias, up, down, stacks):
    n, d = x.shape
    hidden = up[0].shape[1]
    return run(
        functools.partial(ff_forward_kernel, ni),
        "ff_forward",
        cost(16 * n * d * hidden, 16 * d * hidden + 16 * n * hidden + 16 * n * d, 4 * n * hidden),
        (tick, info),
        (x, *parts, gain, bias, *up, *down, *stacks),
        (
            shape_of((n, d), F32),
            shape_of((n, 4 * hidden), BF16),
            shape_of((n, d), BF16),
            shape_of(((micro + 1) * n, d), BF16),
            shape_of(((micro + 1) * n, 4 * hidden), BF16),
            shape_of((micro, ni, d), BF16),
            shape_of((micro, n - ni, d), BF16),
        ),
        [
            pltpu.VMEM((n, d), BF16),
            pltpu.VMEM((3, n, d), BF16),
            pltpu.VMEM((2, 2, d), F32),
            pltpu.VMEM((4, d, hidden), BF16),
            pltpu.VMEM((4, hidden, d), BF16),
            pltpu.VMEM((n, d), F32),
            pltpu.VMEM((n, d), BF16),
            pltpu.VMEM((4, n, hidden), BF16),
            pltpu.VMEM((4, n, hidden), BF16),
            pltpu.VMEM((n, d), BF16),
        ],
        26,
        ((14, 3), (15, 4), (16, 5), (17, 6)) if stacks else (),
    )


def ff_backward_kernel(
    source, tick, info, coti, cott, back, gp, mid, gain, u0, u1, u2, u3, d0, d1, d2, d3, *refs
):
    refs = refs[-(5 + 13) :]
    dmid, da, sums, dm, du = refs[:5]
    cot_v, back_v, gp_v, mid_v, norm, up, down, rows, dm_v, du_v, da_v, sums_v, sems = refs[5:]
    copies = Copies(sems)
    n, d = mid_v.shape
    ni = coti.shape[1]
    nt = n - ni
    hidden = up.shape[2]
    valid = info[AT_VALID + tick[0]].astype(F32)
    slot = info[AT_STACK + tick[0]]
    at_row = pl.multiple_of(slot * n, 8)
    loads = [
        copies.start(coti.at[source], cot_v.at[0:ni]),
        copies.start(cott.at[source], cot_v.at[ni:]),
        copies.start(back, back_v),
    ]
    weights = []
    for i, (u, w) in enumerate(zip((u0, u1, u2, u3), (d0, d1, d2, d3))):
        columns = slice(i * hidden, (i + 1) * hidden)
        weights.append(
            (
                copies.start(w, down.at[i]),
                copies.start(gp.at[:, columns], gp_v.at[i]),
                copies.start(u, up.at[i]),
            )
        )
    rest = [copies.start(mid, mid_v), copies.start(gain, norm)]
    copies.wait(*loads)
    first = info[AT_SECTION] == 0
    place = lax.broadcasted_iota(jnp.int32, (nt, 1), 0) + info[AT_MP] * nt
    kept = (place < info[AT_LENGTH + tick[0]]).astype(F32)
    rows[0:ni, :] = jnp.where(first, back_v[0:ni, :].astype(F32), cot_v[0:ni, :].astype(F32))
    rows[ni:, :] = jnp.where(first, back_v[ni:, :].astype(F32), cot_v[ni:, :].astype(F32) * kept)
    dm_v[...] = rows[...].astype(BF16)
    copies.start(dm_v, dm.at[pl.ds(at_row, n)])

    def descend(i):
        copies.wait(weights[i][0])
        return dot_nt(dm_v[...], down[i])

    total = None
    act_grad = descend(0)
    for i in range(4):
        later = descend(i + 1) if i < 3 else None
        copies.wait(weights[i][1], weights[i][2])
        du_v[i] = (gp_v[i].astype(F32) * act_grad).astype(BF16)
        copies.start(du_v.at[i], du.at[pl.ds(at_row, n), i * hidden : (i + 1) * hidden])
        part = dot_nt(du_v[i], up[i])
        total = part if total is None else total + part
        act_grad = later
    copies.wait(*rest)
    pulled, gain_sum, bias_sum = norm_pull(total, mid_v[...], norm[1:2, :])
    total = rows[...] + pulled
    rows[...] = total
    da_v[...] = total.astype(BF16)
    sums_v[0:1, :] = gain_sum * valid
    sums_v[1:2, :] = bias_sum * valid
    copies.start(da_v, da)
    copies.start(rows, dmid)
    copies.start(sums_v, sums)
    copies.finish()


def ff_backward(tick, info, source, micro, coti, cott, back, gp, mid, gain, up, down, stacks):
    n, d = mid.shape
    hidden = up[0].shape[1]
    return run(
        functools.partial(ff_backward_kernel, source),
        "ff_backward",
        cost(16 * n * d * hidden, 16 * d * hidden + 16 * n * hidden + 16 * n * d),
        (tick, info),
        (coti, cott, back, gp, mid, gain, *up, *down, *stacks),
        (
            shape_of((n, d), F32),
            shape_of((n, d), BF16),
            shape_of((2, d), F32),
            shape_of(((micro + 1) * n, d), BF16),
            shape_of(((micro + 1) * n, 4 * hidden), BF16),
        ),
        [
            pltpu.VMEM((n, d), BF16),
            pltpu.VMEM((n, d), BF16),
            pltpu.VMEM((4, n, hidden), BF16),
            pltpu.VMEM((n, d), F32),
            pltpu.VMEM((2, d), F32),
            pltpu.VMEM((4, d, hidden), BF16),
            pltpu.VMEM((4, hidden, d), BF16),
            pltpu.VMEM((n, d), F32),
            pltpu.VMEM((n, d), BF16),
            pltpu.VMEM((4, n, hidden), BF16),
            pltpu.VMEM((n, d), BF16),
            pltpu.VMEM((2, d), F32),
        ],
        26,
        ((14, 3), (15, 4)) if stacks else (),
    )


def ff_weights_kernel(h2, dm, du, g, one, two):
    piece = pl.program_id(0)
    up_part = dot_tn(h2[...], du[...]).astype(BF16)
    down_part = dot_tn(g[...], dm[...]).astype(BF16)
    for index, out in enumerate((one, two)):

        @pl.when(piece == index)
        def _():
            chunks, rows = out.shape[0], out.shape[1] // 2
            for z in range(chunks):
                span = slice(z * rows, (z + 1) * rows)
                out[z, 0:rows, :] = up_part[span, :]
                out[z, rows:, :] = down_part[span, :]


def ff_weights(pieces, samples, h2, dm, du, g, chunks):
    d = h2.shape[1]
    hidden = du.shape[1] // 4
    n = h2.shape[0] // (samples + 1) * samples
    one, two = pieces
    part = (chunks, 2 * d // chunks, hidden)
    column = lambda i: one + (two - one) * i
    return pl.pallas_call(
        ff_weights_kernel,
        grid=(2,),
        out_shape=(shape_of(part, BF16),) * 2,
        in_specs=[
            whole(n, d),
            whole(n, d),
            pl.BlockSpec((n, hidden), lambda i: (0, column(i))),
            pl.BlockSpec((n, hidden), lambda i: (0, column(i))),
        ],
        out_specs=(whole(*part), whole(*part)),
        compiler_params=params(),
        cost_estimate=cost(8 * n * d * hidden, 4 * n * d + 8 * n * hidden + 8 * d * hidden),
        name="ff_weights",
    )(h2, dm, du, g)


def close_kernel(ni, tick, info, x, a, b, c, dmid, gain, *refs):
    refs = refs[-(4 + 8) :]
    back, sums, image_grad, text_grad = refs[:4]
    x_v, abc, dmid_v, norm, total_v, back_v, sums_v, sems = refs[4:]
    copies = Copies(sems)
    slot = info[AT_STACK + tick[0]]
    loads = [
        copies.start(s, t)
        for s, t in (
            (a, abc.at[0]),
            (b.at[0], abc.at[1]),
            (c, abc.at[2]),
            (x, x_v),
            (gain, norm),
            (dmid, dmid_v),
        )
    ]
    copies.wait(*loads)
    grad = abc[0].astype(F32) + abc[1].astype(F32) + abc[2].astype(F32)
    pulled, gain_sum, bias_sum = norm_pull(grad, x_v[...].astype(F32), norm[0:1, :])
    total = dmid_v[...] + pulled
    total_v[...] = total
    back_v[...] = total.astype(BF16)
    valid = info[AT_VALID + tick[0]]
    sums_v[0:1, :] = gain_sum * valid.astype(F32)
    sums_v[1:2, :] = bias_sum * valid.astype(F32)
    copies.start(back_v, back)
    copies.start(sums_v, sums)

    @pl.when(valid > 0)
    def _():
        image_copy = pltpu.make_async_copy(total_v.at[0:ni], image_grad.at[slot], sems.at[0])
        text_copy = pltpu.make_async_copy(total_v.at[ni:], text_grad.at[slot], sems.at[1])
        image_copy.start()
        text_copy.start()
        image_copy.wait()
        text_copy.wait()

    copies.finish()


def close(tick, info, ni, micro, x, parts, dmid, gain, stacks):
    n, d = x.shape
    return run(
        functools.partial(close_kernel, ni),
        "input_grad",
        cost(20 * n * d, 18 * n * d),
        (tick, info),
        (x, *parts, dmid, gain, *stacks),
        (
            shape_of((n, d), BF16),
            shape_of((2, d), F32),
            shape_of((micro, ni, d), F32),
            shape_of((micro, n - ni, d), F32),
        ),
        [
            pltpu.VMEM((n, d), BF16),
            pltpu.VMEM((3, n, d), BF16),
            pltpu.VMEM((n, d), F32),
            pltpu.VMEM((2, d), F32),
            pltpu.VMEM((n, d), F32),
            pltpu.VMEM((n, d), BF16),
            pltpu.VMEM((2, d), F32),
        ],
        8,
        ((6, 2), (7, 3)) if stacks else (),
    )


def over_y(array):
    return lax.ppermute(array, "mp", [(m, m ^ 2) for m in range(4)])


def over_core(array):
    return lax.ppermute(array, "mp", [(m, m ^ 1) for m in range(4)])


def gathered(own):
    across = over_y(own)
    return (own, across, over_core(own), over_core(across))


def scattered(r0, r1, r23):
    other = over_core(r23)
    across = (r1.astype(F32) + other[1].astype(F32)).astype(BF16)
    return (r0, other, over_y(across))


def shifted(array, by):
    length = lax.axis_size("section")
    return lax.ppermute(array, "section", [(i, i + by) for i in range(length) if 0 <= i + by < length])


def over_everyone(sums):
    groups = lax.axis_size("dp")
    if groups & (groups - 1):
        return lax.psum_scatter(sums, ("dp", "mp"), scatter_dimension=2, tiled=True)
    for flip in (1, 2):
        sums = sums + lax.ppermute(sums, "mp", [(m, m ^ flip) for m in range(4)])
    flip = 1
    while flip < groups:
        sums = sums + lax.ppermute(sums, "dp", [(z, z ^ flip) for z in range(groups)])
        flip *= 2
    own = sums.shape[2] // (4 * groups)
    mine = lax.axis_index("dp") * 4 + lax.axis_index("mp")
    return lax.dynamic_slice_in_dim(sums, mine * own, own, axis=2)


def after(value, *earlier):
    return lax.optimization_barrier((value, *earlier))[0]


def shards(
    image, text, lengths, image_cot, text_cot, qkv_image, out_image, qkv_text, out_text,
    query_cross, kv_cross, out_cross, up_proj, down_proj, norm_gain, norm_bias,
):
    section = lax.axis_index("section")
    me = lax.axis_index("mp")
    groups = lax.axis_size("dp")
    micro = image.shape[0]
    ticks = micro + SKEW
    ni, d = image.shape[1:]
    nt = text.shape[1]
    gain, bias = norm_gain[0], norm_bias[0]
    width = out_image.shape[1]
    w_image = jnp.concatenate(
        (kv_cross[0].reshape(d, 2 * width), qkv_image[0].reshape(d, 3 * width)), axis=1
    )
    w_text = jnp.concatenate((qkv_text[0].reshape(d, 3 * width), query_cross[0]), axis=1)
    wo_image = out_image[0]
    wo_text = jnp.concatenate((out_text[0], out_cross[0]), axis=0)

    flips = jnp.array(FLIPS, jnp.int32)
    turn = jnp.arange(ticks) - section * SKEW
    valid = (turn >= 0) & (turn < micro)
    gap = jnp.zeros((16 - ticks,), jnp.int32)
    info = jnp.concatenate(
        (
            ((me ^ flips) - section) % 4,
            me ^ flips,
            jnp.stack((section, me)).astype(jnp.int32),
            jnp.zeros((AT_LENGTH - 10,), jnp.int32),
            lengths[jnp.clip(turn, 0, micro - 1)],
            gap,
            valid.astype(jnp.int32),
            gap,
            jnp.where(valid, turn, micro).astype(jnp.int32),
        )
    ).astype(jnp.int32)
    place = jnp.arange(4 * ni)
    turned = (place % PATCH_COLS - section * SHIFT) % PATCH_COLS
    edge = PATCH_ROWS - section * SHIFT
    row_region = (place // PATCH_COLS >= PATCH_ROWS - WIN).astype(jnp.int32) + (
        place // PATCH_COLS >= edge
    ).astype(jnp.int32)
    col_region = (turned >= PATCH_COLS - WIN).astype(jnp.int32) + (turned >= edge).astype(jnp.int32)
    region = row_region * 3 + col_region
    gidc = region[:, None]
    gidr = region[None, :]

    tick_at = [jnp.full((1,), t, jnp.int32) for t in range(ticks)]
    nothing = jnp.zeros((ni + nt, d), BF16)
    up = down = None
    image_stacks = text_stacks = ff_stacks = ()
    state = {}
    relayed = {}

    def attend(t):
        nonlocal image_stacks, text_stacks, up, down
        got = relayed.get(t - SKEW, nothing)
        x, h = entry(tick_at[t], info, min(t, micro - 1), image, text, got, gain, bias)
        pieces = gathered(h)
        if up is None:
            up_own, down_own, _ = lax.optimization_barrier((up_proj[0], down_proj[0], pieces[1]))
            up, down = gathered(up_own), gathered(down_own)
        r0, r1, r23, qkvi, oti, tti, hx, oi = image_forward(
            tick_at[t], info, ni, micro, pieces, w_image, wo_image, gidc, gidr, image_stacks
        )
        image_stacks = (hx, oi)
        r0, r1, r23, qkvt, ott, ttt, hy, o = text_forward(
            tick_at[t], info, nt, micro, pieces, w_text, wo_text, qkvi, (r0, r1, r23), text_stacks
        )
        text_stacks = (hy, o)
        state[t] = [x, qkvi, oti, tti, qkvt, ott, ttt]
        return scattered(r0, r1, r23)

    def feed(t, parts):
        nonlocal ff_stacks
        mid, gp, z, *ff_stacks = ff_forward(
            tick_at[t], info, ni, micro, state[t][0], parts, gain, bias, up, down, ff_stacks
        )
        state[t] += [mid, gp]
        if t + SKEW < ticks:
            relayed[t] = shifted(z, 1)

    for t in range(ticks):
        feed(t, attend(t))
    h2, g, image_result, text_result = ff_stacks

    sums_one = sums_two = jnp.zeros((2, d), F32)
    relayed = {}
    ff_stacks = text_back = image_back = close_stacks = ()
    for k in range(ticks):
        t = ticks - 1 - k
        x, qkvi, oti, tti, qkvt, ott, ttt, mid, gp = state[t]
        back = relayed.get(k - SKEW, nothing)
        dmid, da, sums, *ff_stacks = ff_backward(
            tick_at[t], info, max(t - SKEW, 0), micro, image_cot, text_cot, back, gp, mid, gain,
            up, down, ff_stacks,
        )
        sums_two = sums_two + sums
        pieces = gathered(da)
        if k == ticks - 1:
            dm, du = ff_stacks
            far, y_part = ff_weights((3, 1), micro, h2, dm, du, g, groups)
            near, core_part = ff_weights((0, 2), micro, h2, dm, after(du, far), g, groups)
            across = (y_part.astype(F32) + over_core(far).astype(F32)).astype(BF16)
            near, core_part, across, *pieces = lax.optimization_barrier(
                (near, core_part, across, *pieces)
            )
            a, b, c = near, over_core(core_part), over_y(across)
            ff_sum = (a.astype(F32) + b.astype(F32) + c.astype(F32)).astype(BF16)
        r0, r1, r23, dkv, *text_back = text_backward(
            tick_at[t], info, nt, micro, pieces, w_text, wo_text, qkvi, qkvt, ott, ttt, text_back
        )
        if k == ticks - 1:
            text_w = attention_weights(
                text_stacks[0], text_back[1], text_stacks[1], text_back[0], groups, "text_weights"
            )
            dkv, text_w = lax.optimization_barrier((dkv, text_w))
        r0, r1, r23, *image_back = image_backward(
            tick_at[t], info, ni, micro, pieces, w_image, wo_image, gidc, gidr, qkvi, oti, tti, dkv,
            (r0, r1, r23), image_back,
        )
        parts = scattered(r0, r1, r23)
        if k == ticks - 1:
            image_w = attention_weights(
                image_stacks[0], image_back[1], image_stacks[1], image_back[0], groups, "image_weights"
            )
            dmid = after(dmid, image_w, ff_sum)
        back, sums, *close_stacks = close(
            tick_at[t], info, ni, micro, x, parts, dmid, gain, close_stacks
        )
        sums_one = sums_one + sums
        if k + SKEW < ticks:
            relayed[k] = shifted(back, -1)

    def over_dp(array):
        return lax.psum_scatter(array, "dp", scatter_dimension=0, tiled=True)[0].astype(F32)

    ff_grad = over_dp(ff_sum)
    text_grad = over_dp(text_w)
    image_grad = over_dp(image_w)
    rows, wo_rows = d // groups, width // groups
    gain_grad, bias_grad = over_everyone(jnp.stack((sums_one, sums_two), axis=1))
    return (
        image_result[None],
        text_result[None],
        close_stacks[0][None],
        close_stacks[1][None],
        image_grad[:rows, 2 * width :].reshape(1, rows, 3, width),
        image_grad[rows:, :d][None],
        text_grad[:rows, : 3 * width].reshape(1, rows, 3, width),
        text_grad[rows : rows + wo_rows, :d][None],
        text_grad[:rows, 3 * width :][None],
        image_grad[:rows, : 2 * width].reshape(1, rows, 2, width),
        text_grad[rows + wo_rows :, :d][None],
        ff_grad[:rows][None],
        ff_grad[rows:][None],
        gain_grad[None],
        bias_grad[None],
    )


def solution(mesh):
    return jax.shard_map(
        shards,
        mesh=mesh,
        in_specs=(
            P("dp", "mp", None),
            P("dp", "mp", None),
            P("dp"),
            P("dp", "mp", None),
            P("dp", "mp", None),
            P("section", None, None, "mp"),
            P("section", "mp", None),
            P("section", None, None, "mp"),
            P("section", "mp", None),
            P("section", None, "mp"),
            P("section", None, None, "mp"),
            P("section", "mp", None),
            P("section", None, "mp"),
            P("section", "mp", None),
            P("section", None, None),
            P("section", None, None),
        ),
        out_specs=(
            P("section", "dp", "mp", None),
            P("section", "dp", "mp", None),
            P("section", "dp", "mp", None),
            P("section", "dp", "mp", None),
            P("section", "dp", None, "mp"),
            P("section", ("mp", "dp"), None),
            P("section", "dp", None, "mp"),
            P("section", ("mp", "dp"), None),
            P("section", "dp", "mp"),
            P("section", "dp", None, "mp"),
            P("section", ("mp", "dp"), None),
            P("section", "dp", "mp"),
            P("section", ("mp", "dp"), None),
            P("section", None, ("dp", "mp")),
            P("section", None, ("dp", "mp")),
        ),
        check_vma=False,
    )
```

time: 1180 us -> 883 us (0.75)
  Pallas kernels: 619 us -> 503 us
  waiting for transfers between devices: 341 us -> 236 us
  starting transfers between devices: 104 us -> 63.8 us
  other arithmetic: 32.4 us -> 18.8 us
    pallas_call x50 -> x52, Pallas kernels: 619 us -> 503 us  [the longest x48 450 us: run(): pl.pallas_call(kernel, out_shape=tuple(outs), in_specs=[SMEM_SPEC] * lead...]
    reduce_scatter x3, waiting for transfers between devices: 108 us -> 0.01 us  [over_dp(): lax.psum_scatter(array, 'dp', scatter_dimension=0, tiled=True)[0]]
    ppermute x16 -> x8, waiting for transfers between devices: 62.4 us -> 15.1 us  [shifted(): lax.ppermute(array, 'section', [(i, i + by) for i in range(length) if 0 <...]
    ppermute x51 -> x27, waiting for transfers between devices: 164 us -> 202 us  [over_y(): return lax.ppermute(array, 'mp', [(m, m ^ 2) for m in range(4)])]
    ppermute x51 -> x27, starting transfers between devices: 55.4 us -> 35.3 us  [over_y(): return lax.ppermute(array, 'mp', [(m, m ^ 2) for m in range(4)])]
    ppermute x102 -> x42, starting transfers between devices: 23 us -> 8.4 us  [over_core(): return lax.ppermute(array, 'mp', [(m, m ^ 1) for m in range(4)])]
    unnamed x483 -> x213, local copies, waits for them, and re-layouts: 44.4 us -> 30.3 us
    ppermute x16 -> x8, starting transfers between devices: 25.9 us -> 13.8 us  [shifted(): lax.ppermute(array, 'section', [(i, i + by) for i in range(length) if 0 <...]
  transfers between devices with their start and end apart: 174 -> 84, of which waited for: 31 -> 35; matrix products, arithmetic and copies ran while one was open for 4% -> 3% of each run, Pallas kernels for 46% -> 48%
where the time goes in v2:
time: 883 us; the launch traced here: 879 us
  Pallas kernels  503 us (57%)
  waiting for transfers between devices  236 us (27%)
  starting transfers between devices  63.8 us (7%)
  local copies, waits for them, and re-layouts  41.7 us (5%)
  other arithmetic  18.8 us (2%)
  between operations  15.6 us (2%)
    pallas_call x48, Pallas kernels, run(): pl.pallas_call(kernel, out_shape=tuple(outs), in_specs=[SMEM_SPEC] * lead...  450 us
    ppermute x27, waiting for transfers between devices, over_y(): return lax.ppermute(array, 'mp', [(m, m ^ 2) for m in range(4)])  202 us
    ppermute x27, starting transfers between devices, over_y(): return lax.ppermute(array, 'mp', [(m, m ^ 2) for m in range(4)])  35.3 us
    unnamed x213, local copies, waits for them, and re-layouts  30.3 us
    pallas_call x2, Pallas kernels, ff_weights(): pl.pallas_call(ff_weights_kernel, grid=(2,), out_shape=(shape_of(part, BF...  28.2 us
    pallas_call x2, Pallas kernels, attention_weights(): pl.pallas_call(attention_weights_kernel, grid=(slots - 1,), out_shape=sha...  25 us
  transfers between devices with their start and end apart: 84, of which 35 were waited for; matrix products, arithmetic and copies ran while one was open for 3% of the time, Pallas kernels for 48%

profile of v2, /device:TPU:0, one launch (start us, length us, event | category | flops | bytes accessed | tf_op | source)
XLA Modules:
  0.0 879.0 jit_solution(7963083392536618393)
XLA Ops:
  48.2 13.7 %text_forward.6 = (bf16[344,768]{1,0:T(8,128)(2,1)}, bf16[344,768]{1,0:T(8,128)(2,1)}, bf16[2,344,768]{2,1,0:T(8,128)(2,1)}, bf16[4,800,192]{2,1,0:T(8,128)(2,1)...) custom-call(s32[1]{0:T(128)} %constant.78.clone.1.tick, ...), custom_call_target="tpu_custom_call", output_to_operand_aliasing={{0}: (9, {}), {1}: (10, {}), {2}: (11, {})} | custom-call | flops 4010803200 | bytes 7299072 | tf_op jit(solution)/shard_map/text_forward/pallas_call | solution.py:118
  70.6 13.2 %text_forward.7 = (bf16[344,768]{1,0:T(8,128)(2,1)}, bf16[344,768]{1,0:T(8,128)(2,1)}, bf16[2,344,768]{2,1,0:T(8,128)(2,1)}, bf16[4,800,192]{2,1,0:T(8,128)(2,1)...) custom-call(s32[1]{0:T(128)} %constant.71.clone.1.tick, ...), custom_call_target="tpu_custom_call", output_to_operand_aliasing={{0}: (9, {}), {1}: (10, {}), {2}: (11, {}), {6}: (12, {}), ... | custom-call | flops 4010803200 | bytes 7299072 | tf_op jit(solution)/shard_map/text_forward/pallas_call | solution.py:118
  95.7 11.8 %collective-permute-done.15.c = bf16[344,768]{1,0:T(8,128)(2,1)S(1)} collective-permute-done((bf16[344,768]{1,0:T(8,128)(2,1)S(1)}, bf16[344,768]{1,0:T(8,128)(2,1)S(1)}, u32[]{:S(2)}, u32[]{:S(2)}) %collective-permute-start.15) | collective-permute-done | bytes 528416 | tf_op jit(solution)/shard_map/ppermute | solution.py:970
  109.1 11.3 %ff_forward.6 = (f32[344,768]{1,0:T(8,128)}, bf16[344,3072]{1,0:T(8,128)(2,1)}, bf16[344,768]{1,0:T(8,128)(2,1)}, bf16[1720,768]{1,0:T(8,128)(2,1)}, bf16[1720,3...) custom-call(s32[1]{0:T(128)} %constant.78.clone.1.tick, s32[54]{0:T(128)} %concatenate.12.info, ...), custom_call_target="tpu_custom_call" | custom-call | flops 3246391296 | bytes 17891328 | tf_op jit(solution)/shard_map/ff_forward/pallas_call | solution.py:118
  173.0 13.3 %text_forward.8 = (bf16[344,768]{1,0:T(8,128)(2,1)}, bf16[344,768]{1,0:T(8,128)(2,1)}, bf16[2,344,768]{2,1,0:T(8,128)(2,1)}, bf16[4,800,192]{2,1,0:T(8,128)(2,1)...) custom-call(s32[1]{0:T(128)} %constant.79.clone.1.tick, ...), custom_call_target="tpu_custom_call", output_to_operand_aliasing={{0}: (9, {}), {1}: (10, {}), {2}: (11, {}), {6}: (12, {}), ... | custom-call | flops 4010803200 | bytes 7299072 | tf_op jit(solution)/shard_map/text_forward/pallas_call | solution.py:118
  194.9 13.6 %text_forward.9 = (bf16[344,768]{1,0:T(8,128)(2,1)}, bf16[344,768]{1,0:T(8,128)(2,1)}, bf16[2,344,768]{2,1,0:T(8,128)(2,1)}, bf16[4,800,192]{2,1,0:T(8,128)(2,1)...) custom-call(s32[1]{0:T(128)} %constant.70.clone.1.tick, ...), custom_call_target="tpu_custom_call", output_to_operand_aliasing={{0}: (9, {}), {1}: (10, {}), {2}: (11, {}), {6}: (12, {}), ... | custom-call | flops 4010803200 | bytes 7299072 | tf_op jit(solution)/shard_map/text_forward/pallas_call | solution.py:118
  224.5 11.3 %ff_forward.8 = (f32[344,768]{1,0:T(8,128)}, bf16[344,3072]{1,0:T(8,128)(2,1)}, bf16[344,768]{1,0:T(8,128)(2,1)}, bf16[1720,768]{1,0:T(8,128)(2,1)}, bf16[1720,3...) custom-call(s32[1]{0:T(128)} %constant.79.clone.1.tick, ...), custom_call_target="tpu_custom_call", output_to_operand_aliasing={{3}: (16, {}), {4}: (17, {}), {5}: (18, {}), {6}: (19, {})} | custom-call | flops 3246391296 | bytes 17891328 | tf_op jit(solution)/shard_map/ff_forward/pallas_call | solution.py:118
  238.6 11.3 %ff_forward.9 = (f32[344,768]{1,0:T(8,128)}, bf16[344,3072]{1,0:T(8,128)(2,1)}, bf16[344,768]{1,0:T(8,128)(2,1)}, bf16[1720,768]{1,0:T(8,128)(2,1)}, bf16[1720,3...) custom-call(s32[1]{0:T(128)} %constant.70.clone.1.tick, ...), custom_call_target="tpu_custom_call", output_to_operand_aliasing={{3}: (16, {}), {4}: (17, {}), {5}: (18, {}), {6}: (19, {})} | custom-call | flops 3246391296 | bytes 17891328 | tf_op jit(solution)/shard_map/ff_forward/pallas_call | solution.py:118
  288.3 13.3 %text_forward.10 = (bf16[344,768]{1,0:T(8,128)(2,1)}, bf16[344,768]{1,0:T(8,128)(2,1)}, bf16[2,344,768]{2,1,0:T(8,128)(2,1)}, bf16[4,800,192]{2,1,0:T(8,128)(2,1...) custom-call(s32[1]{0:T(128)} %constant.80.clone.1.tick, ...), custom_call_target="tpu_custom_call", output_to_operand_aliasing={{0}: (9, {}), {1}: (10, {}), {2}: (11, {}), {6}: (12, {}), ... | custom-call | flops 4010803200 | bytes 7299072 | tf_op jit(solution)/shard_map/text_forward/pallas_call | solution.py:118
  310.4 13.6 %text_forward.11 = (bf16[344,768]{1,0:T(8,128)(2,1)}, bf16[344,768]{1,0:T(8,128)(2,1)}, bf16[2,344,768]{2,1,0:T(8,128)(2,1)}, bf16[4,800,192]{2,1,0:T(8,128)(2,1...) custom-call(s32[1]{0:T(128)} %constant.32.clone.1.tick, ...), custom_call_target="tpu_custom_call", output_to_operand_aliasing={{0}: (9, {}), {1}: (10, {}), {2}: (11, {}), {6}: (12, {}), ... | custom-call | flops 4010803200 | bytes 7299072 | tf_op jit(solution)/shard_map/text_forward/pallas_call | solution.py:118
  386.7 11.6 %collective-permute-done.40.p1 = bf16[344,768]{1,0:T(8,128)(2,1)S(1)} collective-permute-done((bf16[344,768]{1,0:T(8,128)(2,1)}, bf16[344,768]{1,0:T(8,128)(2,1)S(1)}, u32[]{:S(2)}, u32[]{:S(2)}) %collective-permute-start.40) | collective-permute-done | bytes 528416 | tf_op jit(solution)/shard_map/ppermute | solution.py:970
  399.4 16.5 %text_backward.6 = (bf16[344,768]{1,0:T(8,128)(2,1)}, bf16[344,768]{1,0:T(8,128)(2,1)}, bf16[2,344,768]{2,1,0:T(8,128)(2,1)}, bf16[2,576,192]{2,1,0:T(8,128)(2,1...) custom-call(s32[1]{0:T(128)} %constant.32.clone.1.tick, s32[54]{0:T(128)} %concatenate.12.info, ...), custom_call_target="tpu_custom_call" | custom-call | flops 7903641600 | bytes 8527872 | tf_op jit(solution)/shard_map/text_backward/pallas_call | solution.py:118
  425.8 16.5 %text_backward.7 = (bf16[344,768]{1,0:T(8,128)(2,1)}, bf16[344,768]{1,0:T(8,128)(2,1)}, bf16[2,344,768]{2,1,0:T(8,128)(2,1)}, bf16[2,576,192]{2,1,0:T(8,128)(2,1...) custom-call(s32[1]{0:T(128)} %constant.80.clone.1.tick, ...), custom_call_target="tpu_custom_call", output_to_operand_aliasing={{4}: (12, {}), {5}: (13, {})} | custom-call | flops 7903641600 | bytes 8527872 | tf_op jit(solution)/shard_map/text_backward/pallas_call | solution.py:118
  524.2 16.8 %text_backward.8 = (bf16[344,768]{1,0:T(8,128)(2,1)}, bf16[344,768]{1,0:T(8,128)(2,1)}, bf16[2,344,768]{2,1,0:T(8,128)(2,1)}, bf16[2,576,192]{2,1,0:T(8,128)(2,1...) custom-call(s32[1]{0:T(128)} %constant.70.clone.1.tick, ...), custom_call_target="tpu_custom_call", output_to_operand_aliasing={{4}: (12, {}), {5}: (13, {})} | custom-call | flops 7903641600 | bytes 8527872 | tf_op jit(solution)/shard_map/text_backward/pallas_call | solution.py:118
  550.6 16.6 %text_backward.9 = (bf16[344,768]{1,0:T(8,128)(2,1)}, bf16[344,768]{1,0:T(8,128)(2,1)}, bf16[2,344,768]{2,1,0:T(8,128)(2,1)}, bf16[2,576,192]{2,1,0:T(8,128)(2,1...) custom-call(s32[1]{0:T(128)} %constant.79.clone.1.tick, ...), custom_call_target="tpu_custom_call", output_to_operand_aliasing={{4}: (12, {}), {5}: (13, {})} | custom-call | flops 7903641600 | bytes 8527872 | tf_op jit(solution)/shard_map/text_backward/pallas_call | solution.py:118
  634.3 14.1 %ff_weights.2 = (bf16[4,384,768]{2,1,0:T(8,128)(2,1)}, bf16[4,384,768]{2,1,0:T(8,128)(2,1)}) custom-call(bf16[1720,768]{1,0:T(8,128)(2,1)} %get-tuple-element.400.h2, bf16[1720,768]{1,0:T(8,128)(2,1)} %get-tuple-element.501.dm, bf16[1720,3072]{1,0:T(8,128)(2,1)} %get-tuple-element.505.du, bf16[1720,3072]{1,0:T(8,128)(2,1)} %get-tuple-element.503.g), custom_call_target="tpu_custom_call" | custom-call | flops 6492782592 | bytes 17399808 | tf_op jit(solution)/shard_map/ff_weights/pallas_call | solution.py:883
  650.7 12.6 %collective-permute-done.68.p1 = bf16[344,768]{1,0:T(8,128)(2,1)S(1)} collective-permute-done((bf16[344,768]{1,0:T(8,128)(2,1)S(1)}, bf16[344,768]{1,0:T(8,128)(2,1)S(1)}, u32[]{:S(2)}, u32[]{:S(2)}) %collective-permute-start.68) | collective-permute-done | bytes 528416 | tf_op jit(solution)/shard_map/ppermute | solution.py:970
  663.2 14.1 %ff_weights.3 = (bf16[4,384,768]{2,1,0:T(8,128)(2,1)}, bf16[4,384,768]{2,1,0:T(8,128)(2,1)}) custom-call(bf16[1720,768]{1,0:T(8,128)(2,1)} %get-tuple-element.400.h2, bf16[1720,768]{1,0:T(8,128)(2,1)} %get-tuple-element.501.dm, bf16[1720,3072]{1,0:T(8,128)(2,1)} %get-tuple-element.505.du, bf16[1720,3072]{1,0:T(8,128)(2,1)} %get-tuple-element.503.g), custom_call_target="tpu_custom_call" | custom-call | flops 6492782592 | bytes 17399808 | tf_op jit(solution)/shard_map/ff_weights/pallas_call | solution.py:883
  678.8 16.5 %text_backward.10 = (bf16[344,768]{1,0:T(8,128)(2,1)}, bf16[344,768]{1,0:T(8,128)(2,1)}, bf16[2,344,768]{2,1,0:T(8,128)(2,1)}, bf16[2,576,192]{2,1,0:T(8,128)(2,...) custom-call(s32[1]{0:T(128)} %constant.71.clone.1.tick, ...), custom_call_target="tpu_custom_call", output_to_operand_aliasing={{4}: (12, {}), {5}: (13, {})} | custom-call | flops 7903641600 | bytes 8527872 | tf_op jit(solution)/shard_map/text_backward/pallas_call | solution.py:118
  696.4 16.5 %text_backward.11 = (bf16[344,768]{1,0:T(8,128)(2,1)}, bf16[344,768]{1,0:T(8,128)(2,1)}, bf16[2,344,768]{2,1,0:T(8,128)(2,1)}, bf16[2,576,192]{2,1,0:T(8,128)(2,...) custom-call(s32[1]{0:T(128)} %constant.78.clone.1.tick, ...), custom_call_target="tpu_custom_call", output_to_operand_aliasing={{4}: (12, {}), {5}: (13, {})} | custom-call | flops 7903641600 | bytes 8527872 | tf_op jit(solution)/shard_map/text_backward/pallas_call | solution.py:118
  712.9 13.2 %text_weights.1 = bf16[4,288,768]{2,1,0:T(8,128)(2,1)} custom-call(bf16[5,800,768]{2,1,0:T(8,128)(2,1)} %get-tuple-element.528.h, bf16[5,800,768]{2,1,0:T(8,128)(2,1)} %get-tuple-element.529.dd, bf16[5,800,384]{2,1,0:T(8,128)(2,1)} %get-tuple-element.530.o, bf16[5,800,768]{2,1,0:T(8,128)(2,1)} %get-tuple-element.531.da), custom_call_target="tpu_custom_call" | custom-call | flops 7077888000 | bytes 21504000 | tf_op jit(solution)/shard_map/text_weights/pallas_call | solution.py:640
  742.1 11.7 %image_weights.1 = bf16[4,240,960]{2,1,0:T(8,128)(2,1)} custom-call(bf16[5,576,768]{2,1,0:T(8,128)(2,1)} %get-tuple-element.550.h, bf16[5,576,960]{2,1,0:T(8,128)(2,1)} %get-tuple-element.551.dd, bf16[5,576,192]{2,1,0:T(8,128)(2,1)} %get-tuple-element.552.o, bf16[5,576,768]{2,1,0:T(8,128)(2,1)} %get-tuple-element.553.da), custom_call_target="tpu_custom_call" | custom-call | flops 5096079360 | bytes 15482880 | tf_op jit(solution)/shard_map/image_weights/pallas_call | solution.py:640
  758.7 48.9 %collective-permute-done.74 = bf16[4,384,768]{2,1,0:T(8,128)(2,1)S(1)} collective-permute-done((bf16[4,384,768]{2,1,0:T(8,128)(2,1)S(1)}, bf16[4,384,768]{2,1,0:T(8,128)(2,1)S(1)}, u32[]{:S(2)}, u32[]{:S(2)}) %collective-permute-start.74) | collective-permute-done | bytes 2359328 | tf_op jit(solution)/shard_map/ppermute | solution.py:970
  818.7 12.0 %collective-permute-done.76.c = bf16[344,768]{1,0:T(8,128)(2,1)S(1)} collective-permute-done((bf16[344,768]{1,0:T(8,128)(2,1)S(1)}, bf16[344,768]{1,0:T(8,128)(2,1)S(1)}, u32[]{:S(2)}, u32[]{:S(2)}) %collective-permute-start.76) | collective-permute-done | bytes 528416 | tf_op jit(solution)/shard_map/ppermute | solution.py:970
  (464 shorter events, 499.3 us)
Async XLA Ops:
  7.2 854.7 %reduce-scatter.6.cloned.1.call-start = ((), (), s32[]{:S(2)}) async-start(), calls=%async_computation.4 | async-start | bytes 2211840 | tf_op jit(solution)/shard_map/reduce_scatter | solution.py:1148
  20.0 42.5 %collective-permute-start.1 = (bf16[344,768]{1,0:T(8,128)(2,1)}, bf16[344,768]{1,0:T(8,128)(2,1)S(1)}, u32[]{:S(2)}, u32[]{:S(2)}) collective-permute-start(bf16[344,768]{1,0:T(8,128)(2,1)} %get-tuple-element.299.p0), channel_id=1, source_target_pairs={{0,1},{1,0},{2,3},{3,2},{4,5},{5,4},{6,7},{7,6},{8,9},{9,8},{10,11... | collective-permute-start | bytes 1585160 | tf_op jit(solution)/shard_map/ppermute | solution.py:974
  35.0 49.4 %collective-permute-start.8 = (bf16[768,768]{1,0:T(8,128)(2,1)S(1)}, bf16[768,768]{1,0:T(8,128)(2,1)S(1)}, u32[]{:S(2)}, u32[]{:S(2)}) collective-permute-start(bf16[768,768]{1,0:T(8,128)(2,1)S(1)} %bitcast.108), channel_id=1, source_target_pairs={{0,2},{1,3},{2,0},{3,1},{4,6},{5,7},{6,4},{7,5},{8,10},{9,11},{10,... | collective-permute-start | bytes 3538952 | tf_op jit(solution)/shard_map/ppermute | solution.py:970
  37.1 53.6 %collective-permute-start.11 = (bf16[768,768]{1,0:T(8,128)(2,1)S(1)}, bf16[768,768]{1,0:T(8,128)(2,1)S(1)}, u32[]{:S(2)}, u32[]{:S(2)}) collective-permute-start(bf16[768,768]{1,0:T(8,128)(2,1)S(1)} %bitcast.122), channel_id=1, source_target_pairs={{0,2},{1,3},{2,0},{3,1},{4,6},{5,7},{6,4},{7,5},{8,10},{9,11},{10,... | collective-permute-start | bytes 3538952 | tf_op jit(solution)/shard_map/ppermute | solution.py:970
  61.9 28.8 %collective-permute-start.14 = (bf16[2,344,768]{2,1,0:T(8,128)(2,1)}, bf16[2,344,768]{2,1,0:T(8,128)(2,1)}, u32[]{:S(2)}, u32[]{:S(2)}) collective-permute-start(bf16[2,344,768]{2,1,0:T(8,128)(2,1)} %get-tuple-element.320), channel_id=1, source_target_pairs={{0,1},{1,0},{2,3},{3,2},{4,5},{5,4},{6,7},{7,6},{8,9},{9,8},{10,11... | collective-permute-start | bytes 3170312 | tf_op jit(solution)/shard_map/ppermute | solution.py:974
  95.3 27.9 %collective-permute-start.7 = (bf16[344,768]{1,0:T(8,128)(2,1)}, bf16[344,768]{1,0:T(8,128)(2,1)S(1)}, u32[]{:S(2)}, u32[]{:S(2)}) collective-permute-start(bf16[344,768]{1,0:T(8,128)(2,1)} %fusion.11), channel_id=1, source_target_pairs={{0,2},{1,3},{2,0},{3,1},{4,6},{5,7},{6,4},{7,5},{8,10},{9,11},{10,... | collective-permute-start | bytes 1585160 | tf_op jit(solution)/shard_map/ppermute | solution.py:970
  155.8 31.0 %collective-permute-start.18 = (bf16[344,768]{1,0:T(8,128)(2,1)}, bf16[344,768]{1,0:T(8,128)(2,1)S(1)}, u32[]{:S(2)}, u32[]{:S(2)}) collective-permute-start(bf16[344,768]{1,0:T(8,128)(2,1)} %get-tuple-element.328.p0), channel_id=1, source_target_pairs={{0,1},{1,0},{2,3},{3,2},{4,5},{5,4},{6,7},{7,6},{8,9},{9,8},{10,11... | collective-permute-start | bytes 1585160 | tf_op jit(solution)/shard_map/ppermute | solution.py:974
  211.7 26.1 %collective-permute-start.25 = (bf16[344,768]{1,0:T(8,128)(2,1)S(1)}, bf16[344,768]{1,0:T(8,128)(2,1)S(1)}, u32[]{:S(2)}, u32[]{:S(2)}) collective-permute-start(bf16[344,768]{1,0:T(8,128)(2,1)S(1)} %fusion.9), channel_id=1, source_target_pairs={{0,2},{1,3},{2,0},{3,1},{4,6},{5,7},{6,4},{7,5},{8,10},{9,11},{10,... | collective-permute-start | bytes 1585160 | tf_op jit(solution)/shard_map/ppermute | solution.py:970
  270.0 32.2 %collective-permute-start.30 = (bf16[344,768]{1,0:T(8,128)(2,1)}, bf16[344,768]{1,0:T(8,128)(2,1)S(1)}, u32[]{:S(2)}, u32[]{:S(2)}) collective-permute-start(bf16[344,768]{1,0:T(8,128)(2,1)} %get-tuple-element.364.p0), channel_id=1, source_target_pairs={{0,1},{1,0},{2,3},{3,2},{4,5},{5,4},{6,7},{7,6},{8,9},{9,8},{10,11... | collective-permute-start | bytes 1585160 | tf_op jit(solution)/shard_map/ppermute | solution.py:974
  327.2 23.3 %collective-permute-start.37 = (bf16[344,768]{1,0:T(8,128)(2,1)S(1)}, bf16[344,768]{1,0:T(8,128)(2,1)S(1)}, u32[]{:S(2)}, u32[]{:S(2)}) collective-permute-start(bf16[344,768]{1,0:T(8,128)(2,1)S(1)} %fusion.7), channel_id=1, source_target_pairs={{0,2},{1,3},{2,0},{3,1},{4,6},{5,7},{6,4},{7,5},{8,10},{9,11},{10,... | collective-permute-start | bytes 1585160 | tf_op jit(solution)/shard_map/ppermute | solution.py:970
  386.2 38.6 %collective-permute-start.41 = (bf16[344,768]{1,0:T(8,128)(2,1)}, bf16[344,768]{1,0:T(8,128)(2,1)S(1)}, u32[]{:S(2)}, u32[]{:S(2)}) collective-permute-start(bf16[344,768]{1,0:T(8,128)(2,1)} %get-tuple-element.407.p0), channel_id=1, source_target_pairs={{0,1},{1,0},{2,3},{3,2},{4,5},{5,4},{6,7},{7,6},{8,9},{9,8},{10,11... | collective-permute-start | bytes 1585160 | tf_op jit(solution)/shard_map/ppermute | solution.py:974
  398.3 26.5 %collective-permute-start.42 = (bf16[344,768]{1,0:T(8,128)(2,1)S(1)}, bf16[344,768]{1,0:T(8,128)(2,1)S(1)}, u32[]{:S(2)}, u32[]{:S(2)}) collective-permute-start(bf16[344,768]{1,0:T(8,128)(2,1)S(1)} %collective-permute-done.40.p1), channel_id=1, source_target_pairs={{0,1},{1,0},{2,3},{3,2},{4,5},{5,4},{6,7},{7,6},{8,9},{9,8},{10,11... | collective-permute-start | bytes 1585160 | tf_op jit(solution)/shard_map/ppermute | solution.py:974
  424.3 26.3 %collective-permute-start.48 = (bf16[2,344,768]{2,1,0:T(8,128)(2,1)}, bf16[2,344,768]{2,1,0:T(8,128)(2,1)S(1)}, u32[]{:S(2)}, u32[]{:S(2)}) collective-permute-start(bf16[2,344,768]{2,1,0:T(8,128)(2,1)} %get-tuple-element.436), channel_id=1, source_target_pairs={{0,1},{1,0},{2,3},{3,2},{4,5},{5,4},{6,7},{7,6},{8,9},{9,8},{10,11... | collective-permute-start | bytes 3170312 | tf_op jit(solution)/shard_map/ppermute | solution.py:974
  512.5 37.1 %collective-permute-start.53 = (bf16[344,768]{1,0:T(8,128)(2,1)}, bf16[344,768]{1,0:T(8,128)(2,1)S(1)}, u32[]{:S(2)}, u32[]{:S(2)}) collective-permute-start(bf16[344,768]{1,0:T(8,128)(2,1)} %get-tuple-element.451.p0), channel_id=1, source_target_pairs={{0,1},{1,0},{2,3},{3,2},{4,5},{5,4},{6,7},{7,6},{8,9},{9,8},{10,11... | collective-permute-start | bytes 1585160 | tf_op jit(solution)/shard_map/ppermute | solution.py:974
  523.2 26.5 %collective-permute-start.54 = (bf16[344,768]{1,0:T(8,128)(2,1)S(1)}, bf16[344,768]{1,0:T(8,128)(2,1)S(1)}, u32[]{:S(2)}, u32[]{:S(2)}) collective-permute-start(bf16[344,768]{1,0:T(8,128)(2,1)S(1)} %collective-permute-done.52.p1), channel_id=1, source_target_pairs={{0,1},{1,0},{2,3},{3,2},{4,5},{5,4},{6,7},{7,6},{8,9},{9,8},{10,11... | collective-permute-start | bytes 1585160 | tf_op jit(solution)/shard_map/ppermute | solution.py:974
  549.1 26.4 %collective-permute-start.60 = (bf16[2,344,768]{2,1,0:T(8,128)(2,1)}, bf16[2,344,768]{2,1,0:T(8,128)(2,1)S(1)}, u32[]{:S(2)}, u32[]{:S(2)}) collective-permute-start(bf16[2,344,768]{2,1,0:T(8,128)(2,1)} %get-tuple-element.484), channel_id=1, source_target_pairs={{0,1},{1,0},{2,3},{3,2},{4,5},{5,4},{6,7},{7,6},{8,9},{9,8},{10,11... | collective-permute-start | bytes 3170312 | tf_op jit(solution)/shard_map/ppermute | solution.py:974
  648.4 47.0 %collective-permute-start.64 = (bf16[4,384,768]{2,1,0:T(8,128)(2,1)}, bf16[4,384,768]{2,1,0:T(8,128)(2,1)S(1)}, u32[]{:S(2)}, u32[]{:S(2)}) collective-permute-start(bf16[4,384,768]{2,1,0:T(8,128)(2,1)} %get-tuple-element.504), channel_id=1, source_target_pairs={{0,1},{1,0},{2,3},{3,2},{4,5},{5,4},{6,7},{7,6},{8,9},{9,8},{10,11... | collective-permute-start | bytes 7077896 | tf_op jit(solution)/shard_map/ppermute | solution.py:974
  649.7 46.6 %collective-permute-start.66 = (bf16[344,768]{1,0:T(8,128)(2,1)S(1)}, bf16[344,768]{1,0:T(8,128)(2,1)}, u32[]{:S(2)}, u32[]{:S(2)}) collective-permute-start(bf16[344,768]{1,0:T(8,128)(2,1)S(1)} %copy-done.74), channel_id=1, source_target_pairs={{0,1},{1,0},{2,3},{3,2},{4,5},{5,4},{6,7},{7,6},{8,9},{9,8},{10,11... | collective-permute-start | bytes 1585160 | tf_op jit(solution)/shard_map/ppermute | solution.py:974
  649.9 27.5 %collective-permute-start.65 = (bf16[344,768]{1,0:T(8,128)(2,1)S(1)}, bf16[344,768]{1,0:T(8,128)(2,1)}, u32[]{:S(2)}, u32[]{:S(2)}) collective-permute-start(bf16[344,768]{1,0:T(8,128)(2,1)S(1)} %copy-done.74), channel_id=1, source_target_pairs={{0,2},{1,3},{2,0},{3,1},{4,6},{5,7},{6,4},{7,5},{8,10},{9,11},{10,... | collective-permute-start | bytes 1585160 | tf_op jit(solution)/shard_map/ppermute | solution.py:970
  650.6 27.2 %collective-permute-start.69 = (bf16[344,768]{1,0:T(8,128)(2,1)S(1)}, bf16[344,768]{1,0:T(8,128)(2,1)S(1)}, u32[]{:S(2)}, u32[]{:S(2)}) collective-permute-start(bf16[344,768]{1,0:T(8,128)(2,1)S(1)} %copy-done.75), channel_id=1, source_target_pairs={{0,1},{1,0},{2,3},{3,2},{4,5},{5,4},{6,7},{7,6},{8,9},{9,8},{10,11... | collective-permute-start | bytes 1585160 | tf_op jit(solution)/shard_map/ppermute | solution.py:974
  726.1 139.8 %reduce-scatter.4.cloned.1.call-start = ((), (), s32[]{:S(2)}) async-start(), calls=%async_computation.3 | async-start | bytes 2457600 | tf_op jit(solution)/shard_map/reduce_scatter | solution.py:1148
  753.9 116.2 %reduce-scatter.8.cloned.1.call-start = ((), (), s32[]{:S(2)}) async-start(), calls=%async_computation.5 | async-start | bytes 2949120 | tf_op jit(solution)/shard_map/reduce_scatter | solution.py:1148
  754.2 53.5 %collective-permute-start.74 = (bf16[4,384,768]{2,1,0:T(8,128)(2,1)S(1)}, bf16[4,384,768]{2,1,0:T(8,128)(2,1)S(1)}, u32[]{:S(2)}, u32[]{:S(2)}) collective-permute-start(bf16[4,384,768]{2,1,0:T(8,128)(2,1)S(1)} %add_convert_fusion.1), channel_id=1, source_target_pairs={{0,2},{1,3},{2,0},{3,1},{4,6},{5,7},{6,4},{7,5},{8,10},{9,11},{10,... | collective-permute-start | bytes 7077896 | tf_op jit(solution)/shard_map/ppermute | solution.py:970
  817.4 23.9 %collective-permute-start.72 = (bf16[344,768]{1,0:T(8,128)(2,1)S(1)}, bf16[344,768]{1,0:T(8,128)(2,1)S(1)}, u32[]{:S(2)}, u32[]{:S(2)}) collective-permute-start(bf16[344,768]{1,0:T(8,128)(2,1)S(1)} %fusion.1), channel_id=1, source_target_pairs={{0,2},{1,3},{2,0},{3,1},{4,6},{5,7},{6,4},{7,5},{8,10},{9,11},{10,... | collective-permute-start | bytes 1585160 | tf_op jit(solution)/shard_map/ppermute | solution.py:970
  (165 other events, 1349.3 us)
Sparse Core Ops, SparseCore 0:
  726.2 38.4 reduce-scatter.5
  767.2 40.5 reduce-scatter.3
  811.9 48.3 reduce-scatter.7

commit v3 on v2

--- a/solution.py
+++ b/solution.py
@@ -22,7 +22,8 @@
 VMEM_MIB = 56
 SKEW = 2
 SELF_BLOCK = 256
-CROSS_BLOCK = 1024
+CROSS_BLOCK = 512
+CROSS_BACK = 512
 
 F32 = jnp.float32
 BF16 = jnp.bfloat16
@@ -130,22 +131,23 @@
 
 def entry_kernel(source, tick, info, image, text, got, gain, bias, x, h, own, got_v, norm, xv, hv, sems):
     copies = Copies(sems)
-    ni = image.shape[1]
+    n, ni = got_v.shape[0], image.shape[1]
+    both = [copies.start(gain, norm.at[0]), copies.start(bias, norm.at[1])]
+    spans = (slice(0, ni), slice(ni, n))
     loads = [
-        copies.start(image.at[source], own.at[0:ni]),
-        copies.start(text.at[source], own.at[ni:]),
-        copies.start(got, got_v),
-        copies.start(gain, norm.at[0]),
-        copies.start(bias, norm.at[1]),
+        (copies.start(rows.at[source], own.at[span]), copies.start(got.at[span], got_v.at[span]))
+        for rows, span in zip((image, text), spans)
     ]
-    copies.wait(*loads)
+    copies.wait(*both)
     first = info[AT_SECTION] == 0
-    values = jnp.where(first, own[...].astype(F32), got_v[...].astype(F32))
-    xv[...] = values.astype(BF16)
-    unit, _ = normalized(values)
-    hv[...] = (unit * norm[0, 0:1, :] + norm[1, 0:1, :]).astype(BF16)
-    copies.start(hv, h)
-    copies.start(xv, x)
+    for span, load in zip(spans, loads):
+        copies.wait(*load)
+        values = jnp.where(first, own[span, :].astype(F32), got_v[span, :].astype(F32))
+        xv[span, :] = values.astype(BF16)
+        unit, _ = normalized(values)
+        hv[span, :] = (unit * norm[0, 0:1, :] + norm[1, 0:1, :]).astype(BF16)
+        copies.start(hv.at[span], h.at[span])
+        copies.start(xv.at[span], x.at[span])
     copies.finish()
 
 
@@ -160,16 +162,16 @@
         (shape_of((n, d), BF16),) * 2,
         [pltpu.VMEM((n, d), BF16), pltpu.VMEM((n, d), BF16), pltpu.VMEM((2, 2, d), F32)]
         + [pltpu.VMEM((n, d), BF16)] * 2,
-        7,
+        10,
     )
 
 
 def image_forward_kernel(
     tick, info, p0, p1, p2, p3, w, wo, gidc, gidr, *refs
 ):
-    refs = refs[-(8 + 12) :]
+    refs = refs[-(8 + 11) :]
     r0, r1, r23, qkv, ot, tt, hx, o = refs[:8]
-    hx_v, w_v, wo_v, gidc_v, gidr_v, qkv_v, ot_v, tt_v, o_v, part, v_tall, sems = refs[8:]
+    hx_v, w_v, wo_v, gidc_v, gidr_v, qkv_v, ot_v, tt_v, o_v, part, sems = refs[8:]
     copies = Copies(sems)
     rows, d = hx_v.shape
     shard = rows // 4
@@ -190,20 +192,28 @@
     copies.start(hx_v, hx.at[slot])
     copies.start(qkv_v, qkv)
     copies.wait(*more)
-    for b in range(2):
-        span = slice(b * band, (b + 1) * band)
-        bias = jnp.where(gidc_v[span, :] == gidr_v[0:1, span], F32(0.0), F32(MASKED_SCORE))
-        v_tall[...] = qkv_v[4, span, :].astype(F32).T.astype(BF16)
-        for head in range(heads):
-            query = qkv_v[2, span, :] * head_mask(head, width, SCALE)
-            scores = dot_nt(qkv_v[3, span, :], query) + bias
-            largest = jnp.max(scores, axis=0, keepdims=True)
-            weights = jnp.exp(scores - largest)
-            total = jnp.sum(weights, axis=0, keepdims=True)
-            tt_v[b * heads + head] = largest + jnp.log(total)
-            at = head * HEAD_DIM
-            mixed = dot(v_tall[at : at + HEAD_DIM, :], weights.astype(BF16))
-            ot_v[b, at : at + HEAD_DIM, :] = mixed * (1.0 / total)
+    spans = [slice(b * band, (b + 1) * band) for b in range(2)]
+    allowed = [gidc_v[span, :] == gidr_v[0:1, span] for span in spans]
+    bias = [jnp.where(mask, F32(0.0), F32(MASKED_SCORE)) for mask in allowed]
+    v_tall = [qkv_v[4, span, :].astype(F32).T.astype(BF16) for span in spans]
+    items = [(b, head) for b in range(2) for head in range(heads)]
+
+    def score(b, head):
+        query = qkv_v[2, spans[b], :] * head_mask(head, width, SCALE)
+        return dot_nt(qkv_v[3, spans[b], :], query) + bias[b]
+
+    scores = score(*items[0])
+    for index, (b, head) in enumerate(items):
+        later = score(*items[index + 1]) if index + 1 < len(items) else None
+        largest = jnp.max(scores, axis=0, keepdims=True)
+        weights = jnp.exp(scores - largest)
+        total = jnp.sum(weights, axis=0, keepdims=True)
+        tt_v[b * heads + head] = largest + jnp.log(total)
+        own = slice(head * HEAD_DIM, (head + 1) * HEAD_DIM)
+        mixed = dot(v_tall[b][own, :], weights.astype(BF16))
+        ot_v[b, own, :] = mixed * (1.0 / total)
+        scores = later
+    for b, span in enumerate(spans):
         o_v[span, :] = ot_v[b].T.astype(BF16)
     copies.start(ot_v, ot)
     copies.start(tt_v, tt)
@@ -251,7 +261,6 @@
             pltpu.VMEM((2 * heads, 1, band), F32),
             pltpu.VMEM((rows, width), BF16),
             pltpu.VMEM((rows, d), BF16),
-            pltpu.VMEM((width, band), BF16),
         ],
         18,
         ((8, 6), (9, 7)) if stacks else (),
@@ -404,26 +413,32 @@
     copies.start(hy_v, hy.at[slot])
     copies.start(qkv_v, qkv)
     copies.wait(*more)
-    for kind in range(2):
-        values = qkv_v[2] if kind == 0 else kv_v[1]
-        v_tall = values.astype(F32).T.astype(BF16)
-        for start, size in query_blocks(rows, CROSS_BLOCK if kind else SELF_BLOCK):
-            seen = start + size if kind == 0 else patches
-            for head in range(heads):
-                at = head * HEAD_DIM
-                mask = head_mask(head, width, SCALE)
-                query = qkv_v[3 if kind else 0, start : start + size, :] * mask
-                keys = kv_v[0] if kind else qkv_v[1, 0:seen, :]
-                scores = dot_nt(keys, query)
-                if kind == 0:
-                    scores = causal(scores, start, last_key)
-                largest = jnp.max(scores, axis=0, keepdims=True)
-                weights = jnp.exp(scores - largest)
-                total = jnp.sum(weights, axis=0, keepdims=True)
-                tt_v[kind * heads + head, :, start : start + size] = largest + jnp.log(total)
-                mixed = dot(v_tall[at : at + HEAD_DIM, 0:seen], weights.astype(BF16))
-                out_at = kind * width + at
-                ot_v[out_at : out_at + HEAD_DIM, start : start + size] = mixed * (1.0 / total)
+    v_tall = [values.astype(F32).T.astype(BF16) for values in (qkv_v[2], kv_v[1])]
+    items = [
+        (kind, head, start, size)
+        for kind in range(2)
+        for start, size in query_blocks(rows, CROSS_BLOCK if kind else SELF_BLOCK)
+        for head in range(heads)
+    ]
+
+    def score(kind, head, start, size):
+        query = qkv_v[3 if kind else 0, start : start + size, :] * head_mask(head, width, SCALE)
+        keys = kv_v[0] if kind else qkv_v[1, 0 : start + size, :]
+        scores = dot_nt(keys, query)
+        return scores if kind else causal(scores, start, last_key)
+
+    scores = score(*items[0])
+    for index, (kind, head, start, size) in enumerate(items):
+        later = score(*items[index + 1]) if index + 1 < len(items) else None
+        at = head * HEAD_DIM
+        largest = jnp.max(scores, axis=0, keepdims=True)
+        weights = jnp.exp(scores - largest)
+        total = jnp.sum(weights, axis=0, keepdims=True)
+        tt_v[kind * heads + head, :, start : start + size] = largest + jnp.log(total)
+        mixed = dot(v_tall[kind][at : at + HEAD_DIM, 0 : weights.shape[0]], weights.astype(BF16))
+        out_at = kind * width + at
+        ot_v[out_at : out_at + HEAD_DIM, start : start + size] = mixed * (1.0 / total)
+        scores = later
     copies.start(ot_v, ot)
     copies.start(tt_v, tt)
     o_v[...] = ot_v[...].T.astype(BF16)
@@ -513,7 +528,7 @@
         k_tall[:, 0:span] = whole_keys.astype(F32).T.astype(BF16)
         dk_sum[...] = jnp.zeros_like(dk_sum)
         dv_sum[...] = jnp.zeros_like(dv_sum)
-        for start, size in query_blocks(rows, CROSS_BLOCK if kind else SELF_BLOCK):
+        for start, size in query_blocks(rows, CROSS_BACK if kind else SELF_BLOCK):
             seen = start + size if kind == 0 else patches
             block = slice(start, start + size)
             keys = kv_v[0] if kind else qkv_v[1, 0:seen, :]
@@ -902,40 +917,52 @@
     back, sums, image_grad, text_grad = refs[:4]
     x_v, abc, dmid_v, norm, total_v, back_v, sums_v, sems = refs[4:]
     copies = Copies(sems)
+    n = x_v.shape[0]
     slot = info[AT_STACK + tick[0]]
+    valid = info[AT_VALID + tick[0]]
+    ready = copies.start(gain, norm)
+    spans = (slice(0, ni), slice(ni, n))
     loads = [
-        copies.start(s, t)
-        for s, t in (
-            (a, abc.at[0]),
-            (b.at[0], abc.at[1]),
-            (c, abc.at[2]),
-            (x, x_v),
-            (gain, norm),
-            (dmid, dmid_v),
-        )
+        [
+            copies.start(source.at[span], target.at[span])
+            for source, target in (
+                (a, abc.at[0]),
+                (b.at[0], abc.at[1]),
+                (c, abc.at[2]),
+                (x, x_v),
+                (dmid, dmid_v),
+            )
+        ]
+        for span in spans
     ]
-    copies.wait(*loads)
-    grad = abc[0].astype(F32) + abc[1].astype(F32) + abc[2].astype(F32)
-    pulled, gain_sum, bias_sum = norm_pull(grad, x_v[...].astype(F32), norm[0:1, :])
-    total = dmid_v[...] + pulled
-    total_v[...] = total
-    back_v[...] = total.astype(BF16)
-    valid = info[AT_VALID + tick[0]]
-    sums_v[0:1, :] = gain_sum * valid.astype(F32)
-    sums_v[1:2, :] = bias_sum * valid.astype(F32)
-    copies.start(back_v, back)
+    copies.wait(ready)
+    gain_total = bias_total = None
+    for index, (span, load) in enumerate(zip(spans, loads)):
+        copies.wait(*load)
+        grad = abc[0, span, :].astype(F32) + abc[1, span, :].astype(F32) + abc[2, span, :].astype(F32)
+        pulled, gain_sum, bias_sum = norm_pull(grad, x_v[span, :].astype(F32), norm[0:1, :])
+        total = dmid_v[span, :] + pulled
+        total_v[span, :] = total
+        back_v[span, :] = total.astype(BF16)
+        copies.start(back_v.at[span], back.at[span])
+        out = (image_grad, text_grad)[index]
+        copy = pltpu.make_async_copy(total_v.at[span], out.at[slot], sems.at[16 + index])
+
+        @pl.when(valid > 0)
+        def _():
+            copy.start()
+
+        gain_total = gain_sum if index == 0 else gain_total + gain_sum
+        bias_total = bias_sum if index == 0 else bias_total + bias_sum
+    sums_v[0:1, :] = gain_total * valid.astype(F32)
+    sums_v[1:2, :] = bias_total * valid.astype(F32)
     copies.start(sums_v, sums)
-
-    @pl.when(valid > 0)
-    def _():
-        image_copy = pltpu.make_async_copy(total_v.at[0:ni], image_grad.at[slot], sems.at[0])
-        text_copy = pltpu.make_async_copy(total_v.at[ni:], text_grad.at[slot], sems.at[1])
-        image_copy.start()
-        text_copy.start()
-        image_copy.wait()
-        text_copy.wait()
-
     copies.finish()
+    for index, (span, out) in enumerate(zip(spans, (image_grad, text_grad))):
+
+        @pl.when(valid > 0)
+        def _():
+            pltpu.make_async_copy(total_v.at[span], out.at[slot], sems.at[16 + index]).wait()
 
 
 def close(tick, info, ni, micro, x, parts, dmid, gain, stacks):
@@ -961,7 +988,7 @@
             pltpu.VMEM((n, d), BF16),
             pltpu.VMEM((2, d), F32),
         ],
-        8,
+        18,
         ((6, 2), (7, 3)) if stacks else (),
     )
 
@@ -979,10 +1006,9 @@
     return (own, across, over_core(own), over_core(across))
 
 
-def scattered(r0, r1, r23):
+def for_y(r1, r23):
     other = over_core(r23)
-    across = (r1.astype(F32) + other[1].astype(F32)).astype(BF16)
-    return (r0, other, over_y(across))
+    return other, (r1.astype(F32) + other[1].astype(F32)).astype(BF16)
 
 
 def shifted(array, by):
@@ -1005,8 +1031,8 @@
     return lax.dynamic_slice_in_dim(sums, mine * own, own, axis=2)
 
 
-def after(value, *earlier):
-    return lax.optimization_barrier((value, *earlier))[0]
+def hold(values, *earlier):
+    return lax.optimization_barrier((tuple(values), *earlier))[0]
 
 
 def shards(
@@ -1063,25 +1089,35 @@
     image_stacks = text_stacks = ff_stacks = ()
     state = {}
     relayed = {}
+    ahead = {}
 
     def attend(t):
         nonlocal image_stacks, text_stacks, up, down
         got = relayed.get(t - SKEW, nothing)
+        if t >= SKEW and t % SKEW == 0:
+            got = hold((got,), ahead["out"])[0]
         x, h = entry(tick_at[t], info, min(t, micro - 1), image, text, got, gain, bias)
         pieces = gathered(h)
         if up is None:
             up_own, down_own, _ = lax.optimization_barrier((up_proj[0], down_proj[0], pieces[1]))
             up, down = gathered(up_own), gathered(down_own)
+        second = t % SKEW > 0
+        if second:
+            pieces = hold(pieces, ahead["own"])
         r0, r1, r23, qkvi, oti, tti, hx, oi = image_forward(
             tick_at[t], info, ni, micro, pieces, w_image, wo_image, gidc, gidr, image_stacks
         )
         image_stacks = (hx, oi)
+        if second and t > SKEW:
+            r0, r1, r23 = hold((r0, r1, r23), ahead["across"])
         r0, r1, r23, qkvt, ott, ttt, hy, o = text_forward(
             tick_at[t], info, nt, micro, pieces, w_text, wo_text, qkvi, (r0, r1, r23), text_stacks
         )
         text_stacks = (hy, o)
         state[t] = [x, qkvi, oti, tti, qkvt, ott, ttt]
-        return scattered(r0, r1, r23)
+        other, across = for_y(r1, r23)
+        ahead.update(own=r0, across=across)
+        return (r0, other, over_y(across))
 
     def feed(t, parts):
         nonlocal ff_stacks
@@ -1089,60 +1125,116 @@
             tick_at[t], info, ni, micro, state[t][0], parts, gain, bias, up, down, ff_stacks
         )
         state[t] += [mid, gp]
+        ahead["out"] = z
         if t + SKEW < ticks:
             relayed[t] = shifted(z, 1)
 
-    for t in range(ticks):
-        feed(t, attend(t))
+    for t in range(0, ticks, SKEW):
+        sums = [attend(t + i) for i in range(SKEW)]
+        for i in range(SKEW):
+            feed(t + i, sums[i])
     h2, g, image_result, text_result = ff_stacks
 
     sums_one = sums_two = jnp.zeros((2, d), F32)
     relayed = {}
     ff_stacks = text_back = image_back = close_stacks = ()
-    for k in range(ticks):
+    ahead = {}
+
+    def descend(k):
+        nonlocal ff_stacks, sums_two
         t = ticks - 1 - k
-        x, qkvi, oti, tti, qkvt, ott, ttt, mid, gp = state[t]
+        mid, gp = state[t][7:9]
         back = relayed.get(k - SKEW, nothing)
+        if k >= SKEW and k % SKEW == 0:
+            back = hold((back,), ahead["out"])[0]
         dmid, da, sums, *ff_stacks = ff_backward(
             tick_at[t], info, max(t - SKEW, 0), micro, image_cot, text_cot, back, gp, mid, gain,
             up, down, ff_stacks,
         )
         sums_two = sums_two + sums
-        pieces = gathered(da)
-        if k == ticks - 1:
-            dm, du = ff_stacks
-            far, y_part = ff_weights((3, 1), micro, h2, dm, du, g, groups)
-            near, core_part = ff_weights((0, 2), micro, h2, dm, after(du, far), g, groups)
-            across = (y_part.astype(F32) + over_core(far).astype(F32)).astype(BF16)
-            near, core_part, across, *pieces = lax.optimization_barrier(
-                (near, core_part, across, *pieces)
-            )
-            a, b, c = near, over_core(core_part), over_y(across)
-            ff_sum = (a.astype(F32) + b.astype(F32) + c.astype(F32)).astype(BF16)
+        return dmid, gathered(da)
+
+    def text_part(k, pieces):
+        nonlocal text_back
+        t = ticks - 1 - k
+        qkvi, _, _, qkvt, ott, ttt = state[t][1:7]
         r0, r1, r23, dkv, *text_back = text_backward(
             tick_at[t], info, nt, micro, pieces, w_text, wo_text, qkvi, qkvt, ott, ttt, text_back
         )
-        if k == ticks - 1:
-            text_w = attention_weights(
-                text_stacks[0], text_back[1], text_stacks[1], text_back[0], groups, "text_weights"
-            )
-            dkv, text_w = lax.optimization_barrier((dkv, text_w))
+        return (r0, r1, r23), dkv
+
+    def image_part(k, pieces, parts, dkv):
+        nonlocal image_back
+        t = ticks - 1 - k
+        qkvi, oti, tti = state[t][1:4]
         r0, r1, r23, *image_back = image_backward(
             tick_at[t], info, ni, micro, pieces, w_image, wo_image, gidc, gidr, qkvi, oti, tti, dkv,
-            (r0, r1, r23), image_back,
+            parts, image_back,
         )
-        parts = scattered(r0, r1, r23)
-        if k == ticks - 1:
-            image_w = attention_weights(
-                image_stacks[0], image_back[1], image_stacks[1], image_back[0], groups, "image_weights"
-            )
-            dmid = after(dmid, image_w, ff_sum)
+        other, across = for_y(r1, r23)
+        return r0, other, across
+
+    def finish(k, parts, dmid):
+        nonlocal close_stacks, sums_one
+        t = ticks - 1 - k
         back, sums, *close_stacks = close(
-            tick_at[t], info, ni, micro, x, parts, dmid, gain, close_stacks
+            tick_at[t], info, ni, micro, state[t][0], parts, dmid, gain, close_stacks
         )
         sums_one = sums_one + sums
+        ahead["out"] = back
         if k + SKEW < ticks:
             relayed[k] = shifted(back, -1)
+
+    final = ticks - SKEW
+    fed = {}
+    for k in range(final):
+        second = k % SKEW > 0
+        if not second:
+            fed = {k + i: descend(k + i) for i in range(SKEW)}
+        dmid, pieces = fed[k]
+        if second:
+            pieces = hold(pieces, ahead["own"])
+        parts, dkv = text_part(k, pieces)
+        if second:
+            parts = hold(parts, ahead["across"])
+        r0, other, across = image_part(k, pieces, parts, dkv)
+        ahead.update(own=r0, across=across)
+        fed[k] = (k, (r0, other, over_y(across)), dmid)
+        if k % SKEW == SKEW - 1:
+            for i in range(k - SKEW + 1, k + 1):
+                finish(*fed[i])
+
+    one, two = final, final + 1
+    (dmid_one, pieces_one), (dmid_two, pieces_two) = descend(one), descend(two)
+    parts_one, dkv_one = text_part(one, pieces_one)
+    pieces_two = hold(pieces_two, parts_one[0])
+    parts_two, dkv_two = text_part(two, pieces_two)
+    text_w = attention_weights(
+        text_stacks[0], text_back[1], text_stacks[1], text_back[0], groups, "text_weights"
+    )
+    dm, du = hold(ff_stacks, text_w)
+    far, y_part = ff_weights((3, 1), micro, h2, dm, du, g, groups)
+    parts_one = hold(parts_one, far)
+    r0_one, other_one, across_one = image_part(one, pieces_one, parts_one, dkv_one)
+    ff_across = (y_part.astype(F32) + over_core(far).astype(F32)).astype(BF16)
+    parts_two = hold(parts_two, r0_one, ff_across)
+    r0_two, other_two, across_two = image_part(two, pieces_two, parts_two, dkv_two)
+    quarter = ff_across.shape[1] // 4
+    crossed = [over_y(ff_across[:, i * quarter : (i + 1) * quarter]) for i in range(4)]
+    image_stacks = hold((*image_stacks, *image_back), crossed[0], across_one)
+    image_w = attention_weights(
+        image_stacks[0], image_stacks[3], image_stacks[1], image_stacks[2], groups, "image_weights"
+    )
+    du = hold((du,), image_w, crossed[1], across_two)[0]
+    near, core_part = ff_weights((0, 2), micro, h2, dm, du, g, groups)
+    core_part = hold((core_part,), crossed[2])[0]
+    dmid_one = hold((dmid_one,), near)[0]
+    finish(one, (r0_one, other_one, over_y(across_one)), dmid_one)
+    dmid_two = hold((dmid_two,), crossed[3])[0]
+    finish(two, (r0_two, other_two, over_y(across_two)), dmid_two)
+    ff_sum = (
+        near.astype(F32) + over_core(core_part).astype(F32) + jnp.concatenate(crossed, axis=1).astype(F32)
+    ).astype(BF16)
 
     def over_dp(array):
         return lax.psum_scatter(array, "dp", scatter_dimension=0, tiled=True)[0].astype(F32)

time: 883 us -> 847 us (0.959)
  waiting for transfers between devices: 236 us -> 204 us
  Pallas kernels: 503 us -> 488 us
    ppermute x27 -> x30, waiting for transfers between devices: 202 us -> 176 us  [over_y(): return lax.ppermute(array, 'mp', [(m, m ^ 2) for m in range(4)])]
    pallas_call x48, Pallas kernels: 450 us -> 436 us  [run(): pl.pallas_call(kernel, out_shape=tuple(outs), in_specs=[SMEM_SPEC] * lead...]
    ppermute x27 -> x30, starting transfers between devices: 35.3 us -> 33.8 us  [over_y(): return lax.ppermute(array, 'mp', [(m, m ^ 2) for m in range(4)])]
  transfers between devices with their start and end apart: 84 -> 87, of which waited for: 35 -> 37; matrix products, arithmetic and copies ran while one was open for 3% -> 4% of each run, Pallas kernels for 48% -> 44%
where the time goes in v3:
time: 847 us; the launch traced here: 843 us
  Pallas kernels  488 us (58%)
  waiting for transfers between devices  204 us (24%)
  starting transfers between devices  65.2 us (8%)
  local copies, waits for them, and re-layouts  44.3 us (5%)
  other arithmetic  24.7 us (3%)
  between operations  15.8 us (2%)
    pallas_call x48, Pallas kernels, run(): pl.pallas_call(kernel, out_shape=tuple(outs), in_specs=[SMEM_SPEC] * lead...  436 us
    ppermute x30, waiting for transfers between devices, over_y(): return lax.ppermute(array, 'mp', [(m, m ^ 2) for m in range(4)])  176 us
    ppermute x30, starting transfers between devices, over_y(): return lax.ppermute(array, 'mp', [(m, m ^ 2) for m in range(4)])  33.8 us
    unnamed x213, local copies, waits for them, and re-layouts  31.8 us
    pallas_call x2, Pallas kernels, ff_weights(): pl.pallas_call(ff_weights_kernel, grid=(2,), out_shape=(shape_of(part, BF...  27.9 us
    pallas_call x2, Pallas kernels, attention_weights(): pl.pallas_call(attention_weights_kernel, grid=(slots - 1,), out_shape=sha...  24.6 us
    ppermute x8, starting transfers between devices, shifted(): lax.ppermute(array, 'section', [(i, i + by) for i in range(length) if 0 <...  17.2 us
  transfers between devices with their start and end apart: 87, of which 37 were waited for; matrix products, arithmetic and copies ran while one was open for 4% of the time, Pallas kernels for 44%

profile of v3, /device:TPU:0, one launch (start us, length us, event | category | flops | bytes accessed | tf_op | source)
XLA Modules:
  0.0 842.5 jit_solution(1640515128064662724)
XLA Ops:
  47.5 11.6 %text_forward.6 = (bf16[344,768]{1,0:T(8,128)(2,1)}, bf16[344,768]{1,0:T(8,128)(2,1)}, bf16[2,344,768]{2,1,0:T(8,128)(2,1)}, bf16[4,800,192]{2,1,0:T(8,128)(2,1)...) custom-call(s32[1]{0:T(128)} %constant.73.clone.1.tick, ...), custom_call_target="tpu_custom_call", output_to_operand_aliasing={{0}: (9, {}), {1}: (10, {}), {2}: (11, {})} | custom-call | flops 4010803200 | bytes 7299072 | tf_op jit(solution)/shard_map/text_forward/pallas_call | solution.py:119
  67.9 11.6 %text_forward.7 = (bf16[344,768]{1,0:T(8,128)(2,1)}, bf16[344,768]{1,0:T(8,128)(2,1)}, bf16[2,344,768]{2,1,0:T(8,128)(2,1)}, bf16[4,800,192]{2,1,0:T(8,128)(2,1)...) custom-call(s32[1]{0:T(128)} %constant.71.clone.1.tick, ...), custom_call_target="tpu_custom_call", output_to_operand_aliasing={{0}: (9, {}), {1}: (10, {}), {2}: (11, {}), {6}: (12, {}), ... | custom-call | flops 4010803200 | bytes 7299072 | tf_op jit(solution)/shard_map/text_forward/pallas_call | solution.py:119
  95.4 11.8 %collective-permute-done.15.c = bf16[344,768]{1,0:T(8,128)(2,1)S(1)} collective-permute-done((bf16[344,768]{1,0:T(8,128)(2,1)S(1)}, bf16[344,768]{1,0:T(8,128)(2,1)S(1)}, u32[]{:S(2)}, u32[]{:S(2)}) %collective-permute-start.15) | collective-permute-done | bytes 528416 | tf_op jit(solution)/shard_map/ppermute | solution.py:997
  109.0 11.5 %ff_forward.6 = (f32[344,768]{1,0:T(8,128)}, bf16[344,3072]{1,0:T(8,128)(2,1)}, bf16[344,768]{1,0:T(8,128)(2,1)}, bf16[1720,768]{1,0:T(8,128)(2,1)}, bf16[1720,3...) custom-call(s32[1]{0:T(128)} %constant.73.clone.1.tick, s32[54]{0:T(128)} %concatenate.15.info, ...), custom_call_target="tpu_custom_call" | custom-call | flops 3246391296 | bytes 17891328 | tf_op jit(solution)/shard_map/ff_forward/pallas_call | solution.py:119
  124.2 11.3 %ff_forward.7 = (f32[344,768]{1,0:T(8,128)}, bf16[344,3072]{1,0:T(8,128)(2,1)}, bf16[344,768]{1,0:T(8,128)(2,1)}, bf16[1720,768]{1,0:T(8,128)(2,1)}, bf16[1720,3...) custom-call(s32[1]{0:T(128)} %constant.71.clone.1.tick, ...), custom_call_target="tpu_custom_call", output_to_operand_aliasing={{3}: (16, {}), {4}: (17, {}), {5}: (18, {}), {6}: (19, {})} | custom-call | flops 3246391296 | bytes 17891328 | tf_op jit(solution)/shard_map/ff_forward/pallas_call | solution.py:119
  165.2 11.8 %text_forward.8 = (bf16[344,768]{1,0:T(8,128)(2,1)}, bf16[344,768]{1,0:T(8,128)(2,1)}, bf16[2,344,768]{2,1,0:T(8,128)(2,1)}, bf16[4,800,192]{2,1,0:T(8,128)(2,1)...) custom-call(s32[1]{0:T(128)} %constant.79.clone.1.tick, ...), custom_call_target="tpu_custom_call", output_to_operand_aliasing={{0}: (9, {}), {1}: (10, {}), {2}: (11, {}), {6}: (12, {}), ... | custom-call | flops 4010803200 | bytes 7299072 | tf_op jit(solution)/shard_map/text_forward/pallas_call | solution.py:119
  189.5 11.6 %text_forward.9 = (bf16[344,768]{1,0:T(8,128)(2,1)}, bf16[344,768]{1,0:T(8,128)(2,1)}, bf16[2,344,768]{2,1,0:T(8,128)(2,1)}, bf16[4,800,192]{2,1,0:T(8,128)(2,1)...) custom-call(s32[1]{0:T(128)} %constant.70.clone.1.tick, ...), custom_call_target="tpu_custom_call", output_to_operand_aliasing={{0}: (9, {}), {1}: (10, {}), {2}: (11, {}), {6}: (12, {}), ... | custom-call | flops 4010803200 | bytes 7299072 | tf_op jit(solution)/shard_map/text_forward/pallas_call | solution.py:119
  217.0 11.5 %ff_forward.8 = (f32[344,768]{1,0:T(8,128)}, bf16[344,3072]{1,0:T(8,128)(2,1)}, bf16[344,768]{1,0:T(8,128)(2,1)}, bf16[1720,768]{1,0:T(8,128)(2,1)}, bf16[1720,3...) custom-call(s32[1]{0:T(128)} %constant.79.clone.1.tick, ...), custom_call_target="tpu_custom_call", output_to_operand_aliasing={{3}: (16, {}), {4}: (17, {}), {5}: (18, {}), {6}: (19, {})} | custom-call | flops 3246391296 | bytes 17891328 | tf_op jit(solution)/shard_map/ff_forward/pallas_call | solution.py:119
  274.4 11.8 %text_forward.10 = (bf16[344,768]{1,0:T(8,128)(2,1)}, bf16[344,768]{1,0:T(8,128)(2,1)}, bf16[2,344,768]{2,1,0:T(8,128)(2,1)}, bf16[4,800,192]{2,1,0:T(8,128)(2,1...) custom-call(s32[1]{0:T(128)} %constant.80.clone.1.tick, ...), custom_call_target="tpu_custom_call", output_to_operand_aliasing={{0}: (9, {}), {1}: (10, {}), {2}: (11, {}), {6}: (12, {}), ... | custom-call | flops 4010803200 | bytes 7299072 | tf_op jit(solution)/shard_map/text_forward/pallas_call | solution.py:119
  298.7 11.6 %text_forward.11 = (bf16[344,768]{1,0:T(8,128)(2,1)}, bf16[344,768]{1,0:T(8,128)(2,1)}, bf16[2,344,768]{2,1,0:T(8,128)(2,1)}, bf16[4,800,192]{2,1,0:T(8,128)(2,1...) custom-call(s32[1]{0:T(128)} %constant.32.clone.1.tick, ...), custom_call_target="tpu_custom_call", output_to_operand_aliasing={{0}: (9, {}), {1}: (10, {}), {2}: (11, {}), {6}: (12, {}), ... | custom-call | flops 4010803200 | bytes 7299072 | tf_op jit(solution)/shard_map/text_forward/pallas_call | solution.py:119
  372.8 11.3 %collective-permute-done.40.p1 = bf16[344,768]{1,0:T(8,128)(2,1)S(1)} collective-permute-done((bf16[344,768]{1,0:T(8,128)(2,1)}, bf16[344,768]{1,0:T(8,128)(2,1)S(1)}, u32[]{:S(2)}, u32[]{:S(2)}) %collective-permute-start.40) | collective-permute-done | bytes 528416 | tf_op jit(solution)/shard_map/ppermute | solution.py:997
  385.2 16.6 %text_backward.6 = (bf16[344,768]{1,0:T(8,128)(2,1)}, bf16[344,768]{1,0:T(8,128)(2,1)}, bf16[2,344,768]{2,1,0:T(8,128)(2,1)}, bf16[2,576,192]{2,1,0:T(8,128)(2,1...) custom-call(s32[1]{0:T(128)} %constant.32.clone.1.tick, s32[54]{0:T(128)} %concatenate.15.info, ...), custom_call_target="tpu_custom_call" | custom-call | flops 7903641600 | bytes 8527872 | tf_op jit(solution)/shard_map/text_backward/pallas_call | solution.py:119
  411.5 16.3 %text_backward.7 = (bf16[344,768]{1,0:T(8,128)(2,1)}, bf16[344,768]{1,0:T(8,128)(2,1)}, bf16[2,344,768]{2,1,0:T(8,128)(2,1)}, bf16[2,576,192]{2,1,0:T(8,128)(2,1...) custom-call(s32[1]{0:T(128)} %constant.80.clone.1.tick, ...), custom_call_target="tpu_custom_call", output_to_operand_aliasing={{4}: (12, {}), {5}: (13, {})} | custom-call | flops 7903641600 | bytes 8527872 | tf_op jit(solution)/shard_map/text_backward/pallas_call | solution.py:119
  510.8 16.4 %text_backward.8 = (bf16[344,768]{1,0:T(8,128)(2,1)}, bf16[344,768]{1,0:T(8,128)(2,1)}, bf16[2,344,768]{2,1,0:T(8,128)(2,1)}, bf16[2,576,192]{2,1,0:T(8,128)(2,1...) custom-call(s32[1]{0:T(128)} %constant.70.clone.1.tick, ...), custom_call_target="tpu_custom_call", output_to_operand_aliasing={{4}: (12, {}), {5}: (13, {})} | custom-call | flops 7903641600 | bytes 8527872 | tf_op jit(solution)/shard_map/text_backward/pallas_call | solution.py:119
  536.9 16.8 %text_backward.9 = (bf16[344,768]{1,0:T(8,128)(2,1)}, bf16[344,768]{1,0:T(8,128)(2,1)}, bf16[2,344,768]{2,1,0:T(8,128)(2,1)}, bf16[2,576,192]{2,1,0:T(8,128)(2,1...) custom-call(s32[1]{0:T(128)} %constant.79.clone.1.tick, ...), custom_call_target="tpu_custom_call", output_to_operand_aliasing={{4}: (12, {}), {5}: (13, {})} | custom-call | flops 7903641600 | bytes 8527872 | tf_op jit(solution)/shard_map/text_backward/pallas_call | solution.py:119
  635.0 16.6 %text_backward.10 = (bf16[344,768]{1,0:T(8,128)(2,1)}, bf16[344,768]{1,0:T(8,128)(2,1)}, bf16[2,344,768]{2,1,0:T(8,128)(2,1)}, bf16[2,576,192]{2,1,0:T(8,128)(2,...) custom-call(s32[1]{0:T(128)} %constant.71.clone.1.tick, ...), custom_call_target="tpu_custom_call", output_to_operand_aliasing={{4}: (12, {}), {5}: (13, {})} | custom-call | flops 7903641600 | bytes 8527872 | tf_op jit(solution)/shard_map/text_backward/pallas_call | solution.py:119
  652.6 16.3 %text_backward.11 = (bf16[344,768]{1,0:T(8,128)(2,1)}, bf16[344,768]{1,0:T(8,128)(2,1)}, bf16[2,344,768]{2,1,0:T(8,128)(2,1)}, bf16[2,576,192]{2,1,0:T(8,128)(2,...) custom-call(s32[1]{0:T(128)} %constant.73.clone.1.tick, ...), custom_call_target="tpu_custom_call", output_to_operand_aliasing={{4}: (12, {}), {5}: (13, {})} | custom-call | flops 7903641600 | bytes 8527872 | tf_op jit(solution)/shard_map/text_backward/pallas_call | solution.py:119
  668.9 13.1 %text_weights.1 = bf16[4,288,768]{2,1,0:T(8,128)(2,1)} custom-call(bf16[5,800,768]{2,1,0:T(8,128)(2,1)} %get-tuple-element.612.h, bf16[5,800,768]{2,1,0:T(8,128)(2,1)} %get-tuple-element.613.dd, bf16[5,800,384]{2,1,0:T(8,128)(2,1)} %get-tuple-element.614.o, bf16[5,800,768]{2,1,0:T(8,128)(2,1)} %get-tuple-element.615.da), custom_call_target="tpu_custom_call" | custom-call | flops 7077888000 | bytes 21504000 | tf_op jit(solution)/shard_map/text_weights/pallas_call | solution.py:655
  682.0 14.1 %ff_weights.2 = (bf16[4,384,768]{2,1,0:T(8,128)(2,1)}, bf16[4,384,768]{2,1,0:T(8,128)(2,1)}) custom-call(bf16[1720,768]{1,0:T(8,128)(2,1)} %get-tuple-element.609.h2, bf16[1720,768]{1,0:T(8,128)(2,1)} %get-tuple-element.616.dm, bf16[1720,3072]{1,0:T(8,128)(2,1)} %get-tuple-element.648.du, bf16[1720,3072]{1,0:T(8,128)(2,1)} %get-tuple-element.618.g), custom_call_target="tpu_custom_call" | custom-call | flops 6492782592 | bytes 17399808 | tf_op jit(solution)/shard_map/ff_weights/pallas_call | solution.py:898
  723.2 11.4 %image_weights.1 = bf16[4,240,960]{2,1,0:T(8,128)(2,1)} custom-call(bf16[5,576,768]{2,1,0:T(8,128)(2,1)} %get-tuple-element.644.h, bf16[5,576,960]{2,1,0:T(8,128)(2,1)} %get-tuple-element.645.dd, bf16[5,576,192]{2,1,0:T(8,128)(2,1)} %get-tuple-element.646.o, bf16[5,576,768]{2,1,0:T(8,128)(2,1)} %get-tuple-element.647.da), custom_call_target="tpu_custom_call" | custom-call | flops 5096079360 | bytes 15482880 | tf_op jit(solution)/shard_map/image_weights/pallas_call | solution.py:655
  735.8 12.3 %collective-permute-done.77 = bf16[4,96,768]{2,1,0:T(8,128)(2,1)} collective-permute-done((bf16[4,96,768]{2,1,0:T(8,128)(2,1)}, bf16[4,96,768]{2,1,0:T(8,128)(2,1)}, u32[]{:S(2)}, u32[]{:S(2)}) %collective-permute-start.77) | collective-permute-done | bytes 589856 | tf_op jit(solution)/shard_map/ppermute | solution.py:997
  748.1 13.9 %ff_weights.3 = (bf16[4,384,768]{2,1,0:T(8,128)(2,1)}, bf16[4,384,768]{2,1,0:T(8,128)(2,1)}) custom-call(bf16[1720,768]{1,0:T(8,128)(2,1)} %get-tuple-element.609.h2, bf16[1720,768]{1,0:T(8,128)(2,1)} %get-tuple-element.616.dm, bf16[1720,3072]{1,0:T(8,128)(2,1)} %get-tuple-element.648.du, bf16[1720,3072]{1,0:T(8,128)(2,1)} %get-tuple-element.618.g), custom_call_target="tpu_custom_call" | custom-call | flops 6492782592 | bytes 17399808 | tf_op jit(solution)/shard_map/ff_weights/pallas_call | solution.py:898
  762.9 14.9 %collective-permute-done.73 = bf16[4,96,768]{2,1,0:T(8,128)(2,1)S(1)} collective-permute-done((bf16[4,96,768]{2,1,0:T(8,128)(2,1)S(1)}, bf16[4,96,768]{2,1,0:T(8,128)(2,1)S(1)}, u32[]{:S(2)}, u32[]{:S(2)}) %collective-permute-start.73) | collective-permute-done | bytes 589856 | tf_op jit(solution)/shard_map/ppermute | solution.py:997
  784.4 12.8 %collective-permute-done.75.c = bf16[344,768]{1,0:T(8,128)(2,1)S(1)} collective-permute-done((bf16[344,768]{1,0:T(8,128)(2,1)S(1)}, bf16[344,768]{1,0:T(8,128)(2,1)S(1)}, u32[]{:S(2)}, u32[]{:S(2)}) %collective-permute-start.75) | collective-permute-done | bytes 528416 | tf_op jit(solution)/shard_map/ppermute | solution.py:997
  (471 shorter events, 507.9 us)
Async XLA Ops:
  7.2 808.3 %reduce-scatter.6.cloned.1.call-start = ((), (), s32[]{:S(2)}) async-start(), calls=%async_computation.4 | async-start | bytes 2211840 | tf_op jit(solution)/shard_map/reduce_scatter | solution.py:1240
  16.3 20.5 %collective-permute-start.4 = (bf16[344,768]{1,0:T(8,128)(2,1)}, bf16[344,768]{1,0:T(8,128)(2,1)}, u32[]{:S(2)}, u32[]{:S(2)}) collective-permute-start(bf16[344,768]{1,0:T(8,128)(2,1)} %get-tuple-element.345.p0), channel_id=1, source_target_pairs={{0,1},{1,0},{2,3},{3,2},{4,5},{5,4},{6,7},{7,6},{8,9},{9,8},{10,11... | collective-permute-start | bytes 1585160 | tf_op jit(solution)/shard_map/ppermute | solution.py:1001
  19.5 40.2 %collective-permute-start.1 = (bf16[344,768]{1,0:T(8,128)(2,1)}, bf16[344,768]{1,0:T(8,128)(2,1)S(1)}, u32[]{:S(2)}, u32[]{:S(2)}) collective-permute-start(bf16[344,768]{1,0:T(8,128)(2,1)} %get-tuple-element.351.p0), channel_id=1, source_target_pairs={{0,1},{1,0},{2,3},{3,2},{4,5},{5,4},{6,7},{7,6},{8,9},{9,8},{10,11... | collective-permute-start | bytes 1585160 | tf_op jit(solution)/shard_map/ppermute | solution.py:1001
  20.1 20.7 %collective-permute-start = (bf16[344,768]{1,0:T(8,128)(2,1)}, bf16[344,768]{1,0:T(8,128)(2,1)}, u32[]{:S(2)}, u32[]{:S(2)}) collective-permute-start(bf16[344,768]{1,0:T(8,128)(2,1)} %get-tuple-element.351.p0), channel_id=1, source_target_pairs={{0,2},{1,3},{2,0},{3,1},{4,6},{5,7},{6,4},{7,5},{8,10},{9,11},{10,... | collective-permute-start | bytes 1585160 | tf_op jit(solution)/shard_map/ppermute | solution.py:997
  34.7 45.4 %collective-permute-start.8 = (bf16[768,768]{1,0:T(8,128)(2,1)S(1)}, bf16[768,768]{1,0:T(8,128)(2,1)S(1)}, u32[]{:S(2)}, u32[]{:S(2)}) collective-permute-start(bf16[768,768]{1,0:T(8,128)(2,1)S(1)} %bitcast.108), channel_id=1, source_target_pairs={{0,2},{1,3},{2,0},{3,1},{4,6},{5,7},{6,4},{7,5},{8,10},{9,11},{10,... | collective-permute-start | bytes 3538952 | tf_op jit(solution)/shard_map/ppermute | solution.py:997
  36.8 53.6 %collective-permute-start.11 = (bf16[768,768]{1,0:T(8,128)(2,1)S(1)}, bf16[768,768]{1,0:T(8,128)(2,1)S(1)}, u32[]{:S(2)}, u32[]{:S(2)}) collective-permute-start(bf16[768,768]{1,0:T(8,128)(2,1)S(1)} %bitcast.122), channel_id=1, source_target_pairs={{0,2},{1,3},{2,0},{3,1},{4,6},{5,7},{6,4},{7,5},{8,10},{9,11},{10,... | collective-permute-start | bytes 3538952 | tf_op jit(solution)/shard_map/ppermute | solution.py:997
  59.2 31.2 %collective-permute-start.14 = (bf16[2,344,768]{2,1,0:T(8,128)(2,1)}, bf16[2,344,768]{2,1,0:T(8,128)(2,1)}, u32[]{:S(2)}, u32[]{:S(2)}) collective-permute-start(bf16[2,344,768]{2,1,0:T(8,128)(2,1)} %get-tuple-element.369), channel_id=1, source_target_pairs={{0,1},{1,0},{2,3},{3,2},{4,5},{5,4},{6,7},{7,6},{8,9},{9,8},{10,11... | collective-permute-start | bytes 3170312 | tf_op jit(solution)/shard_map/ppermute | solution.py:1001
  95.0 28.4 %collective-permute-start.7 = (bf16[344,768]{1,0:T(8,128)(2,1)}, bf16[344,768]{1,0:T(8,128)(2,1)S(1)}, u32[]{:S(2)}, u32[]{:S(2)}) collective-permute-start(bf16[344,768]{1,0:T(8,128)(2,1)} %fusion.11), channel_id=1, source_target_pairs={{0,2},{1,3},{2,0},{3,1},{4,6},{5,7},{6,4},{7,5},{8,10},{9,11},{10,... | collective-permute-start | bytes 1585160 | tf_op jit(solution)/shard_map/ppermute | solution.py:997
  155.9 21.6 %collective-permute-start.17 = (bf16[344,768]{1,0:T(8,128)(2,1)}, bf16[344,768]{1,0:T(8,128)(2,1)S(1)}, u32[]{:S(2)}, u32[]{:S(2)}) collective-permute-start(bf16[344,768]{1,0:T(8,128)(2,1)} %get-tuple-element.390.p0), channel_id=1, source_target_pairs={{0,2},{1,3},{2,0},{3,1},{4,6},{5,7},{6,4},{7,5},{8,10},{9,11},{10,... | collective-permute-start | bytes 1585160 | tf_op jit(solution)/shard_map/ppermute | solution.py:997
  205.6 26.3 %collective-permute-start.26 = (bf16[344,768]{1,0:T(8,128)(2,1)S(1)}, bf16[344,768]{1,0:T(8,128)(2,1)S(1)}, u32[]{:S(2)}, u32[]{:S(2)}) collective-permute-start(bf16[344,768]{1,0:T(8,128)(2,1)S(1)} %fusion.8), channel_id=1, source_target_pairs={{0,2},{1,3},{2,0},{3,1},{4,6},{5,7},{6,4},{7,5},{8,10},{9,11},{10,... | collective-permute-start | bytes 1585160 | tf_op jit(solution)/shard_map/ppermute | solution.py:997
  265.7 21.0 %collective-permute-start.29 = (bf16[344,768]{1,0:T(8,128)(2,1)}, bf16[344,768]{1,0:T(8,128)(2,1)S(1)}, u32[]{:S(2)}, u32[]{:S(2)}) collective-permute-start(bf16[344,768]{1,0:T(8,128)(2,1)} %get-tuple-element.434.p0), channel_id=1, source_target_pairs={{0,2},{1,3},{2,0},{3,1},{4,6},{5,7},{6,4},{7,5},{8,10},{9,11},{10,... | collective-permute-start | bytes 1585160 | tf_op jit(solution)/shard_map/ppermute | solution.py:997
  314.8 22.0 %collective-permute-start.38 = (bf16[344,768]{1,0:T(8,128)(2,1)S(1)}, bf16[344,768]{1,0:T(8,128)(2,1)S(1)}, u32[]{:S(2)}, u32[]{:S(2)}) collective-permute-start(bf16[344,768]{1,0:T(8,128)(2,1)S(1)} %fusion.6), channel_id=1, source_target_pairs={{0,2},{1,3},{2,0},{3,1},{4,6},{5,7},{6,4},{7,5},{8,10},{9,11},{10,... | collective-permute-start | bytes 1585160 | tf_op jit(solution)/shard_map/ppermute | solution.py:997
  372.6 37.8 %collective-permute-start.41 = (bf16[344,768]{1,0:T(8,128)(2,1)}, bf16[344,768]{1,0:T(8,128)(2,1)S(1)}, u32[]{:S(2)}, u32[]{:S(2)}) collective-permute-start(bf16[344,768]{1,0:T(8,128)(2,1)} %get-tuple-element.483.p0), channel_id=1, source_target_pairs={{0,1},{1,0},{2,3},{3,2},{4,5},{5,4},{6,7},{7,6},{8,9},{9,8},{10,11... | collective-permute-start | bytes 1585160 | tf_op jit(solution)/shard_map/ppermute | solution.py:1001
  384.2 26.3 %collective-permute-start.42 = (bf16[344,768]{1,0:T(8,128)(2,1)S(1)}, bf16[344,768]{1,0:T(8,128)(2,1)S(1)}, u32[]{:S(2)}, u32[]{:S(2)}) collective-permute-start(bf16[344,768]{1,0:T(8,128)(2,1)S(1)} %collective-permute-done.40.p1), channel_id=1, source_target_pairs={{0,1},{1,0},{2,3},{3,2},{4,5},{5,4},{6,7},{7,6},{8,9},{9,8},{10,11... | collective-permute-start | bytes 1585160 | tf_op jit(solution)/shard_map/ppermute | solution.py:1001
  440.8 21.3 %collective-permute-start.48 = (bf16[344,768]{1,0:T(8,128)(2,1)S(1)}, bf16[344,768]{1,0:T(8,128)(2,1)S(1)}, u32[]{:S(2)}, u32[]{:S(2)}) collective-permute-start(bf16[344,768]{1,0:T(8,128)(2,1)S(1)} %fusion.4), channel_id=1, source_target_pairs={{0,2},{1,3},{2,0},{3,1},{4,6},{5,7},{6,4},{7,5},{8,10},{9,11},{10,... | collective-permute-start | bytes 1585160 | tf_op jit(solution)/shard_map/ppermute | solution.py:997
  499.2 36.7 %collective-permute-start.53 = (bf16[344,768]{1,0:T(8,128)(2,1)}, bf16[344,768]{1,0:T(8,128)(2,1)S(1)}, u32[]{:S(2)}, u32[]{:S(2)}) collective-permute-start(bf16[344,768]{1,0:T(8,128)(2,1)} %get-tuple-element.539.p0), channel_id=1, source_target_pairs={{0,1},{1,0},{2,3},{3,2},{4,5},{5,4},{6,7},{7,6},{8,9},{9,8},{10,11... | collective-permute-start | bytes 1585160 | tf_op jit(solution)/shard_map/ppermute | solution.py:1001
  509.7 26.1 %collective-permute-start.54 = (bf16[344,768]{1,0:T(8,128)(2,1)S(1)}, bf16[344,768]{1,0:T(8,128)(2,1)S(1)}, u32[]{:S(2)}, u32[]{:S(2)}) collective-permute-start(bf16[344,768]{1,0:T(8,128)(2,1)S(1)} %collective-permute-done.52.p1), channel_id=1, source_target_pairs={{0,1},{1,0},{2,3},{3,2},{4,5},{5,4},{6,7},{7,6},{8,9},{9,8},{10,11... | collective-permute-start | bytes 1585160 | tf_op jit(solution)/shard_map/ppermute | solution.py:1001
  566.3 21.3 %collective-permute-start.60 = (bf16[344,768]{1,0:T(8,128)(2,1)S(1)}, bf16[344,768]{1,0:T(8,128)(2,1)S(1)}, u32[]{:S(2)}, u32[]{:S(2)}) collective-permute-start(bf16[344,768]{1,0:T(8,128)(2,1)S(1)} %fusion.2), channel_id=1, source_target_pairs={{0,2},{1,3},{2,0},{3,1},{4,6},{5,7},{6,4},{7,5},{8,10},{9,11},{10,... | collective-permute-start | bytes 1585160 | tf_op jit(solution)/shard_map/ppermute | solution.py:997
  623.1 28.5 %collective-permute-start.65 = (bf16[344,768]{1,0:T(8,128)(2,1)}, bf16[344,768]{1,0:T(8,128)(2,1)S(1)}, u32[]{:S(2)}, u32[]{:S(2)}) collective-permute-start(bf16[344,768]{1,0:T(8,128)(2,1)} %get-tuple-element.589.p0), channel_id=1, source_target_pairs={{0,1},{1,0},{2,3},{3,2},{4,5},{5,4},{6,7},{7,6},{8,9},{9,8},{10,11... | collective-permute-start | bytes 1585160 | tf_op jit(solution)/shard_map/ppermute | solution.py:1001
  696.6 132.6 %reduce-scatter.4.cloned.1.call-start = ((), (), s32[]{:S(2)}) async-start(), calls=%async_computation.3 | async-start | bytes 2457600 | tf_op jit(solution)/shard_map/reduce_scatter | solution.py:1240
  717.1 44.8 %collective-permute-start.78 = (bf16[4,96,768]{2,1,0:T(8,128)(2,1)}, bf16[4,96,768]{2,1,0:T(8,128)(2,1)}, u32[]{:S(2)}, u32[]{:S(2)}) collective-permute-start(bf16[4,96,768]{2,1,0:T(8,128)(2,1)} %get-tuple-element.701), channel_id=1, source_target_pairs={{0,2},{1,3},{2,0},{3,1},{4,6},{5,7},{6,4},{7,5},{8,10},{9,11},{10,... | collective-permute-start | bytes 1769480 | tf_op jit(solution)/shard_map/ppermute | solution.py:997
  718.5 29.7 %collective-permute-start.77 = (bf16[4,96,768]{2,1,0:T(8,128)(2,1)}, bf16[4,96,768]{2,1,0:T(8,128)(2,1)}, u32[]{:S(2)}, u32[]{:S(2)}) collective-permute-start(bf16[4,96,768]{2,1,0:T(8,128)(2,1)} %get-tuple-element.702), channel_id=1, source_target_pairs={{0,2},{1,3},{2,0},{3,1},{4,6},{5,7},{6,4},{7,5},{8,10},{9,11},{10,... | collective-permute-start | bytes 1769480 | tf_op jit(solution)/shard_map/ppermute | solution.py:997
  734.6 98.8 %reduce-scatter.8.cloned.1.call-start = ((), (), s32[]{:S(2)}) async-start(), calls=%async_computation.5 | async-start | bytes 2949120 | tf_op jit(solution)/shard_map/reduce_scatter | solution.py:1240
  783.1 24.1 %collective-permute-start.72 = (bf16[344,768]{1,0:T(8,128)(2,1)S(1)}, bf16[344,768]{1,0:T(8,128)(2,1)S(1)}, u32[]{:S(2)}, u32[]{:S(2)}) collective-permute-start(bf16[344,768]{1,0:T(8,128)(2,1)S(1)} %fusion.1), channel_id=1, source_target_pairs={{0,2},{1,3},{2,0},{3,1},{4,6},{5,7},{6,4},{7,5},{8,10},{9,11},{10,... | collective-permute-start | bytes 1585160 | tf_op jit(solution)/shard_map/ppermute | solution.py:997
  (168 other events, 1380.0 us)
Sparse Core Ops, SparseCore 0:
  696.7 38.2 reduce-scatter.5
  737.4 40.5 reduce-scatter.3
  781.5 48.2 reduce-scatter.7

commit v4 on v3

--- a/solution.py
+++ b/solution.py
@@ -1001,8 +1001,8 @@
     return lax.ppermute(array, "mp", [(m, m ^ 1) for m in range(4)])
 
 
-def gathered(own):
-    across = over_y(own)
+def gathered(own, across=None):
+    across = over_y(own) if across is None else across
     return (own, across, over_core(own), over_core(across))
 
 
@@ -1096,7 +1096,10 @@
         got = relayed.get(t - SKEW, nothing)
         if t >= SKEW and t % SKEW == 0:
             got = hold((got,), ahead["out"])[0]
+        elif t % SKEW > 0:
+            got = hold((got,), ahead["h"])[0]
         x, h = entry(tick_at[t], info, min(t, micro - 1), image, text, got, gain, bias)
+        ahead["h"] = h
         pieces = gathered(h)
         if up is None:
             up_own, down_own, _ = lax.optimization_barrier((up_proj[0], down_proj[0], pieces[1]))
@@ -1121,8 +1124,9 @@
 
     def feed(t, parts):
         nonlocal ff_stacks
+        x = hold((state[t][0],), ahead["out"])[0] if t % SKEW > 0 else state[t][0]
         mid, gp, z, *ff_stacks = ff_forward(
-            tick_at[t], info, ni, micro, state[t][0], parts, gain, bias, up, down, ff_stacks
+            tick_at[t], info, ni, micro, x, parts, gain, bias, up, down, ff_stacks
         )
         state[t] += [mid, gp]
         ahead["out"] = z
@@ -1147,12 +1151,15 @@
         back = relayed.get(k - SKEW, nothing)
         if k >= SKEW and k % SKEW == 0:
             back = hold((back,), ahead["out"])[0]
+        elif k % SKEW > 0:
+            back = hold((back,), ahead["da"])[0]
         dmid, da, sums, *ff_stacks = ff_backward(
             tick_at[t], info, max(t - SKEW, 0), micro, image_cot, text_cot, back, gp, mid, gain,
             up, down, ff_stacks,
         )
         sums_two = sums_two + sums
-        return dmid, gathered(da)
+        ahead["da"] = da
+        return dmid, da, over_y(da)
 
     def text_part(k, pieces):
         nonlocal text_back
@@ -1177,6 +1184,8 @@
     def finish(k, parts, dmid):
         nonlocal close_stacks, sums_one
         t = ticks - 1 - k
+        if k % SKEW > 0:
+            dmid = hold((dmid,), ahead["out"])[0]
         back, sums, *close_stacks = close(
             tick_at[t], info, ni, micro, state[t][0], parts, dmid, gain, close_stacks
         )
@@ -1191,30 +1200,36 @@
         second = k % SKEW > 0
         if not second:
             fed = {k + i: descend(k + i) for i in range(SKEW)}
-        dmid, pieces = fed[k]
+        dmid, da, across = fed[k]
+        across = hold((across,), ahead["text"] if second else ahead["da"])[0]
+        pieces = gathered(da, across)
         if second:
             pieces = hold(pieces, ahead["own"])
         parts, dkv = text_part(k, pieces)
+        ahead["text"] = parts[0]
         if second:
-            parts = hold(parts, ahead["across"])
+            parts = hold(parts, ahead["crossed"])
         r0, other, across = image_part(k, pieces, parts, dkv)
-        ahead.update(own=r0, across=across)
-        fed[k] = (k, (r0, other, over_y(across)), dmid)
+        crossed = over_y(across)
+        ahead.update(own=r0, crossed=crossed)
+        fed[k] = (k, (r0, other, crossed), dmid)
         if k % SKEW == SKEW - 1:
             for i in range(k - SKEW + 1, k + 1):
                 finish(*fed[i])
 
     one, two = final, final + 1
-    (dmid_one, pieces_one), (dmid_two, pieces_two) = descend(one), descend(two)
+    (dmid_one, da_one, a_one), (dmid_two, da_two, a_two) = descend(one), descend(two)
+    pieces_one = gathered(da_one, *hold((a_one,), da_two))
     parts_one, dkv_one = text_part(one, pieces_one)
-    pieces_two = hold(pieces_two, parts_one[0])
+    pieces_two = hold(gathered(da_two, *hold((a_two,), parts_one[0])), parts_one[0])
     parts_two, dkv_two = text_part(two, pieces_two)
+    dm, du = hold(ff_stacks, parts_two[0])
+    far, y_part = ff_weights((3, 1), micro, h2, dm, du, g, groups)
+    text_all = hold((*text_stacks, *text_back), far)
     text_w = attention_weights(
-        text_stacks[0], text_back[1], text_stacks[1], text_back[0], groups, "text_weights"
+        text_all[0], text_all[3], text_all[1], text_all[2], groups, "text_weights"
     )
-    dm, du = hold(ff_stacks, text_w)
-    far, y_part = ff_weights((3, 1), micro, h2, dm, du, g, groups)
-    parts_one = hold(parts_one, far)
+    parts_one = hold(parts_one, text_w)
     r0_one, other_one, across_one = image_part(one, pieces_one, parts_one, dkv_one)
     ff_across = (y_part.astype(F32) + over_core(far).astype(F32)).astype(BF16)
     parts_two = hold(parts_two, r0_one, ff_across)
@@ -1229,8 +1244,8 @@
     near, core_part = ff_weights((0, 2), micro, h2, dm, du, g, groups)
     core_part = hold((core_part,), crossed[2])[0]
     dmid_one = hold((dmid_one,), near)[0]
+    dmid_two = hold((dmid_two,), crossed[3])[0]
     finish(one, (r0_one, other_one, over_y(across_one)), dmid_one)
-    dmid_two = hold((dmid_two,), crossed[3])[0]
     finish(two, (r0_two, other_two, over_y(across_two)), dmid_two)
     ff_sum = (
         near.astype(F32) + over_core(core_part).astype(F32) + jnp.concatenate(crossed, axis=1).astype(F32)

time: 847 us -> 812 us (0.959)
  waiting for transfers between devices: 204 us -> 172 us
    ppermute x30, waiting for transfers between devices: 176 us -> 131 us  [over_y(): return lax.ppermute(array, 'mp', [(m, m ^ 2) for m in range(4)])]
    ppermute x42, waiting for transfers between devices: 14.2 us -> 27.1 us  [over_core(): return lax.ppermute(array, 'mp', [(m, m ^ 1) for m in range(4)])]
    unnamed x213 -> x207, local copies, waits for them, and re-layouts: 31.8 us -> 27.5 us
  transfers between devices with their start and end apart: 87 -> 87, of which waited for: 37 -> 42; matrix products, arithmetic and copies ran while one was open for 4% -> 4% of each run, Pallas kernels for 44% -> 46%
where the time goes in v4:
time: 812 us; the launch traced here: 807 us
  Pallas kernels  488 us (60%)
  waiting for transfers between devices  172 us (21%)
  starting transfers between devices  64.1 us (8%)
  local copies, waits for them, and re-layouts  40 us (5%)
  other arithmetic  27.2 us (3%)
  between operations  15.7 us (2%)
    pallas_call x48, Pallas kernels, run(): pl.pallas_call(kernel, out_shape=tuple(outs), in_specs=[SMEM_SPEC] * lead...  436 us
    ppermute x30, waiting for transfers between devices, over_y(): return lax.ppermute(array, 'mp', [(m, m ^ 2) for m in range(4)])  131 us
    ppermute x30, starting transfers between devices, over_y(): return lax.ppermute(array, 'mp', [(m, m ^ 2) for m in range(4)])  34.6 us
    pallas_call x2, Pallas kernels, ff_weights(): pl.pallas_call(ff_weights_kernel, grid=(2,), out_shape=(shape_of(part, BF...  27.9 us
    unnamed x207, local copies, waits for them, and re-layouts  27.5 us
    ppermute x42, waiting for transfers between devices, over_core(): return lax.ppermute(array, 'mp', [(m, m ^ 1) for m in range(4)])  27.1 us
    pallas_call x2, Pallas kernels, attention_weights(): pl.pallas_call(attention_weights_kernel, grid=(slots - 1,), out_shape=sha...  24.6 us
    ppermute x8, starting transfers between devices, shifted(): lax.ppermute(array, 'section', [(i, i + by) for i in range(length) if 0 <...  17.2 us
  transfers between devices with their start and end apart: 87, of which 42 were waited for; matrix products, arithmetic and copies ran while one was open for 4% of the time, Pallas kernels for 46%

profile of v4, /device:TPU:0, one launch (start us, length us, event | category | flops | bytes accessed | tf_op | source)
XLA Modules:
  0.0 807.1 jit_solution(14950177279550368378)
XLA Ops:
  47.6 11.6 %text_forward.6 = (bf16[344,768]{1,0:T(8,128)(2,1)}, bf16[344,768]{1,0:T(8,128)(2,1)}, bf16[2,344,768]{2,1,0:T(8,128)(2,1)}, bf16[4,800,192]{2,1,0:T(8,128)(2,1)...) custom-call(s32[1]{0:T(128)} %constant.73.clone.1.tick, ...), custom_call_target="tpu_custom_call", output_to_operand_aliasing={{0}: (9, {}), {1}: (10, {}), {2}: (11, {})} | custom-call | flops 4010803200 | bytes 7299072 | tf_op jit(solution)/shard_map/text_forward/pallas_call | solution.py:119
  68.0 11.6 %text_forward.7 = (bf16[344,768]{1,0:T(8,128)(2,1)}, bf16[344,768]{1,0:T(8,128)(2,1)}, bf16[2,344,768]{2,1,0:T(8,128)(2,1)}, bf16[4,800,192]{2,1,0:T(8,128)(2,1)...) custom-call(s32[1]{0:T(128)} %constant.71.clone.1.tick, ...), custom_call_target="tpu_custom_call", output_to_operand_aliasing={{0}: (9, {}), {1}: (10, {}), {2}: (11, {}), {6}: (12, {}), ... | custom-call | flops 4010803200 | bytes 7299072 | tf_op jit(solution)/shard_map/text_forward/pallas_call | solution.py:119
  95.5 11.8 %collective-permute-done.4.c = bf16[344,768]{1,0:T(8,128)(2,1)S(1)} collective-permute-done((bf16[344,768]{1,0:T(8,128)(2,1)S(1)}, bf16[344,768]{1,0:T(8,128)(2,1)S(1)}, u32[]{:S(2)}, u32[]{:S(2)}) %collective-permute-start.4) | collective-permute-done | bytes 528416 | tf_op jit(solution)/shard_map/ppermute | solution.py:997
  109.1 11.5 %ff_forward.6 = (f32[344,768]{1,0:T(8,128)}, bf16[344,3072]{1,0:T(8,128)(2,1)}, bf16[344,768]{1,0:T(8,128)(2,1)}, bf16[1720,768]{1,0:T(8,128)(2,1)}, bf16[1720,3...) custom-call(s32[1]{0:T(128)} %constant.73.clone.1.tick, s32[54]{0:T(128)} %concatenate.15.info, ...), custom_call_target="tpu_custom_call" | custom-call | flops 3246391296 | bytes 17891328 | tf_op jit(solution)/shard_map/ff_forward/pallas_call | solution.py:119
  124.3 11.3 %ff_forward.7 = (f32[344,768]{1,0:T(8,128)}, bf16[344,3072]{1,0:T(8,128)(2,1)}, bf16[344,768]{1,0:T(8,128)(2,1)}, bf16[1720,768]{1,0:T(8,128)(2,1)}, bf16[1720,3...) custom-call(s32[1]{0:T(128)} %constant.71.clone.1.tick, ...), custom_call_target="tpu_custom_call", output_to_operand_aliasing={{3}: (16, {}), {4}: (17, {}), {5}: (18, {}), {6}: (19, {})} | custom-call | flops 3246391296 | bytes 17891328 | tf_op jit(solution)/shard_map/ff_forward/pallas_call | solution.py:119
  165.3 11.8 %text_forward.8 = (bf16[344,768]{1,0:T(8,128)(2,1)}, bf16[344,768]{1,0:T(8,128)(2,1)}, bf16[2,344,768]{2,1,0:T(8,128)(2,1)}, bf16[4,800,192]{2,1,0:T(8,128)(2,1)...) custom-call(s32[1]{0:T(128)} %constant.79.clone.1.tick, ...), custom_call_target="tpu_custom_call", output_to_operand_aliasing={{0}: (9, {}), {1}: (10, {}), {2}: (11, {}), {6}: (12, {}), ... | custom-call | flops 4010803200 | bytes 7299072 | tf_op jit(solution)/shard_map/text_forward/pallas_call | solution.py:119
  189.6 11.6 %text_forward.9 = (bf16[344,768]{1,0:T(8,128)(2,1)}, bf16[344,768]{1,0:T(8,128)(2,1)}, bf16[2,344,768]{2,1,0:T(8,128)(2,1)}, bf16[4,800,192]{2,1,0:T(8,128)(2,1)...) custom-call(s32[1]{0:T(128)} %constant.70.clone.1.tick, ...), custom_call_target="tpu_custom_call", output_to_operand_aliasing={{0}: (9, {}), {1}: (10, {}), {2}: (11, {}), {6}: (12, {}), ... | custom-call | flops 4010803200 | bytes 7299072 | tf_op jit(solution)/shard_map/text_forward/pallas_call | solution.py:119
  217.1 11.5 %ff_forward.8 = (f32[344,768]{1,0:T(8,128)}, bf16[344,3072]{1,0:T(8,128)(2,1)}, bf16[344,768]{1,0:T(8,128)(2,1)}, bf16[1720,768]{1,0:T(8,128)(2,1)}, bf16[1720,3...) custom-call(s32[1]{0:T(128)} %constant.79.clone.1.tick, ...), custom_call_target="tpu_custom_call", output_to_operand_aliasing={{3}: (16, {}), {4}: (17, {}), {5}: (18, {}), {6}: (19, {})} | custom-call | flops 3246391296 | bytes 17891328 | tf_op jit(solution)/shard_map/ff_forward/pallas_call | solution.py:119
  232.8 11.3 %ff_forward.9 = (f32[344,768]{1,0:T(8,128)}, bf16[344,3072]{1,0:T(8,128)(2,1)}, bf16[344,768]{1,0:T(8,128)(2,1)}, bf16[1720,768]{1,0:T(8,128)(2,1)}, bf16[1720,3...) custom-call(s32[1]{0:T(128)} %constant.70.clone.1.tick, ...), custom_call_target="tpu_custom_call", output_to_operand_aliasing={{3}: (16, {}), {4}: (17, {}), {5}: (18, {}), {6}: (19, {})} | custom-call | flops 3246391296 | bytes 17891328 | tf_op jit(solution)/shard_map/ff_forward/pallas_call | solution.py:119
  274.5 11.8 %text_forward.10 = (bf16[344,768]{1,0:T(8,128)(2,1)}, bf16[344,768]{1,0:T(8,128)(2,1)}, bf16[2,344,768]{2,1,0:T(8,128)(2,1)}, bf16[4,800,192]{2,1,0:T(8,128)(2,1...) custom-call(s32[1]{0:T(128)} %constant.80.clone.1.tick, ...), custom_call_target="tpu_custom_call", output_to_operand_aliasing={{0}: (9, {}), {1}: (10, {}), {2}: (11, {}), {6}: (12, {}), ... | custom-call | flops 4010803200 | bytes 7299072 | tf_op jit(solution)/shard_map/text_forward/pallas_call | solution.py:119
  298.8 11.6 %text_forward.11 = (bf16[344,768]{1,0:T(8,128)(2,1)}, bf16[344,768]{1,0:T(8,128)(2,1)}, bf16[2,344,768]{2,1,0:T(8,128)(2,1)}, bf16[4,800,192]{2,1,0:T(8,128)(2,1...) custom-call(s32[1]{0:T(128)} %constant.32.clone.1.tick, ...), custom_call_target="tpu_custom_call", output_to_operand_aliasing={{0}: (9, {}), {1}: (10, {}), {2}: (11, {}), {6}: (12, {}), ... | custom-call | flops 4010803200 | bytes 7299072 | tf_op jit(solution)/shard_map/text_forward/pallas_call | solution.py:119
  375.1 16.6 %text_backward.6 = (bf16[344,768]{1,0:T(8,128)(2,1)}, bf16[344,768]{1,0:T(8,128)(2,1)}, bf16[2,344,768]{2,1,0:T(8,128)(2,1)}, bf16[2,576,192]{2,1,0:T(8,128)(2,1...) custom-call(s32[1]{0:T(128)} %constant.32.clone.1.tick, s32[54]{0:T(128)} %concatenate.15.info, ...), custom_call_target="tpu_custom_call" | custom-call | flops 7903641600 | bytes 8527872 | tf_op jit(solution)/shard_map/text_backward/pallas_call | solution.py:119
  406.9 16.5 %text_backward.7 = (bf16[344,768]{1,0:T(8,128)(2,1)}, bf16[344,768]{1,0:T(8,128)(2,1)}, bf16[2,344,768]{2,1,0:T(8,128)(2,1)}, bf16[2,576,192]{2,1,0:T(8,128)(2,1...) custom-call(s32[1]{0:T(128)} %constant.80.clone.1.tick, ...), custom_call_target="tpu_custom_call", output_to_operand_aliasing={{4}: (12, {}), {5}: (13, {})} | custom-call | flops 7903641600 | bytes 8527872 | tf_op jit(solution)/shard_map/text_backward/pallas_call | solution.py:119
  486.5 16.3 %text_backward.8 = (bf16[344,768]{1,0:T(8,128)(2,1)}, bf16[344,768]{1,0:T(8,128)(2,1)}, bf16[2,344,768]{2,1,0:T(8,128)(2,1)}, bf16[2,576,192]{2,1,0:T(8,128)(2,1...) custom-call(s32[1]{0:T(128)} %constant.70.clone.1.tick, ...), custom_call_target="tpu_custom_call", output_to_operand_aliasing={{4}: (12, {}), {5}: (13, {})} | custom-call | flops 7903641600 | bytes 8527872 | tf_op jit(solution)/shard_map/text_backward/pallas_call | solution.py:119
  518.2 16.7 %text_backward.9 = (bf16[344,768]{1,0:T(8,128)(2,1)}, bf16[344,768]{1,0:T(8,128)(2,1)}, bf16[2,344,768]{2,1,0:T(8,128)(2,1)}, bf16[2,576,192]{2,1,0:T(8,128)(2,1...) custom-call(s32[1]{0:T(128)} %constant.79.clone.1.tick, ...), custom_call_target="tpu_custom_call", output_to_operand_aliasing={{4}: (12, {}), {5}: (13, {})} | custom-call | flops 7903641600 | bytes 8527872 | tf_op jit(solution)/shard_map/text_backward/pallas_call | solution.py:119
  596.3 16.6 %text_backward.10 = (bf16[344,768]{1,0:T(8,128)(2,1)}, bf16[344,768]{1,0:T(8,128)(2,1)}, bf16[2,344,768]{2,1,0:T(8,128)(2,1)}, bf16[2,576,192]{2,1,0:T(8,128)(2,...) custom-call(s32[1]{0:T(128)} %constant.71.clone.1.tick, ...), custom_call_target="tpu_custom_call", output_to_operand_aliasing={{4}: (12, {}), {5}: (13, {})} | custom-call | flops 7903641600 | bytes 8527872 | tf_op jit(solution)/shard_map/text_backward/pallas_call | solution.py:119
  615.7 16.4 %text_backward.11 = (bf16[344,768]{1,0:T(8,128)(2,1)}, bf16[344,768]{1,0:T(8,128)(2,1)}, bf16[2,344,768]{2,1,0:T(8,128)(2,1)}, bf16[2,576,192]{2,1,0:T(8,128)(2,...) custom-call(s32[1]{0:T(128)} %constant.73.clone.1.tick, ...), custom_call_target="tpu_custom_call", output_to_operand_aliasing={{4}: (12, {}), {5}: (13, {})} | custom-call | flops 7903641600 | bytes 8527872 | tf_op jit(solution)/shard_map/text_backward/pallas_call | solution.py:119
  632.2 14.0 %ff_weights.2 = (bf16[4,384,768]{2,1,0:T(8,128)(2,1)}, bf16[4,384,768]{2,1,0:T(8,128)(2,1)}) custom-call(bf16[1720,768]{1,0:T(8,128)(2,1)} %get-tuple-element.649.h2, bf16[1720,768]{1,0:T(8,128)(2,1)} %get-tuple-element.652.dm, bf16[1720,3072]{1,0:T(8,128)(2,1)} %get-tuple-element.688.du, bf16[1720,3072]{1,0:T(8,128)(2,1)} %get-tuple-element.654.g), custom_call_target="tpu_custom_call" | custom-call | flops 6492782592 | bytes 17399808 | tf_op jit(solution)/shard_map/ff_weights/pallas_call | solution.py:898
  646.3 13.1 %text_weights.1 = bf16[4,288,768]{2,1,0:T(8,128)(2,1)} custom-call(bf16[5,800,768]{2,1,0:T(8,128)(2,1)} %get-tuple-element.656.h, bf16[5,800,768]{2,1,0:T(8,128)(2,1)} %get-tuple-element.657.dd, bf16[5,800,384]{2,1,0:T(8,128)(2,1)} %get-tuple-element.658.o, bf16[5,800,768]{2,1,0:T(8,128)(2,1)} %get-tuple-element.659.da), custom_call_target="tpu_custom_call" | custom-call | flops 7077888000 | bytes 21504000 | tf_op jit(solution)/shard_map/text_weights/pallas_call | solution.py:655
  686.4 11.5 %image_weights.1 = bf16[4,240,960]{2,1,0:T(8,128)(2,1)} custom-call(bf16[5,576,768]{2,1,0:T(8,128)(2,1)} %get-tuple-element.684.h, bf16[5,576,960]{2,1,0:T(8,128)(2,1)} %get-tuple-element.685.dd, bf16[5,576,192]{2,1,0:T(8,128)(2,1)} %get-tuple-element.686.o, bf16[5,576,768]{2,1,0:T(8,128)(2,1)} %get-tuple-element.687.da), custom_call_target="tpu_custom_call" | custom-call | flops 5096079360 | bytes 15482880 | tf_op jit(solution)/shard_map/image_weights/pallas_call | solution.py:655
  699.0 11.9 %collective-permute-done.77 = bf16[4,96,768]{2,1,0:T(8,128)(2,1)} collective-permute-done((bf16[4,96,768]{2,1,0:T(8,128)(2,1)}, bf16[4,96,768]{2,1,0:T(8,128)(2,1)}, u32[]{:S(2)}, u32[]{:S(2)}) %collective-permute-start.77) | collective-permute-done | bytes 589856 | tf_op jit(solution)/shard_map/ppermute | solution.py:997
  711.0 13.9 %ff_weights.3 = (bf16[4,384,768]{2,1,0:T(8,128)(2,1)}, bf16[4,384,768]{2,1,0:T(8,128)(2,1)}) custom-call(bf16[1720,768]{1,0:T(8,128)(2,1)} %get-tuple-element.649.h2, bf16[1720,768]{1,0:T(8,128)(2,1)} %get-tuple-element.652.dm, bf16[1720,3072]{1,0:T(8,128)(2,1)} %get-tuple-element.688.du, bf16[1720,3072]{1,0:T(8,128)(2,1)} %get-tuple-element.654.g), custom_call_target="tpu_custom_call" | custom-call | flops 6492782592 | bytes 17399808 | tf_op jit(solution)/shard_map/ff_weights/pallas_call | solution.py:898
  725.8 14.9 %collective-permute-done.73 = bf16[4,96,768]{2,1,0:T(8,128)(2,1)S(1)} collective-permute-done((bf16[4,96,768]{2,1,0:T(8,128)(2,1)S(1)}, bf16[4,96,768]{2,1,0:T(8,128)(2,1)S(1)}, u32[]{:S(2)}, u32[]{:S(2)}) %collective-permute-start.73) | collective-permute-done | bytes 589856 | tf_op jit(solution)/shard_map/ppermute | solution.py:997
  747.3 12.8 %collective-permute-done.75.c = bf16[344,768]{1,0:T(8,128)(2,1)S(1)} collective-permute-done((bf16[344,768]{1,0:T(8,128)(2,1)S(1)}, bf16[344,768]{1,0:T(8,128)(2,1)S(1)}, u32[]{:S(2)}, u32[]{:S(2)}) %collective-permute-start.75) | collective-permute-done | bytes 528416 | tf_op jit(solution)/shard_map/ppermute | solution.py:997
  (465 shorter events, 472.7 us)
Async XLA Ops:
  7.2 771.1 %reduce-scatter.6.cloned.1.call-start = ((), (), s32[]{:S(2)}) async-start(), calls=%async_computation.4 | async-start | bytes 2211840 | tf_op jit(solution)/shard_map/reduce_scatter | solution.py:1255
  16.4 20.5 %collective-permute-start.1 = (bf16[344,768]{1,0:T(8,128)(2,1)}, bf16[344,768]{1,0:T(8,128)(2,1)}, u32[]{:S(2)}, u32[]{:S(2)}) collective-permute-start(bf16[344,768]{1,0:T(8,128)(2,1)} %get-tuple-element.363.p0), channel_id=1, source_target_pairs={{0,1},{1,0},{2,3},{3,2},{4,5},{5,4},{6,7},{7,6},{8,9},{9,8},{10,11... | collective-permute-start | bytes 1585160 | tf_op jit(solution)/shard_map/ppermute | solution.py:1001
  19.6 40.2 %collective-permute-start.12 = (bf16[344,768]{1,0:T(8,128)(2,1)}, bf16[344,768]{1,0:T(8,128)(2,1)S(1)}, u32[]{:S(2)}, u32[]{:S(2)}) collective-permute-start(bf16[344,768]{1,0:T(8,128)(2,1)} %get-tuple-element.379.p0), channel_id=1, source_target_pairs={{0,1},{1,0},{2,3},{3,2},{4,5},{5,4},{6,7},{7,6},{8,9},{9,8},{10,11... | collective-permute-start | bytes 1585160 | tf_op jit(solution)/shard_map/ppermute | solution.py:1001
  20.2 20.7 %collective-permute-start.11 = (bf16[344,768]{1,0:T(8,128)(2,1)}, bf16[344,768]{1,0:T(8,128)(2,1)}, u32[]{:S(2)}, u32[]{:S(2)}) collective-permute-start(bf16[344,768]{1,0:T(8,128)(2,1)} %get-tuple-element.379.p0), channel_id=1, source_target_pairs={{0,2},{1,3},{2,0},{3,1},{4,6},{5,7},{6,4},{7,5},{8,10},{9,11},{10,... | collective-permute-start | bytes 1585160 | tf_op jit(solution)/shard_map/ppermute | solution.py:997
  34.8 45.4 %collective-permute-start.5 = (bf16[768,768]{1,0:T(8,128)(2,1)S(1)}, bf16[768,768]{1,0:T(8,128)(2,1)S(1)}, u32[]{:S(2)}, u32[]{:S(2)}) collective-permute-start(bf16[768,768]{1,0:T(8,128)(2,1)S(1)} %bitcast.108), channel_id=1, source_target_pairs={{0,2},{1,3},{2,0},{3,1},{4,6},{5,7},{6,4},{7,5},{8,10},{9,11},{10,... | collective-permute-start | bytes 3538952 | tf_op jit(solution)/shard_map/ppermute | solution.py:997
  36.9 53.6 %collective-permute-start.8 = (bf16[768,768]{1,0:T(8,128)(2,1)S(1)}, bf16[768,768]{1,0:T(8,128)(2,1)S(1)}, u32[]{:S(2)}, u32[]{:S(2)}) collective-permute-start(bf16[768,768]{1,0:T(8,128)(2,1)S(1)} %bitcast.122), channel_id=1, source_target_pairs={{0,2},{1,3},{2,0},{3,1},{4,6},{5,7},{6,4},{7,5},{8,10},{9,11},{10,... | collective-permute-start | bytes 3538952 | tf_op jit(solution)/shard_map/ppermute | solution.py:997
  40.9 19.0 %collective-permute-start.13 = (bf16[344,768]{1,0:T(8,128)(2,1)}, bf16[344,768]{1,0:T(8,128)(2,1)S(1)}, u32[]{:S(2)}, u32[]{:S(2)}) collective-permute-start(bf16[344,768]{1,0:T(8,128)(2,1)} %collective-permute-done.11.p1), channel_id=1, source_target_pairs={{0,1},{1,0},{2,3},{3,2},{4,5},{5,4},{6,7},{7,6},{8,9},{9,8},{10,11... | collective-permute-start | bytes 1585160 | tf_op jit(solution)/shard_map/ppermute | solution.py:1001
  59.3 31.2 %collective-permute-start.3 = (bf16[2,344,768]{2,1,0:T(8,128)(2,1)}, bf16[2,344,768]{2,1,0:T(8,128)(2,1)}, u32[]{:S(2)}, u32[]{:S(2)}) collective-permute-start(bf16[2,344,768]{2,1,0:T(8,128)(2,1)} %get-tuple-element.372), channel_id=1, source_target_pairs={{0,1},{1,0},{2,3},{3,2},{4,5},{5,4},{6,7},{7,6},{8,9},{9,8},{10,11... | collective-permute-start | bytes 3170312 | tf_op jit(solution)/shard_map/ppermute | solution.py:1001
  95.1 28.3 %collective-permute-start.15 = (bf16[344,768]{1,0:T(8,128)(2,1)}, bf16[344,768]{1,0:T(8,128)(2,1)S(1)}, u32[]{:S(2)}, u32[]{:S(2)}) collective-permute-start(bf16[344,768]{1,0:T(8,128)(2,1)} %fusion.10), channel_id=1, source_target_pairs={{0,2},{1,3},{2,0},{3,1},{4,6},{5,7},{6,4},{7,5},{8,10},{9,11},{10,... | collective-permute-start | bytes 1585160 | tf_op jit(solution)/shard_map/ppermute | solution.py:997
  156.0 21.7 %collective-permute-start.23 = (bf16[344,768]{1,0:T(8,128)(2,1)}, bf16[344,768]{1,0:T(8,128)(2,1)S(1)}, u32[]{:S(2)}, u32[]{:S(2)}) collective-permute-start(bf16[344,768]{1,0:T(8,128)(2,1)} %get-tuple-element.422.p0), channel_id=1, source_target_pairs={{0,2},{1,3},{2,0},{3,1},{4,6},{5,7},{6,4},{7,5},{8,10},{9,11},{10,... | collective-permute-start | bytes 1585160 | tf_op jit(solution)/shard_map/ppermute | solution.py:997
  205.7 26.3 %collective-permute-start.27 = (bf16[344,768]{1,0:T(8,128)(2,1)S(1)}, bf16[344,768]{1,0:T(8,128)(2,1)S(1)}, u32[]{:S(2)}, u32[]{:S(2)}) collective-permute-start(bf16[344,768]{1,0:T(8,128)(2,1)S(1)} %fusion.8), channel_id=1, source_target_pairs={{0,2},{1,3},{2,0},{3,1},{4,6},{5,7},{6,4},{7,5},{8,10},{9,11},{10,... | collective-permute-start | bytes 1585160 | tf_op jit(solution)/shard_map/ppermute | solution.py:997
  265.8 21.0 %collective-permute-start.30 = (bf16[344,768]{1,0:T(8,128)(2,1)}, bf16[344,768]{1,0:T(8,128)(2,1)S(1)}, u32[]{:S(2)}, u32[]{:S(2)}) collective-permute-start(bf16[344,768]{1,0:T(8,128)(2,1)} %get-tuple-element.459.p0), channel_id=1, source_target_pairs={{0,2},{1,3},{2,0},{3,1},{4,6},{5,7},{6,4},{7,5},{8,10},{9,11},{10,... | collective-permute-start | bytes 1585160 | tf_op jit(solution)/shard_map/ppermute | solution.py:997
  314.9 22.0 %collective-permute-start.38 = (bf16[344,768]{1,0:T(8,128)(2,1)S(1)}, bf16[344,768]{1,0:T(8,128)(2,1)S(1)}, u32[]{:S(2)}, u32[]{:S(2)}) collective-permute-start(bf16[344,768]{1,0:T(8,128)(2,1)S(1)} %fusion.6), channel_id=1, source_target_pairs={{0,2},{1,3},{2,0},{3,1},{4,6},{5,7},{6,4},{7,5},{8,10},{9,11},{10,... | collective-permute-start | bytes 1585160 | tf_op jit(solution)/shard_map/ppermute | solution.py:997
  372.4 19.3 %collective-permute-start.40 = (bf16[344,768]{1,0:T(8,128)(2,1)}, bf16[344,768]{1,0:T(8,128)(2,1)S(1)}, u32[]{:S(2)}, u32[]{:S(2)}) collective-permute-start(bf16[344,768]{1,0:T(8,128)(2,1)} %get-tuple-element.511.p0), channel_id=1, source_target_pairs={{0,2},{1,3},{2,0},{3,1},{4,6},{5,7},{6,4},{7,5},{8,10},{9,11},{10,... | collective-permute-start | bytes 1585160 | tf_op jit(solution)/shard_map/ppermute | solution.py:997
  483.7 19.1 %collective-permute-start.52 = (bf16[344,768]{1,0:T(8,128)(2,1)}, bf16[344,768]{1,0:T(8,128)(2,1)S(1)}, u32[]{:S(2)}, u32[]{:S(2)}) collective-permute-start(bf16[344,768]{1,0:T(8,128)(2,1)} %get-tuple-element.571.p0), channel_id=1, source_target_pairs={{0,2},{1,3},{2,0},{3,1},{4,6},{5,7},{6,4},{7,5},{8,10},{9,11},{10,... | collective-permute-start | bytes 1585160 | tf_op jit(solution)/shard_map/ppermute | solution.py:997
  593.6 19.5 %collective-permute-start.68 = (bf16[344,768]{1,0:T(8,128)(2,1)}, bf16[344,768]{1,0:T(8,128)(2,1)S(1)}, u32[]{:S(2)}, u32[]{:S(2)}) collective-permute-start(bf16[344,768]{1,0:T(8,128)(2,1)} %get-tuple-element.625.p0), channel_id=1, source_target_pairs={{0,1},{1,0},{2,3},{3,2},{4,5},{5,4},{6,7},{7,6},{8,9},{9,8},{10,11... | collective-permute-start | bytes 1585160 | tf_op jit(solution)/shard_map/ppermute | solution.py:1001
  594.1 18.8 %collective-permute-start.64 = (bf16[344,768]{1,0:T(8,128)(2,1)}, bf16[344,768]{1,0:T(8,128)(2,1)S(1)}, u32[]{:S(2)}, u32[]{:S(2)}) collective-permute-start(bf16[344,768]{1,0:T(8,128)(2,1)} %get-tuple-element.625.p0), channel_id=1, source_target_pairs={{0,2},{1,3},{2,0},{3,1},{4,6},{5,7},{6,4},{7,5},{8,10},{9,11},{10,... | collective-permute-start | bytes 1585160 | tf_op jit(solution)/shard_map/ppermute | solution.py:997
  646.1 22.1 %collective-permute-start.70 = (bf16[4,384,768]{2,1,0:T(8,128)(2,1)}, bf16[4,384,768]{2,1,0:T(8,128)(2,1)S(1)}, u32[]{:S(2)}, u32[]{:S(2)}) collective-permute-start(bf16[4,384,768]{2,1,0:T(8,128)(2,1)} %get-tuple-element.655), channel_id=1, source_target_pairs={{0,1},{1,0},{2,3},{3,2},{4,5},{5,4},{6,7},{7,6},{8,9},{9,8},{10,11... | collective-permute-start | bytes 7077896 | tf_op jit(solution)/shard_map/ppermute | solution.py:1001
  659.5 134.3 %reduce-scatter.4.cloned.1.call-start = ((), (), s32[]{:S(2)}) async-start(), calls=%async_computation.3 | async-start | bytes 2457600 | tf_op jit(solution)/shard_map/reduce_scatter | solution.py:1255
  679.1 19.0 %collective-permute-start.71 = (bf16[2,344,768]{2,1,0:T(8,128)(2,1)}, bf16[2,344,768]{2,1,0:T(8,128)(2,1)S(1)}, u32[]{:S(2)}, u32[]{:S(2)}) collective-permute-start(bf16[2,344,768]{2,1,0:T(8,128)(2,1)} %get-tuple-element.673), channel_id=1, source_target_pairs={{0,1},{1,0},{2,3},{3,2},{4,5},{5,4},{6,7},{7,6},{8,9},{9,8},{10,11... | collective-permute-start | bytes 3170312 | tf_op jit(solution)/shard_map/ppermute | solution.py:1001
  680.3 44.5 %collective-permute-start.78 = (bf16[4,96,768]{2,1,0:T(8,128)(2,1)}, bf16[4,96,768]{2,1,0:T(8,128)(2,1)}, u32[]{:S(2)}, u32[]{:S(2)}) collective-permute-start(bf16[4,96,768]{2,1,0:T(8,128)(2,1)} %get-tuple-element.741), channel_id=1, source_target_pairs={{0,2},{1,3},{2,0},{3,1},{4,6},{5,7},{6,4},{7,5},{8,10},{9,11},{10,... | collective-permute-start | bytes 1769480 | tf_op jit(solution)/shard_map/ppermute | solution.py:997
  681.5 29.5 %collective-permute-start.77 = (bf16[4,96,768]{2,1,0:T(8,128)(2,1)}, bf16[4,96,768]{2,1,0:T(8,128)(2,1)}, u32[]{:S(2)}, u32[]{:S(2)}) collective-permute-start(bf16[4,96,768]{2,1,0:T(8,128)(2,1)} %get-tuple-element.742), channel_id=1, source_target_pairs={{0,2},{1,3},{2,0},{3,1},{4,6},{5,7},{6,4},{7,5},{8,10},{9,11},{10,... | collective-permute-start | bytes 1769480 | tf_op jit(solution)/shard_map/ppermute | solution.py:997
  697.9 100.1 %reduce-scatter.8.cloned.1.call-start = ((), (), s32[]{:S(2)}) async-start(), calls=%async_computation.5 | async-start | bytes 2949120 | tf_op jit(solution)/shard_map/reduce_scatter | solution.py:1255
  746.0 24.2 %collective-permute-start.72 = (bf16[344,768]{1,0:T(8,128)(2,1)S(1)}, bf16[344,768]{1,0:T(8,128)(2,1)S(1)}, u32[]{:S(2)}, u32[]{:S(2)}) collective-permute-start(bf16[344,768]{1,0:T(8,128)(2,1)S(1)} %fusion.1), channel_id=1, source_target_pairs={{0,2},{1,3},{2,0},{3,1},{4,6},{5,7},{6,4},{7,5},{8,10},{9,11},{10,... | collective-permute-start | bytes 1585160 | tf_op jit(solution)/shard_map/ppermute | solution.py:997
  (165 other events, 1187.7 us)
Sparse Core Ops, SparseCore 0:
  659.6 39.8 reduce-scatter.5
  701.9 40.5 reduce-scatter.3
  744.9 49.3 reduce-scatter.7

commit v5 on v4

--- a/solution.py
+++ b/solution.py
@@ -1103,7 +1103,10 @@
         pieces = gathered(h)
         if up is None:
             up_own, down_own, _ = lax.optimization_barrier((up_proj[0], down_proj[0], pieces[1]))
-            up, down = gathered(up_own), gathered(down_own)
+            up = gathered(up_own)
+            part = down_own.shape[0] // groups
+            own_part = lax.dynamic_slice_in_dim(down_own, lax.axis_index("dp") * part, part, axis=0)
+            part = over_y(own_part)
         second = t % SKEW > 0
         if second:
             pieces = hold(pieces, ahead["own"])
@@ -1120,6 +1123,9 @@
         state[t] = [x, qkvi, oti, tti, qkvt, ott, ttt]
         other, across = for_y(r1, r23)
         ahead.update(own=r0, across=across)
+        if down is None:
+            part = lax.all_gather(hold((part,), r0)[0], "dp", axis=0, tiled=True)
+            down = gathered(down_own, part)
         return (r0, other, over_y(across))
 
     def feed(t, parts):

time: 812 us -> 808 us (level)
    unnamed x207 -> x203, local copies, waits for them, and re-layouts: 27.5 us -> 27.3 us
  transfers between devices with their start and end apart: 87 -> 88, of which waited for: 42 -> 44; matrix products, arithmetic and copies ran while one was open for 4% -> 4% of each run, Pallas kernels for 46% -> 46%
where the time goes in v5:
time: 808 us; the launch traced here: 804 us
  Pallas kernels  488 us (60%)
  waiting for transfers between devices  169 us (21%)
  starting transfers between devices  65.4 us (8%)
  local copies, waits for them, and re-layouts  39.9 us (5%)
  other arithmetic  26.5 us (3%)
  between operations  15.8 us (2%)
    pallas_call x48, Pallas kernels, run(): pl.pallas_call(kernel, out_shape=tuple(outs), in_specs=[SMEM_SPEC] * lead...  435 us
    ppermute x30, waiting for transfers between devices, over_y(): return lax.ppermute(array, 'mp', [(m, m ^ 2) for m in range(4)])  125 us
    ppermute x30, starting transfers between devices, over_y(): return lax.ppermute(array, 'mp', [(m, m ^ 2) for m in range(4)])  35.1 us
    ppermute x42, waiting for transfers between devices, over_core(): return lax.ppermute(array, 'mp', [(m, m ^ 1) for m in range(4)])  29.1 us
    pallas_call x2, Pallas kernels, ff_weights(): pl.pallas_call(ff_weights_kernel, grid=(2,), out_shape=(shape_of(part, BF...  27.7 us
    unnamed x203, local copies, waits for them, and re-layouts  27.3 us
    pallas_call x2, Pallas kernels, attention_weights(): pl.pallas_call(attention_weights_kernel, grid=(slots - 1,), out_shape=sha...  24.6 us
    ppermute x8, starting transfers between devices, shifted(): lax.ppermute(array, 'section', [(i, i + by) for i in range(length) if 0 <...  18.7 us
  transfers between devices with their start and end apart: 88, of which 44 were waited for; matrix products, arithmetic and copies ran while one was open for 4% of the time, Pallas kernels for 46%

profile of v5, /device:TPU:0, one launch (start us, length us, event | category | flops | bytes accessed | tf_op | source)
XLA Modules:
  0.0 804.0 jit_solution(2920326114762558608)
XLA Ops:
  45.9 11.8 %text_forward.6 = (bf16[344,768]{1,0:T(8,128)(2,1)}, bf16[344,768]{1,0:T(8,128)(2,1)}, bf16[2,344,768]{2,1,0:T(8,128)(2,1)}, bf16[4,800,192]{2,1,0:T(8,128)(2,1)...) custom-call(s32[1]{0:T(128)} %constant.74.clone.1.tick, ...), custom_call_target="tpu_custom_call", output_to_operand_aliasing={{0}: (9, {}), {1}: (10, {}), {2}: (11, {})} | custom-call | flops 4010803200 | bytes 7299072 | tf_op jit(solution)/shard_map/text_forward/pallas_call | solution.py:119
  70.2 11.6 %text_forward.7 = (bf16[344,768]{1,0:T(8,128)(2,1)}, bf16[344,768]{1,0:T(8,128)(2,1)}, bf16[2,344,768]{2,1,0:T(8,128)(2,1)}, bf16[4,800,192]{2,1,0:T(8,128)(2,1)...) custom-call(s32[1]{0:T(128)} %constant.72.clone.1.tick, ...), custom_call_target="tpu_custom_call", output_to_operand_aliasing={{0}: (9, {}), {1}: (10, {}), {2}: (11, {}), {6}: (12, {}), ... | custom-call | flops 4010803200 | bytes 7299072 | tf_op jit(solution)/shard_map/text_forward/pallas_call | solution.py:119
  94.1 11.5 %collective-permute-done.4.c = bf16[344,768]{1,0:T(8,128)(2,1)S(1)} collective-permute-done((bf16[344,768]{1,0:T(8,128)(2,1)S(1)}, bf16[344,768]{1,0:T(8,128)(2,1)S(1)}, u32[]{:S(2)}, u32[]{:S(2)}) %collective-permute-start.4) | collective-permute-done | bytes 528416 | tf_op jit(solution)/shard_map/ppermute | solution.py:997
  106.8 11.4 %ff_forward.6 = (f32[344,768]{1,0:T(8,128)}, bf16[344,3072]{1,0:T(8,128)(2,1)}, bf16[344,768]{1,0:T(8,128)(2,1)}, bf16[1720,768]{1,0:T(8,128)(2,1)}, bf16[1720,3...) custom-call(s32[1]{0:T(128)} %constant.74.clone.1.tick, s32[54]{0:T(128)} %concatenate.15.info, ...), custom_call_target="tpu_custom_call" | custom-call | flops 3246391296 | bytes 17891328 | tf_op jit(solution)/shard_map/ff_forward/pallas_call | solution.py:119
  121.6 11.3 %ff_forward.7 = (f32[344,768]{1,0:T(8,128)}, bf16[344,3072]{1,0:T(8,128)(2,1)}, bf16[344,768]{1,0:T(8,128)(2,1)}, bf16[1720,768]{1,0:T(8,128)(2,1)}, bf16[1720,3...) custom-call(s32[1]{0:T(128)} %constant.72.clone.1.tick, ...), custom_call_target="tpu_custom_call", output_to_operand_aliasing={{3}: (16, {}), {4}: (17, {}), {5}: (18, {}), {6}: (19, {})} | custom-call | flops 3246391296 | bytes 17891328 | tf_op jit(solution)/shard_map/ff_forward/pallas_call | solution.py:119
  163.5 11.8 %text_forward.8 = (bf16[344,768]{1,0:T(8,128)(2,1)}, bf16[344,768]{1,0:T(8,128)(2,1)}, bf16[2,344,768]{2,1,0:T(8,128)(2,1)}, bf16[4,800,192]{2,1,0:T(8,128)(2,1)...) custom-call(s32[1]{0:T(128)} %constant.83.clone.1.tick, ...), custom_call_target="tpu_custom_call", output_to_operand_aliasing={{0}: (9, {}), {1}: (10, {}), {2}: (11, {}), {6}: (12, {}), ... | custom-call | flops 4010803200 | bytes 7299072 | tf_op jit(solution)/shard_map/text_forward/pallas_call | solution.py:119
  187.8 11.6 %text_forward.9 = (bf16[344,768]{1,0:T(8,128)(2,1)}, bf16[344,768]{1,0:T(8,128)(2,1)}, bf16[2,344,768]{2,1,0:T(8,128)(2,1)}, bf16[4,800,192]{2,1,0:T(8,128)(2,1)...) custom-call(s32[1]{0:T(128)} %constant.71.clone.1.tick, ...), custom_call_target="tpu_custom_call", output_to_operand_aliasing={{0}: (9, {}), {1}: (10, {}), {2}: (11, {}), {6}: (12, {}), ... | custom-call | flops 4010803200 | bytes 7299072 | tf_op jit(solution)/shard_map/text_forward/pallas_call | solution.py:119
  215.3 11.5 %ff_forward.8 = (f32[344,768]{1,0:T(8,128)}, bf16[344,3072]{1,0:T(8,128)(2,1)}, bf16[344,768]{1,0:T(8,128)(2,1)}, bf16[1720,768]{1,0:T(8,128)(2,1)}, bf16[1720,3...) custom-call(s32[1]{0:T(128)} %constant.83.clone.1.tick, ...), custom_call_target="tpu_custom_call", output_to_operand_aliasing={{3}: (16, {}), {4}: (17, {}), {5}: (18, {}), {6}: (19, {})} | custom-call | flops 3246391296 | bytes 17891328 | tf_op jit(solution)/shard_map/ff_forward/pallas_call | solution.py:119
  231.9 11.3 %ff_forward.9 = (f32[344,768]{1,0:T(8,128)}, bf16[344,3072]{1,0:T(8,128)(2,1)}, bf16[344,768]{1,0:T(8,128)(2,1)}, bf16[1720,768]{1,0:T(8,128)(2,1)}, bf16[1720,3...) custom-call(s32[1]{0:T(128)} %constant.71.clone.1.tick, ...), custom_call_target="tpu_custom_call", output_to_operand_aliasing={{3}: (16, {}), {4}: (17, {}), {5}: (18, {}), {6}: (19, {})} | custom-call | flops 3246391296 | bytes 17891328 | tf_op jit(solution)/shard_map/ff_forward/pallas_call | solution.py:119
  273.5 11.8 %text_forward.10 = (bf16[344,768]{1,0:T(8,128)(2,1)}, bf16[344,768]{1,0:T(8,128)(2,1)}, bf16[2,344,768]{2,1,0:T(8,128)(2,1)}, bf16[4,800,192]{2,1,0:T(8,128)(2,1...) custom-call(s32[1]{0:T(128)} %constant.84.clone.1.tick, ...), custom_call_target="tpu_custom_call", output_to_operand_aliasing={{0}: (9, {}), {1}: (10, {}), {2}: (11, {}), {6}: (12, {}), ... | custom-call | flops 4010803200 | bytes 7299072 | tf_op jit(solution)/shard_map/text_forward/pallas_call | solution.py:119
  297.8 11.6 %text_forward.11 = (bf16[344,768]{1,0:T(8,128)(2,1)}, bf16[344,768]{1,0:T(8,128)(2,1)}, bf16[2,344,768]{2,1,0:T(8,128)(2,1)}, bf16[4,800,192]{2,1,0:T(8,128)(2,1...) custom-call(s32[1]{0:T(128)} %constant.32.clone.1.tick, ...), custom_call_target="tpu_custom_call", output_to_operand_aliasing={{0}: (9, {}), {1}: (10, {}), {2}: (11, {}), {6}: (12, {}), ... | custom-call | flops 4010803200 | bytes 7299072 | tf_op jit(solution)/shard_map/text_forward/pallas_call | solution.py:119
  374.1 16.6 %text_backward.6 = (bf16[344,768]{1,0:T(8,128)(2,1)}, bf16[344,768]{1,0:T(8,128)(2,1)}, bf16[2,344,768]{2,1,0:T(8,128)(2,1)}, bf16[2,576,192]{2,1,0:T(8,128)(2,1...) custom-call(s32[1]{0:T(128)} %constant.32.clone.1.tick, s32[54]{0:T(128)} %concatenate.15.info, ...), custom_call_target="tpu_custom_call" | custom-call | flops 7903641600 | bytes 8527872 | tf_op jit(solution)/shard_map/text_backward/pallas_call | solution.py:119
  405.9 16.5 %text_backward.7 = (bf16[344,768]{1,0:T(8,128)(2,1)}, bf16[344,768]{1,0:T(8,128)(2,1)}, bf16[2,344,768]{2,1,0:T(8,128)(2,1)}, bf16[2,576,192]{2,1,0:T(8,128)(2,1...) custom-call(s32[1]{0:T(128)} %constant.84.clone.1.tick, ...), custom_call_target="tpu_custom_call", output_to_operand_aliasing={{4}: (12, {}), {5}: (13, {})} | custom-call | flops 7903641600 | bytes 8527872 | tf_op jit(solution)/shard_map/text_backward/pallas_call | solution.py:119
  485.5 16.4 %text_backward.8 = (bf16[344,768]{1,0:T(8,128)(2,1)}, bf16[344,768]{1,0:T(8,128)(2,1)}, bf16[2,344,768]{2,1,0:T(8,128)(2,1)}, bf16[2,576,192]{2,1,0:T(8,128)(2,1...) custom-call(s32[1]{0:T(128)} %constant.71.clone.1.tick, ...), custom_call_target="tpu_custom_call", output_to_operand_aliasing={{4}: (12, {}), {5}: (13, {})} | custom-call | flops 7903641600 | bytes 8527872 | tf_op jit(solution)/shard_map/text_backward/pallas_call | solution.py:119
  517.3 16.7 %text_backward.9 = (bf16[344,768]{1,0:T(8,128)(2,1)}, bf16[344,768]{1,0:T(8,128)(2,1)}, bf16[2,344,768]{2,1,0:T(8,128)(2,1)}, bf16[2,576,192]{2,1,0:T(8,128)(2,1...) custom-call(s32[1]{0:T(128)} %constant.83.clone.1.tick, ...), custom_call_target="tpu_custom_call", output_to_operand_aliasing={{4}: (12, {}), {5}: (13, {})} | custom-call | flops 7903641600 | bytes 8527872 | tf_op jit(solution)/shard_map/text_backward/pallas_call | solution.py:119
  595.4 16.6 %text_backward.10 = (bf16[344,768]{1,0:T(8,128)(2,1)}, bf16[344,768]{1,0:T(8,128)(2,1)}, bf16[2,344,768]{2,1,0:T(8,128)(2,1)}, bf16[2,576,192]{2,1,0:T(8,128)(2,...) custom-call(s32[1]{0:T(128)} %constant.72.clone.1.tick, ...), custom_call_target="tpu_custom_call", output_to_operand_aliasing={{4}: (12, {}), {5}: (13, {})} | custom-call | flops 7903641600 | bytes 8527872 | tf_op jit(solution)/shard_map/text_backward/pallas_call | solution.py:119
  614.8 16.4 %text_backward.11 = (bf16[344,768]{1,0:T(8,128)(2,1)}, bf16[344,768]{1,0:T(8,128)(2,1)}, bf16[2,344,768]{2,1,0:T(8,128)(2,1)}, bf16[2,576,192]{2,1,0:T(8,128)(2,...) custom-call(s32[1]{0:T(128)} %constant.74.clone.1.tick, ...), custom_call_target="tpu_custom_call", output_to_operand_aliasing={{4}: (12, {}), {5}: (13, {})} | custom-call | flops 7903641600 | bytes 8527872 | tf_op jit(solution)/shard_map/text_backward/pallas_call | solution.py:119
  631.2 13.8 %ff_weights.2 = (bf16[4,384,768]{2,1,0:T(8,128)(2,1)}, bf16[4,384,768]{2,1,0:T(8,128)(2,1)}) custom-call(bf16[1720,768]{1,0:T(8,128)(2,1)} %get-tuple-element.651.h2, bf16[1720,768]{1,0:T(8,128)(2,1)} %get-tuple-element.654.dm, bf16[1720,3072]{1,0:T(8,128)(2,1)} %get-tuple-element.690.du, bf16[1720,3072]{1,0:T(8,128)(2,1)} %get-tuple-element.656.g), custom_call_target="tpu_custom_call" | custom-call | flops 6492782592 | bytes 17399808 | tf_op jit(solution)/shard_map/ff_weights/pallas_call | solution.py:898
  645.2 13.1 %text_weights.1 = bf16[4,288,768]{2,1,0:T(8,128)(2,1)} custom-call(bf16[5,800,768]{2,1,0:T(8,128)(2,1)} %get-tuple-element.658.h, bf16[5,800,768]{2,1,0:T(8,128)(2,1)} %get-tuple-element.659.dd, bf16[5,800,384]{2,1,0:T(8,128)(2,1)} %get-tuple-element.660.o, bf16[5,800,768]{2,1,0:T(8,128)(2,1)} %get-tuple-element.661.da), custom_call_target="tpu_custom_call" | custom-call | flops 7077888000 | bytes 21504000 | tf_op jit(solution)/shard_map/text_weights/pallas_call | solution.py:655
  685.3 11.4 %image_weights.1 = bf16[4,240,960]{2,1,0:T(8,128)(2,1)} custom-call(bf16[5,576,768]{2,1,0:T(8,128)(2,1)} %get-tuple-element.686.h, bf16[5,576,960]{2,1,0:T(8,128)(2,1)} %get-tuple-element.687.dd, bf16[5,576,192]{2,1,0:T(8,128)(2,1)} %get-tuple-element.688.o, bf16[5,576,768]{2,1,0:T(8,128)(2,1)} %get-tuple-element.689.da), custom_call_target="tpu_custom_call" | custom-call | flops 5096079360 | bytes 15482880 | tf_op jit(solution)/shard_map/image_weights/pallas_call | solution.py:655
  698.0 11.9 %collective-permute-done.77 = bf16[4,96,768]{2,1,0:T(8,128)(2,1)} collective-permute-done((bf16[4,96,768]{2,1,0:T(8,128)(2,1)}, bf16[4,96,768]{2,1,0:T(8,128)(2,1)}, u32[]{:S(2)}, u32[]{:S(2)}) %collective-permute-start.77) | collective-permute-done | bytes 589856 | tf_op jit(solution)/shard_map/ppermute | solution.py:997
  709.9 13.9 %ff_weights.3 = (bf16[4,384,768]{2,1,0:T(8,128)(2,1)}, bf16[4,384,768]{2,1,0:T(8,128)(2,1)}) custom-call(bf16[1720,768]{1,0:T(8,128)(2,1)} %get-tuple-element.651.h2, bf16[1720,768]{1,0:T(8,128)(2,1)} %get-tuple-element.654.dm, bf16[1720,3072]{1,0:T(8,128)(2,1)} %get-tuple-element.690.du, bf16[1720,3072]{1,0:T(8,128)(2,1)} %get-tuple-element.656.g), custom_call_target="tpu_custom_call" | custom-call | flops 6492782592 | bytes 17399808 | tf_op jit(solution)/shard_map/ff_weights/pallas_call | solution.py:898
  724.7 14.8 %collective-permute-done.73 = bf16[4,96,768]{2,1,0:T(8,128)(2,1)S(1)} collective-permute-done((bf16[4,96,768]{2,1,0:T(8,128)(2,1)S(1)}, bf16[4,96,768]{2,1,0:T(8,128)(2,1)S(1)}, u32[]{:S(2)}, u32[]{:S(2)}) %collective-permute-start.73) | collective-permute-done | bytes 589856 | tf_op jit(solution)/shard_map/ppermute | solution.py:997
  746.2 12.8 %collective-permute-done.75.c = bf16[344,768]{1,0:T(8,128)(2,1)S(1)} collective-permute-done((bf16[344,768]{1,0:T(8,128)(2,1)S(1)}, bf16[344,768]{1,0:T(8,128)(2,1)S(1)}, u32[]{:S(2)}, u32[]{:S(2)}) %collective-permute-start.75) | collective-permute-done | bytes 528416 | tf_op jit(solution)/shard_map/ppermute | solution.py:997
  (465 shorter events, 470.1 us)
Async XLA Ops:
  7.2 82.1 %all-gather.2.cloned.1.call-start = ((), (), s32[]{:S(2)}) async-start(), calls=%async_computation.3 | async-start | bytes 1474560 | tf_op jit(solution)/shard_map/all_gather | solution.py:1127
  16.4 22.7 %collective-permute-start.1 = (bf16[344,768]{1,0:T(8,128)(2,1)}, bf16[344,768]{1,0:T(8,128)(2,1)}, u32[]{:S(2)}, u32[]{:S(2)}) collective-permute-start(bf16[344,768]{1,0:T(8,128)(2,1)} %get-tuple-element.364.p0), channel_id=1, source_target_pairs={{0,1},{1,0},{2,3},{3,2},{4,5},{5,4},{6,7},{7,6},{8,9},{9,8},{10,11... | collective-permute-start | bytes 1585160 | tf_op jit(solution)/shard_map/ppermute | solution.py:1001
  19.6 39.5 %collective-permute-start.11 = (bf16[344,768]{1,0:T(8,128)(2,1)}, bf16[344,768]{1,0:T(8,128)(2,1)}, u32[]{:S(2)}, u32[]{:S(2)}) collective-permute-start(bf16[344,768]{1,0:T(8,128)(2,1)} %get-tuple-element.381.p0), channel_id=1, source_target_pairs={{0,2},{1,3},{2,0},{3,1},{4,6},{5,7},{6,4},{7,5},{8,10},{9,11},{10,... | collective-permute-start | bytes 1585160 | tf_op jit(solution)/shard_map/ppermute | solution.py:997
  37.0 20.7 %collective-permute-start.8 = (bf16[192,768]{1,0:T(8,128)(2,1)S(1)}, bf16[192,768]{1,0:T(8,128)(2,1)S(1)}, u32[]{:S(2)}, u32[]{:S(2)}) collective-permute-start(bf16[192,768]{1,0:T(8,128)(2,1)S(1)} %constant_dynamic-slice_fusion), channel_id=1, source_target_pairs={{0,2},{1,3},{2,0},{3,1},{4,6},{5,7},{6,4},{7,5},{8,10},{9,11},{10,... | collective-permute-start | bytes 884744 | tf_op jit(solution)/shard_map/ppermute | solution.py:997
  58.4 718.8 %reduce-scatter.6.cloned.1.call-start = ((), (), s32[]{:S(2)}) async-start(), calls=%async_computation.5 | async-start | bytes 2211840 | tf_op jit(solution)/shard_map/reduce_scatter | solution.py:1261
  59.4 28.1 %collective-permute-start.5 = (bf16[768,768]{1,0:T(8,128)(2,1)S(1)}, bf16[768,768]{1,0:T(8,128)(2,1)S(1)}, u32[]{:S(2)}, u32[]{:S(2)}) collective-permute-start(bf16[768,768]{1,0:T(8,128)(2,1)S(1)} %bitcast.122), channel_id=1, source_target_pairs={{0,2},{1,3},{2,0},{3,1},{4,6},{5,7},{6,4},{7,5},{8,10},{9,11},{10,... | collective-permute-start | bytes 3538952 | tf_op jit(solution)/shard_map/ppermute | solution.py:997
  59.6 28.0 %collective-permute-start.3 = (bf16[2,344,768]{2,1,0:T(8,128)(2,1)}, bf16[2,344,768]{2,1,0:T(8,128)(2,1)}, u32[]{:S(2)}, u32[]{:S(2)}) collective-permute-start(bf16[2,344,768]{2,1,0:T(8,128)(2,1)} %get-tuple-element.373), channel_id=1, source_target_pairs={{0,1},{1,0},{2,3},{3,2},{4,5},{5,4},{6,7},{7,6},{8,9},{9,8},{10,11... | collective-permute-start | bytes 3170312 | tf_op jit(solution)/shard_map/ppermute | solution.py:1001
  87.5 18.0 %collective-permute-start.7 = (bf16[768,768]{1,0:T(8,128)(2,1)S(1)}, bf16[768,768]{1,0:T(8,128)(2,1)}, u32[]{:S(2)}, u32[]{:S(2)}) collective-permute-start(bf16[768,768]{1,0:T(8,128)(2,1)S(1)} %collective-permute-done.5.u1), channel_id=1, source_target_pairs={{0,1},{1,0},{2,3},{3,2},{4,5},{5,4},{6,7},{7,6},{8,9},{9,8},{10,11... | collective-permute-start | bytes 3538952 | tf_op jit(solution)/shard_map/ppermute | solution.py:1001
  93.4 27.4 %collective-permute-start.15 = (bf16[344,768]{1,0:T(8,128)(2,1)S(1)}, bf16[344,768]{1,0:T(8,128)(2,1)S(1)}, u32[]{:S(2)}, u32[]{:S(2)}) collective-permute-start(bf16[344,768]{1,0:T(8,128)(2,1)S(1)} %fusion.10), channel_id=1, source_target_pairs={{0,2},{1,3},{2,0},{3,1},{4,6},{5,7},{6,4},{7,5},{8,10},{9,11},{10,... | collective-permute-start | bytes 1585160 | tf_op jit(solution)/shard_map/ppermute | solution.py:997
  155.0 20.8 %collective-permute-start.23 = (bf16[344,768]{1,0:T(8,128)(2,1)}, bf16[344,768]{1,0:T(8,128)(2,1)S(1)}, u32[]{:S(2)}, u32[]{:S(2)}) collective-permute-start(bf16[344,768]{1,0:T(8,128)(2,1)} %get-tuple-element.424.p0), channel_id=1, source_target_pairs={{0,2},{1,3},{2,0},{3,1},{4,6},{5,7},{6,4},{7,5},{8,10},{9,11},{10,... | collective-permute-start | bytes 1585160 | tf_op jit(solution)/shard_map/ppermute | solution.py:997
  203.9 27.2 %collective-permute-start.27 = (bf16[344,768]{1,0:T(8,128)(2,1)S(1)}, bf16[344,768]{1,0:T(8,128)(2,1)S(1)}, u32[]{:S(2)}, u32[]{:S(2)}) collective-permute-start(bf16[344,768]{1,0:T(8,128)(2,1)S(1)} %fusion.8), channel_id=1, source_target_pairs={{0,2},{1,3},{2,0},{3,1},{4,6},{5,7},{6,4},{7,5},{8,10},{9,11},{10,... | collective-permute-start | bytes 1585160 | tf_op jit(solution)/shard_map/ppermute | solution.py:997
  264.9 21.0 %collective-permute-start.30 = (bf16[344,768]{1,0:T(8,128)(2,1)}, bf16[344,768]{1,0:T(8,128)(2,1)S(1)}, u32[]{:S(2)}, u32[]{:S(2)}) collective-permute-start(bf16[344,768]{1,0:T(8,128)(2,1)} %get-tuple-element.461.p0), channel_id=1, source_target_pairs={{0,2},{1,3},{2,0},{3,1},{4,6},{5,7},{6,4},{7,5},{8,10},{9,11},{10,... | collective-permute-start | bytes 1585160 | tf_op jit(solution)/shard_map/ppermute | solution.py:997
  314.0 22.0 %collective-permute-start.38 = (bf16[344,768]{1,0:T(8,128)(2,1)S(1)}, bf16[344,768]{1,0:T(8,128)(2,1)S(1)}, u32[]{:S(2)}, u32[]{:S(2)}) collective-permute-start(bf16[344,768]{1,0:T(8,128)(2,1)S(1)} %fusion.6), channel_id=1, source_target_pairs={{0,2},{1,3},{2,0},{3,1},{4,6},{5,7},{6,4},{7,5},{8,10},{9,11},{10,... | collective-permute-start | bytes 1585160 | tf_op jit(solution)/shard_map/ppermute | solution.py:997
  371.4 19.3 %collective-permute-start.40 = (bf16[344,768]{1,0:T(8,128)(2,1)}, bf16[344,768]{1,0:T(8,128)(2,1)S(1)}, u32[]{:S(2)}, u32[]{:S(2)}) collective-permute-start(bf16[344,768]{1,0:T(8,128)(2,1)} %get-tuple-element.513.p0), channel_id=1, source_target_pairs={{0,2},{1,3},{2,0},{3,1},{4,6},{5,7},{6,4},{7,5},{8,10},{9,11},{10,... | collective-permute-start | bytes 1585160 | tf_op jit(solution)/shard_map/ppermute | solution.py:997
  482.8 19.1 %collective-permute-start.52 = (bf16[344,768]{1,0:T(8,128)(2,1)}, bf16[344,768]{1,0:T(8,128)(2,1)S(1)}, u32[]{:S(2)}, u32[]{:S(2)}) collective-permute-start(bf16[344,768]{1,0:T(8,128)(2,1)} %get-tuple-element.573.p0), channel_id=1, source_target_pairs={{0,2},{1,3},{2,0},{3,1},{4,6},{5,7},{6,4},{7,5},{8,10},{9,11},{10,... | collective-permute-start | bytes 1585160 | tf_op jit(solution)/shard_map/ppermute | solution.py:997
  592.7 19.5 %collective-permute-start.68 = (bf16[344,768]{1,0:T(8,128)(2,1)}, bf16[344,768]{1,0:T(8,128)(2,1)S(1)}, u32[]{:S(2)}, u32[]{:S(2)}) collective-permute-start(bf16[344,768]{1,0:T(8,128)(2,1)} %get-tuple-element.627.p0), channel_id=1, source_target_pairs={{0,1},{1,0},{2,3},{3,2},{4,5},{5,4},{6,7},{7,6},{8,9},{9,8},{10,11... | collective-permute-start | bytes 1585160 | tf_op jit(solution)/shard_map/ppermute | solution.py:1001
  593.2 18.8 %collective-permute-start.64 = (bf16[344,768]{1,0:T(8,128)(2,1)}, bf16[344,768]{1,0:T(8,128)(2,1)S(1)}, u32[]{:S(2)}, u32[]{:S(2)}) collective-permute-start(bf16[344,768]{1,0:T(8,128)(2,1)} %get-tuple-element.627.p0), channel_id=1, source_target_pairs={{0,2},{1,3},{2,0},{3,1},{4,6},{5,7},{6,4},{7,5},{8,10},{9,11},{10,... | collective-permute-start | bytes 1585160 | tf_op jit(solution)/shard_map/ppermute | solution.py:997
  645.1 22.2 %collective-permute-start.70 = (bf16[4,384,768]{2,1,0:T(8,128)(2,1)}, bf16[4,384,768]{2,1,0:T(8,128)(2,1)S(1)}, u32[]{:S(2)}, u32[]{:S(2)}) collective-permute-start(bf16[4,384,768]{2,1,0:T(8,128)(2,1)} %get-tuple-element.657), channel_id=1, source_target_pairs={{0,1},{1,0},{2,3},{3,2},{4,5},{5,4},{6,7},{7,6},{8,9},{9,8},{10,11... | collective-permute-start | bytes 7077896 | tf_op jit(solution)/shard_map/ppermute | solution.py:1001
  658.4 132.3 %reduce-scatter.4.cloned.1.call-start = ((), (), s32[]{:S(2)}) async-start(), calls=%async_computation.4 | async-start | bytes 2457600 | tf_op jit(solution)/shard_map/reduce_scatter | solution.py:1261
  678.0 19.0 %collective-permute-start.71 = (bf16[2,344,768]{2,1,0:T(8,128)(2,1)}, bf16[2,344,768]{2,1,0:T(8,128)(2,1)S(1)}, u32[]{:S(2)}, u32[]{:S(2)}) collective-permute-start(bf16[2,344,768]{2,1,0:T(8,128)(2,1)} %get-tuple-element.675), channel_id=1, source_target_pairs={{0,1},{1,0},{2,3},{3,2},{4,5},{5,4},{6,7},{7,6},{8,9},{9,8},{10,11... | collective-permute-start | bytes 3170312 | tf_op jit(solution)/shard_map/ppermute | solution.py:1001
  679.2 44.5 %collective-permute-start.78 = (bf16[4,96,768]{2,1,0:T(8,128)(2,1)}, bf16[4,96,768]{2,1,0:T(8,128)(2,1)}, u32[]{:S(2)}, u32[]{:S(2)}) collective-permute-start(bf16[4,96,768]{2,1,0:T(8,128)(2,1)} %get-tuple-element.743), channel_id=1, source_target_pairs={{0,2},{1,3},{2,0},{3,1},{4,6},{5,7},{6,4},{7,5},{8,10},{9,11},{10,... | collective-permute-start | bytes 1769480 | tf_op jit(solution)/shard_map/ppermute | solution.py:997
  680.4 29.5 %collective-permute-start.77 = (bf16[4,96,768]{2,1,0:T(8,128)(2,1)}, bf16[4,96,768]{2,1,0:T(8,128)(2,1)}, u32[]{:S(2)}, u32[]{:S(2)}) collective-permute-start(bf16[4,96,768]{2,1,0:T(8,128)(2,1)} %get-tuple-element.744), channel_id=1, source_target_pairs={{0,2},{1,3},{2,0},{3,1},{4,6},{5,7},{6,4},{7,5},{8,10},{9,11},{10,... | collective-permute-start | bytes 1769480 | tf_op jit(solution)/shard_map/ppermute | solution.py:997
  696.8 98.1 %reduce-scatter.8.cloned.1.call-start = ((), (), s32[]{:S(2)}) async-start(), calls=%async_computation.6 | async-start | bytes 2949120 | tf_op jit(solution)/shard_map/reduce_scatter | solution.py:1261
  744.9 24.0 %collective-permute-start.72 = (bf16[344,768]{1,0:T(8,128)(2,1)S(1)}, bf16[344,768]{1,0:T(8,128)(2,1)S(1)}, u32[]{:S(2)}, u32[]{:S(2)}) collective-permute-start(bf16[344,768]{1,0:T(8,128)(2,1)S(1)} %fusion.1), channel_id=1, source_target_pairs={{0,2},{1,3},{2,0},{3,1},{4,6},{5,7},{6,4},{7,5},{8,10},{9,11},{10,... | collective-permute-start | bytes 1585160 | tf_op jit(solution)/shard_map/ppermute | solution.py:997
  (164 other events, 1142.4 us)
Sparse Core Ops, SparseCore 0:
  58.5 30.7 all-gather.1
  658.5 37.7 reduce-scatter.5
  698.7 40.5 reduce-scatter.3
  743.2 47.9 reduce-scatter.7

commit v6 on v5

--- a/solution.py
+++ b/solution.py
@@ -22,6 +22,7 @@
 VMEM_MIB = 56
 SKEW = 2
 SELF_BLOCK = 256
+SELF_AHEAD = 512
 CROSS_BLOCK = 512
 CROSS_BACK = 512
 
@@ -417,7 +418,7 @@
     items = [
         (kind, head, start, size)
         for kind in range(2)
-        for start, size in query_blocks(rows, CROSS_BLOCK if kind else SELF_BLOCK)
+        for start, size in query_blocks(rows, CROSS_BLOCK if kind else SELF_AHEAD)
         for head in range(heads)
     ]
 

time: 808 us -> 808 us (level)
  no operation moved by 1% of the time
where the time goes in v6:
time: 808 us; the launch traced here: 803 us
  Pallas kernels  487 us (60%)
  waiting for transfers between devices  169 us (21%)
  starting transfers between devices  65.7 us (8%)
  local copies, waits for them, and re-layouts  39.9 us (5%)
  other arithmetic  26.5 us (3%)
  between operations  15.8 us (2%)
    pallas_call x48, Pallas kernels, run(): pl.pallas_call(kernel, out_shape=tuple(outs), in_specs=[SMEM_SPEC] * lead...  434 us
    ppermute x30, waiting for transfers between devices, over_y(): return lax.ppermute(array, 'mp', [(m, m ^ 2) for m in range(4)])  125 us
    ppermute x30, starting transfers between devices, over_y(): return lax.ppermute(array, 'mp', [(m, m ^ 2) for m in range(4)])  35 us
    ppermute x42, waiting for transfers between devices, over_core(): return lax.ppermute(array, 'mp', [(m, m ^ 1) for m in range(4)])  29.3 us
    pallas_call x2, Pallas kernels, ff_weights(): pl.pallas_call(ff_weights_kernel, grid=(2,), out_shape=(shape_of(part, BF...  27.7 us
    unnamed x203, local copies, waits for them, and re-layouts  27.3 us
    pallas_call x2, Pallas kernels, attention_weights(): pl.pallas_call(attention_weights_kernel, grid=(slots - 1,), out_shape=sha...  24.6 us
    ppermute x8, starting transfers between devices, shifted(): lax.ppermute(array, 'section', [(i, i + by) for i in range(length) if 0 <...  19.2 us
  transfers between devices with their start and end apart: 88, of which 44 were waited for; matrix products, arithmetic and copies ran while one was open for 4% of the time, Pallas kernels for 46%

profile of v6, /device:TPU:0, one launch (start us, length us, event | category | flops | bytes accessed | tf_op | source)
XLA Modules:
  0.0 803.2 jit_solution(13921562761340616221)
XLA Ops:
  45.9 11.6 %text_forward.6 = (bf16[344,768]{1,0:T(8,128)(2,1)}, bf16[344,768]{1,0:T(8,128)(2,1)}, bf16[2,344,768]{2,1,0:T(8,128)(2,1)}, bf16[4,800,192]{2,1,0:T(8,128)(2,1)...) custom-call(s32[1]{0:T(128)} %constant.74.clone.1.tick, ...), custom_call_target="tpu_custom_call", output_to_operand_aliasing={{0}: (9, {}), {1}: (10, {}), {2}: (11, {})} | custom-call | flops 4010803200 | bytes 7299072 | tf_op jit(solution)/shard_map/text_forward/pallas_call | solution.py:120
  70.0 11.5 %text_forward.7 = (bf16[344,768]{1,0:T(8,128)(2,1)}, bf16[344,768]{1,0:T(8,128)(2,1)}, bf16[2,344,768]{2,1,0:T(8,128)(2,1)}, bf16[4,800,192]{2,1,0:T(8,128)(2,1)...) custom-call(s32[1]{0:T(128)} %constant.72.clone.1.tick, ...), custom_call_target="tpu_custom_call", output_to_operand_aliasing={{0}: (9, {}), {1}: (10, {}), {2}: (11, {}), {6}: (12, {}), ... | custom-call | flops 4010803200 | bytes 7299072 | tf_op jit(solution)/shard_map/text_forward/pallas_call | solution.py:120
  93.9 11.5 %collective-permute-done.4.c = bf16[344,768]{1,0:T(8,128)(2,1)S(1)} collective-permute-done((bf16[344,768]{1,0:T(8,128)(2,1)S(1)}, bf16[344,768]{1,0:T(8,128)(2,1)S(1)}, u32[]{:S(2)}, u32[]{:S(2)}) %collective-permute-start.4) | collective-permute-done | bytes 528416 | tf_op jit(solution)/shard_map/ppermute | solution.py:998
  106.6 11.4 %ff_forward.6 = (f32[344,768]{1,0:T(8,128)}, bf16[344,3072]{1,0:T(8,128)(2,1)}, bf16[344,768]{1,0:T(8,128)(2,1)}, bf16[1720,768]{1,0:T(8,128)(2,1)}, bf16[1720,3...) custom-call(s32[1]{0:T(128)} %constant.74.clone.1.tick, s32[54]{0:T(128)} %concatenate.15.info, ...), custom_call_target="tpu_custom_call" | custom-call | flops 3246391296 | bytes 17891328 | tf_op jit(solution)/shard_map/ff_forward/pallas_call | solution.py:120
  121.5 11.3 %ff_forward.7 = (f32[344,768]{1,0:T(8,128)}, bf16[344,3072]{1,0:T(8,128)(2,1)}, bf16[344,768]{1,0:T(8,128)(2,1)}, bf16[1720,768]{1,0:T(8,128)(2,1)}, bf16[1720,3...) custom-call(s32[1]{0:T(128)} %constant.72.clone.1.tick, ...), custom_call_target="tpu_custom_call", output_to_operand_aliasing={{3}: (16, {}), {4}: (17, {}), {5}: (18, {}), {6}: (19, {})} | custom-call | flops 3246391296 | bytes 17891328 | tf_op jit(solution)/shard_map/ff_forward/pallas_call | solution.py:120
  163.4 11.6 %text_forward.8 = (bf16[344,768]{1,0:T(8,128)(2,1)}, bf16[344,768]{1,0:T(8,128)(2,1)}, bf16[2,344,768]{2,1,0:T(8,128)(2,1)}, bf16[4,800,192]{2,1,0:T(8,128)(2,1)...) custom-call(s32[1]{0:T(128)} %constant.83.clone.1.tick, ...), custom_call_target="tpu_custom_call", output_to_operand_aliasing={{0}: (9, {}), {1}: (10, {}), {2}: (11, {}), {6}: (12, {}), ... | custom-call | flops 4010803200 | bytes 7299072 | tf_op jit(solution)/shard_map/text_forward/pallas_call | solution.py:120
  187.5 11.5 %text_forward.9 = (bf16[344,768]{1,0:T(8,128)(2,1)}, bf16[344,768]{1,0:T(8,128)(2,1)}, bf16[2,344,768]{2,1,0:T(8,128)(2,1)}, bf16[4,800,192]{2,1,0:T(8,128)(2,1)...) custom-call(s32[1]{0:T(128)} %constant.71.clone.1.tick, ...), custom_call_target="tpu_custom_call", output_to_operand_aliasing={{0}: (9, {}), {1}: (10, {}), {2}: (11, {}), {6}: (12, {}), ... | custom-call | flops 4010803200 | bytes 7299072 | tf_op jit(solution)/shard_map/text_forward/pallas_call | solution.py:120
  214.9 11.5 %ff_forward.8 = (f32[344,768]{1,0:T(8,128)}, bf16[344,3072]{1,0:T(8,128)(2,1)}, bf16[344,768]{1,0:T(8,128)(2,1)}, bf16[1720,768]{1,0:T(8,128)(2,1)}, bf16[1720,3...) custom-call(s32[1]{0:T(128)} %constant.83.clone.1.tick, ...), custom_call_target="tpu_custom_call", output_to_operand_aliasing={{3}: (16, {}), {4}: (17, {}), {5}: (18, {}), {6}: (19, {})} | custom-call | flops 3246391296 | bytes 17891328 | tf_op jit(solution)/shard_map/ff_forward/pallas_call | solution.py:120
  231.5 11.3 %ff_forward.9 = (f32[344,768]{1,0:T(8,128)}, bf16[344,3072]{1,0:T(8,128)(2,1)}, bf16[344,768]{1,0:T(8,128)(2,1)}, bf16[1720,768]{1,0:T(8,128)(2,1)}, bf16[1720,3...) custom-call(s32[1]{0:T(128)} %constant.71.clone.1.tick, ...), custom_call_target="tpu_custom_call", output_to_operand_aliasing={{3}: (16, {}), {4}: (17, {}), {5}: (18, {}), {6}: (19, {})} | custom-call | flops 3246391296 | bytes 17891328 | tf_op jit(solution)/shard_map/ff_forward/pallas_call | solution.py:120
  273.1 11.6 %text_forward.10 = (bf16[344,768]{1,0:T(8,128)(2,1)}, bf16[344,768]{1,0:T(8,128)(2,1)}, bf16[2,344,768]{2,1,0:T(8,128)(2,1)}, bf16[4,800,192]{2,1,0:T(8,128)(2,1...) custom-call(s32[1]{0:T(128)} %constant.84.clone.1.tick, ...), custom_call_target="tpu_custom_call", output_to_operand_aliasing={{0}: (9, {}), {1}: (10, {}), {2}: (11, {}), {6}: (12, {}), ... | custom-call | flops 4010803200 | bytes 7299072 | tf_op jit(solution)/shard_map/text_forward/pallas_call | solution.py:120
  297.3 11.5 %text_forward.11 = (bf16[344,768]{1,0:T(8,128)(2,1)}, bf16[344,768]{1,0:T(8,128)(2,1)}, bf16[2,344,768]{2,1,0:T(8,128)(2,1)}, bf16[4,800,192]{2,1,0:T(8,128)(2,1...) custom-call(s32[1]{0:T(128)} %constant.32.clone.1.tick, ...), custom_call_target="tpu_custom_call", output_to_operand_aliasing={{0}: (9, {}), {1}: (10, {}), {2}: (11, {}), {6}: (12, {}), ... | custom-call | flops 4010803200 | bytes 7299072 | tf_op jit(solution)/shard_map/text_forward/pallas_call | solution.py:120
  373.5 16.6 %text_backward.6 = (bf16[344,768]{1,0:T(8,128)(2,1)}, bf16[344,768]{1,0:T(8,128)(2,1)}, bf16[2,344,768]{2,1,0:T(8,128)(2,1)}, bf16[2,576,192]{2,1,0:T(8,128)(2,1...) custom-call(s32[1]{0:T(128)} %constant.32.clone.1.tick, s32[54]{0:T(128)} %concatenate.15.info, ...), custom_call_target="tpu_custom_call" | custom-call | flops 7903641600 | bytes 8527872 | tf_op jit(solution)/shard_map/text_backward/pallas_call | solution.py:120
  405.4 16.4 %text_backward.7 = (bf16[344,768]{1,0:T(8,128)(2,1)}, bf16[344,768]{1,0:T(8,128)(2,1)}, bf16[2,344,768]{2,1,0:T(8,128)(2,1)}, bf16[2,576,192]{2,1,0:T(8,128)(2,1...) custom-call(s32[1]{0:T(128)} %constant.84.clone.1.tick, ...), custom_call_target="tpu_custom_call", output_to_operand_aliasing={{4}: (12, {}), {5}: (13, {})} | custom-call | flops 7903641600 | bytes 8527872 | tf_op jit(solution)/shard_map/text_backward/pallas_call | solution.py:120
  484.8 16.4 %text_backward.8 = (bf16[344,768]{1,0:T(8,128)(2,1)}, bf16[344,768]{1,0:T(8,128)(2,1)}, bf16[2,344,768]{2,1,0:T(8,128)(2,1)}, bf16[2,576,192]{2,1,0:T(8,128)(2,1...) custom-call(s32[1]{0:T(128)} %constant.71.clone.1.tick, ...), custom_call_target="tpu_custom_call", output_to_operand_aliasing={{4}: (12, {}), {5}: (13, {})} | custom-call | flops 7903641600 | bytes 8527872 | tf_op jit(solution)/shard_map/text_backward/pallas_call | solution.py:120
  516.6 16.7 %text_backward.9 = (bf16[344,768]{1,0:T(8,128)(2,1)}, bf16[344,768]{1,0:T(8,128)(2,1)}, bf16[2,344,768]{2,1,0:T(8,128)(2,1)}, bf16[2,576,192]{2,1,0:T(8,128)(2,1...) custom-call(s32[1]{0:T(128)} %constant.83.clone.1.tick, ...), custom_call_target="tpu_custom_call", output_to_operand_aliasing={{4}: (12, {}), {5}: (13, {})} | custom-call | flops 7903641600 | bytes 8527872 | tf_op jit(solution)/shard_map/text_backward/pallas_call | solution.py:120
  594.7 16.6 %text_backward.10 = (bf16[344,768]{1,0:T(8,128)(2,1)}, bf16[344,768]{1,0:T(8,128)(2,1)}, bf16[2,344,768]{2,1,0:T(8,128)(2,1)}, bf16[2,576,192]{2,1,0:T(8,128)(2,...) custom-call(s32[1]{0:T(128)} %constant.72.clone.1.tick, ...), custom_call_target="tpu_custom_call", output_to_operand_aliasing={{4}: (12, {}), {5}: (13, {})} | custom-call | flops 7903641600 | bytes 8527872 | tf_op jit(solution)/shard_map/text_backward/pallas_call | solution.py:120
  614.1 16.4 %text_backward.11 = (bf16[344,768]{1,0:T(8,128)(2,1)}, bf16[344,768]{1,0:T(8,128)(2,1)}, bf16[2,344,768]{2,1,0:T(8,128)(2,1)}, bf16[2,576,192]{2,1,0:T(8,128)(2,...) custom-call(s32[1]{0:T(128)} %constant.74.clone.1.tick, ...), custom_call_target="tpu_custom_call", output_to_operand_aliasing={{4}: (12, {}), {5}: (13, {})} | custom-call | flops 7903641600 | bytes 8527872 | tf_op jit(solution)/shard_map/text_backward/pallas_call | solution.py:120
  630.5 13.8 %ff_weights.2 = (bf16[4,384,768]{2,1,0:T(8,128)(2,1)}, bf16[4,384,768]{2,1,0:T(8,128)(2,1)}) custom-call(bf16[1720,768]{1,0:T(8,128)(2,1)} %get-tuple-element.651.h2, bf16[1720,768]{1,0:T(8,128)(2,1)} %get-tuple-element.654.dm, bf16[1720,3072]{1,0:T(8,128)(2,1)} %get-tuple-element.690.du, bf16[1720,3072]{1,0:T(8,128)(2,1)} %get-tuple-element.656.g), custom_call_target="tpu_custom_call" | custom-call | flops 6492782592 | bytes 17399808 | tf_op jit(solution)/shard_map/ff_weights/pallas_call | solution.py:899
  644.5 13.1 %text_weights.1 = bf16[4,288,768]{2,1,0:T(8,128)(2,1)} custom-call(bf16[5,800,768]{2,1,0:T(8,128)(2,1)} %get-tuple-element.658.h, bf16[5,800,768]{2,1,0:T(8,128)(2,1)} %get-tuple-element.659.dd, bf16[5,800,384]{2,1,0:T(8,128)(2,1)} %get-tuple-element.660.o, bf16[5,800,768]{2,1,0:T(8,128)(2,1)} %get-tuple-element.661.da), custom_call_target="tpu_custom_call" | custom-call | flops 7077888000 | bytes 21504000 | tf_op jit(solution)/shard_map/text_weights/pallas_call | solution.py:656
  684.6 11.4 %image_weights.1 = bf16[4,240,960]{2,1,0:T(8,128)(2,1)} custom-call(bf16[5,576,768]{2,1,0:T(8,128)(2,1)} %get-tuple-element.686.h, bf16[5,576,960]{2,1,0:T(8,128)(2,1)} %get-tuple-element.687.dd, bf16[5,576,192]{2,1,0:T(8,128)(2,1)} %get-tuple-element.688.o, bf16[5,576,768]{2,1,0:T(8,128)(2,1)} %get-tuple-element.689.da), custom_call_target="tpu_custom_call" | custom-call | flops 5096079360 | bytes 15482880 | tf_op jit(solution)/shard_map/image_weights/pallas_call | solution.py:656
  697.2 11.9 %collective-permute-done.77 = bf16[4,96,768]{2,1,0:T(8,128)(2,1)} collective-permute-done((bf16[4,96,768]{2,1,0:T(8,128)(2,1)}, bf16[4,96,768]{2,1,0:T(8,128)(2,1)}, u32[]{:S(2)}, u32[]{:S(2)}) %collective-permute-start.77) | collective-permute-done | bytes 589856 | tf_op jit(solution)/shard_map/ppermute | solution.py:998
  709.2 13.9 %ff_weights.3 = (bf16[4,384,768]{2,1,0:T(8,128)(2,1)}, bf16[4,384,768]{2,1,0:T(8,128)(2,1)}) custom-call(bf16[1720,768]{1,0:T(8,128)(2,1)} %get-tuple-element.651.h2, bf16[1720,768]{1,0:T(8,128)(2,1)} %get-tuple-element.654.dm, bf16[1720,3072]{1,0:T(8,128)(2,1)} %get-tuple-element.690.du, bf16[1720,3072]{1,0:T(8,128)(2,1)} %get-tuple-element.656.g), custom_call_target="tpu_custom_call" | custom-call | flops 6492782592 | bytes 17399808 | tf_op jit(solution)/shard_map/ff_weights/pallas_call | solution.py:899
  724.0 14.8 %collective-permute-done.73 = bf16[4,96,768]{2,1,0:T(8,128)(2,1)S(1)} collective-permute-done((bf16[4,96,768]{2,1,0:T(8,128)(2,1)S(1)}, bf16[4,96,768]{2,1,0:T(8,128)(2,1)S(1)}, u32[]{:S(2)}, u32[]{:S(2)}) %collective-permute-start.73) | collective-permute-done | bytes 589856 | tf_op jit(solution)/shard_map/ppermute | solution.py:998
  745.5 12.8 %collective-permute-done.75.c = bf16[344,768]{1,0:T(8,128)(2,1)S(1)} collective-permute-done((bf16[344,768]{1,0:T(8,128)(2,1)S(1)}, bf16[344,768]{1,0:T(8,128)(2,1)S(1)}, u32[]{:S(2)}, u32[]{:S(2)}) %collective-permute-start.75) | collective-permute-done | bytes 528416 | tf_op jit(solution)/shard_map/ppermute | solution.py:998
  (465 shorter events, 470.3 us)
Async XLA Ops:
  7.2 82.0 %all-gather.2.cloned.1.call-start = ((), (), s32[]{:S(2)}) async-start(), calls=%async_computation.3 | async-start | bytes 1474560 | tf_op jit(solution)/shard_map/all_gather | solution.py:1128
  16.4 22.7 %collective-permute-start.1 = (bf16[344,768]{1,0:T(8,128)(2,1)}, bf16[344,768]{1,0:T(8,128)(2,1)}, u32[]{:S(2)}, u32[]{:S(2)}) collective-permute-start(bf16[344,768]{1,0:T(8,128)(2,1)} %get-tuple-element.364.p0), channel_id=1, source_target_pairs={{0,1},{1,0},{2,3},{3,2},{4,5},{5,4},{6,7},{7,6},{8,9},{9,8},{10,11... | collective-permute-start | bytes 1585160 | tf_op jit(solution)/shard_map/ppermute | solution.py:1002
  19.6 39.4 %collective-permute-start.11 = (bf16[344,768]{1,0:T(8,128)(2,1)}, bf16[344,768]{1,0:T(8,128)(2,1)}, u32[]{:S(2)}, u32[]{:S(2)}) collective-permute-start(bf16[344,768]{1,0:T(8,128)(2,1)} %get-tuple-element.381.p0), channel_id=1, source_target_pairs={{0,2},{1,3},{2,0},{3,1},{4,6},{5,7},{6,4},{7,5},{8,10},{9,11},{10,... | collective-permute-start | bytes 1585160 | tf_op jit(solution)/shard_map/ppermute | solution.py:998
  37.0 20.5 %collective-permute-start.8 = (bf16[192,768]{1,0:T(8,128)(2,1)S(1)}, bf16[192,768]{1,0:T(8,128)(2,1)S(1)}, u32[]{:S(2)}, u32[]{:S(2)}) collective-permute-start(bf16[192,768]{1,0:T(8,128)(2,1)S(1)} %constant_dynamic-slice_fusion), channel_id=1, source_target_pairs={{0,2},{1,3},{2,0},{3,1},{4,6},{5,7},{6,4},{7,5},{8,10},{9,11},{10,... | collective-permute-start | bytes 884744 | tf_op jit(solution)/shard_map/ppermute | solution.py:998
  58.2 718.2 %reduce-scatter.6.cloned.1.call-start = ((), (), s32[]{:S(2)}) async-start(), calls=%async_computation.5 | async-start | bytes 2211840 | tf_op jit(solution)/shard_map/reduce_scatter | solution.py:1262
  59.3 28.1 %collective-permute-start.5 = (bf16[768,768]{1,0:T(8,128)(2,1)S(1)}, bf16[768,768]{1,0:T(8,128)(2,1)S(1)}, u32[]{:S(2)}, u32[]{:S(2)}) collective-permute-start(bf16[768,768]{1,0:T(8,128)(2,1)S(1)} %bitcast.122), channel_id=1, source_target_pairs={{0,2},{1,3},{2,0},{3,1},{4,6},{5,7},{6,4},{7,5},{8,10},{9,11},{10,... | collective-permute-start | bytes 3538952 | tf_op jit(solution)/shard_map/ppermute | solution.py:998
  59.4 28.0 %collective-permute-start.3 = (bf16[2,344,768]{2,1,0:T(8,128)(2,1)}, bf16[2,344,768]{2,1,0:T(8,128)(2,1)}, u32[]{:S(2)}, u32[]{:S(2)}) collective-permute-start(bf16[2,344,768]{2,1,0:T(8,128)(2,1)} %get-tuple-element.373), channel_id=1, source_target_pairs={{0,1},{1,0},{2,3},{3,2},{4,5},{5,4},{6,7},{7,6},{8,9},{9,8},{10,11... | collective-permute-start | bytes 3170312 | tf_op jit(solution)/shard_map/ppermute | solution.py:1002
  87.4 18.0 %collective-permute-start.7 = (bf16[768,768]{1,0:T(8,128)(2,1)S(1)}, bf16[768,768]{1,0:T(8,128)(2,1)}, u32[]{:S(2)}, u32[]{:S(2)}) collective-permute-start(bf16[768,768]{1,0:T(8,128)(2,1)S(1)} %collective-permute-done.5.u1), channel_id=1, source_target_pairs={{0,1},{1,0},{2,3},{3,2},{4,5},{5,4},{6,7},{7,6},{8,9},{9,8},{10,11... | collective-permute-start | bytes 3538952 | tf_op jit(solution)/shard_map/ppermute | solution.py:1002
  93.3 27.4 %collective-permute-start.15 = (bf16[344,768]{1,0:T(8,128)(2,1)S(1)}, bf16[344,768]{1,0:T(8,128)(2,1)S(1)}, u32[]{:S(2)}, u32[]{:S(2)}) collective-permute-start(bf16[344,768]{1,0:T(8,128)(2,1)S(1)} %fusion.10), channel_id=1, source_target_pairs={{0,2},{1,3},{2,0},{3,1},{4,6},{5,7},{6,4},{7,5},{8,10},{9,11},{10,... | collective-permute-start | bytes 1585160 | tf_op jit(solution)/shard_map/ppermute | solution.py:998
  154.9 20.7 %collective-permute-start.23 = (bf16[344,768]{1,0:T(8,128)(2,1)}, bf16[344,768]{1,0:T(8,128)(2,1)S(1)}, u32[]{:S(2)}, u32[]{:S(2)}) collective-permute-start(bf16[344,768]{1,0:T(8,128)(2,1)} %get-tuple-element.424.p0), channel_id=1, source_target_pairs={{0,2},{1,3},{2,0},{3,1},{4,6},{5,7},{6,4},{7,5},{8,10},{9,11},{10,... | collective-permute-start | bytes 1585160 | tf_op jit(solution)/shard_map/ppermute | solution.py:998
  203.5 27.2 %collective-permute-start.27 = (bf16[344,768]{1,0:T(8,128)(2,1)S(1)}, bf16[344,768]{1,0:T(8,128)(2,1)S(1)}, u32[]{:S(2)}, u32[]{:S(2)}) collective-permute-start(bf16[344,768]{1,0:T(8,128)(2,1)S(1)} %fusion.8), channel_id=1, source_target_pairs={{0,2},{1,3},{2,0},{3,1},{4,6},{5,7},{6,4},{7,5},{8,10},{9,11},{10,... | collective-permute-start | bytes 1585160 | tf_op jit(solution)/shard_map/ppermute | solution.py:998
  264.5 20.9 %collective-permute-start.30 = (bf16[344,768]{1,0:T(8,128)(2,1)}, bf16[344,768]{1,0:T(8,128)(2,1)S(1)}, u32[]{:S(2)}, u32[]{:S(2)}) collective-permute-start(bf16[344,768]{1,0:T(8,128)(2,1)} %get-tuple-element.461.p0), channel_id=1, source_target_pairs={{0,2},{1,3},{2,0},{3,1},{4,6},{5,7},{6,4},{7,5},{8,10},{9,11},{10,... | collective-permute-start | bytes 1585160 | tf_op jit(solution)/shard_map/ppermute | solution.py:998
  313.3 22.0 %collective-permute-start.38 = (bf16[344,768]{1,0:T(8,128)(2,1)S(1)}, bf16[344,768]{1,0:T(8,128)(2,1)S(1)}, u32[]{:S(2)}, u32[]{:S(2)}) collective-permute-start(bf16[344,768]{1,0:T(8,128)(2,1)S(1)} %fusion.6), channel_id=1, source_target_pairs={{0,2},{1,3},{2,0},{3,1},{4,6},{5,7},{6,4},{7,5},{8,10},{9,11},{10,... | collective-permute-start | bytes 1585160 | tf_op jit(solution)/shard_map/ppermute | solution.py:998
  370.8 19.3 %collective-permute-start.40 = (bf16[344,768]{1,0:T(8,128)(2,1)}, bf16[344,768]{1,0:T(8,128)(2,1)S(1)}, u32[]{:S(2)}, u32[]{:S(2)}) collective-permute-start(bf16[344,768]{1,0:T(8,128)(2,1)} %get-tuple-element.513.p0), channel_id=1, source_target_pairs={{0,2},{1,3},{2,0},{3,1},{4,6},{5,7},{6,4},{7,5},{8,10},{9,11},{10,... | collective-permute-start | bytes 1585160 | tf_op jit(solution)/shard_map/ppermute | solution.py:998
  482.1 19.1 %collective-permute-start.52 = (bf16[344,768]{1,0:T(8,128)(2,1)}, bf16[344,768]{1,0:T(8,128)(2,1)S(1)}, u32[]{:S(2)}, u32[]{:S(2)}) collective-permute-start(bf16[344,768]{1,0:T(8,128)(2,1)} %get-tuple-element.573.p0), channel_id=1, source_target_pairs={{0,2},{1,3},{2,0},{3,1},{4,6},{5,7},{6,4},{7,5},{8,10},{9,11},{10,... | collective-permute-start | bytes 1585160 | tf_op jit(solution)/shard_map/ppermute | solution.py:998
  592.0 19.5 %collective-permute-start.68 = (bf16[344,768]{1,0:T(8,128)(2,1)}, bf16[344,768]{1,0:T(8,128)(2,1)S(1)}, u32[]{:S(2)}, u32[]{:S(2)}) collective-permute-start(bf16[344,768]{1,0:T(8,128)(2,1)} %get-tuple-element.627.p0), channel_id=1, source_target_pairs={{0,1},{1,0},{2,3},{3,2},{4,5},{5,4},{6,7},{7,6},{8,9},{9,8},{10,11... | collective-permute-start | bytes 1585160 | tf_op jit(solution)/shard_map/ppermute | solution.py:1002
  592.5 18.8 %collective-permute-start.64 = (bf16[344,768]{1,0:T(8,128)(2,1)}, bf16[344,768]{1,0:T(8,128)(2,1)S(1)}, u32[]{:S(2)}, u32[]{:S(2)}) collective-permute-start(bf16[344,768]{1,0:T(8,128)(2,1)} %get-tuple-element.627.p0), channel_id=1, source_target_pairs={{0,2},{1,3},{2,0},{3,1},{4,6},{5,7},{6,4},{7,5},{8,10},{9,11},{10,... | collective-permute-start | bytes 1585160 | tf_op jit(solution)/shard_map/ppermute | solution.py:998
  644.3 22.2 %collective-permute-start.70 = (bf16[4,384,768]{2,1,0:T(8,128)(2,1)}, bf16[4,384,768]{2,1,0:T(8,128)(2,1)S(1)}, u32[]{:S(2)}, u32[]{:S(2)}) collective-permute-start(bf16[4,384,768]{2,1,0:T(8,128)(2,1)} %get-tuple-element.657), channel_id=1, source_target_pairs={{0,1},{1,0},{2,3},{3,2},{4,5},{5,4},{6,7},{7,6},{8,9},{9,8},{10,11... | collective-permute-start | bytes 7077896 | tf_op jit(solution)/shard_map/ppermute | solution.py:1002
  657.7 132.2 %reduce-scatter.4.cloned.1.call-start = ((), (), s32[]{:S(2)}) async-start(), calls=%async_computation.4 | async-start | bytes 2457600 | tf_op jit(solution)/shard_map/reduce_scatter | solution.py:1262
  677.3 19.0 %collective-permute-start.71 = (bf16[2,344,768]{2,1,0:T(8,128)(2,1)}, bf16[2,344,768]{2,1,0:T(8,128)(2,1)S(1)}, u32[]{:S(2)}, u32[]{:S(2)}) collective-permute-start(bf16[2,344,768]{2,1,0:T(8,128)(2,1)} %get-tuple-element.675), channel_id=1, source_target_pairs={{0,1},{1,0},{2,3},{3,2},{4,5},{5,4},{6,7},{7,6},{8,9},{9,8},{10,11... | collective-permute-start | bytes 3170312 | tf_op jit(solution)/shard_map/ppermute | solution.py:1002
  678.5 44.5 %collective-permute-start.78 = (bf16[4,96,768]{2,1,0:T(8,128)(2,1)}, bf16[4,96,768]{2,1,0:T(8,128)(2,1)}, u32[]{:S(2)}, u32[]{:S(2)}) collective-permute-start(bf16[4,96,768]{2,1,0:T(8,128)(2,1)} %get-tuple-element.743), channel_id=1, source_target_pairs={{0,2},{1,3},{2,0},{3,1},{4,6},{5,7},{6,4},{7,5},{8,10},{9,11},{10,... | collective-permute-start | bytes 1769480 | tf_op jit(solution)/shard_map/ppermute | solution.py:998
  679.7 29.5 %collective-permute-start.77 = (bf16[4,96,768]{2,1,0:T(8,128)(2,1)}, bf16[4,96,768]{2,1,0:T(8,128)(2,1)}, u32[]{:S(2)}, u32[]{:S(2)}) collective-permute-start(bf16[4,96,768]{2,1,0:T(8,128)(2,1)} %get-tuple-element.744), channel_id=1, source_target_pairs={{0,2},{1,3},{2,0},{3,1},{4,6},{5,7},{6,4},{7,5},{8,10},{9,11},{10,... | collective-permute-start | bytes 1769480 | tf_op jit(solution)/shard_map/ppermute | solution.py:998
  696.1 98.1 %reduce-scatter.8.cloned.1.call-start = ((), (), s32[]{:S(2)}) async-start(), calls=%async_computation.6 | async-start | bytes 2949120 | tf_op jit(solution)/shard_map/reduce_scatter | solution.py:1262
  744.2 24.0 %collective-permute-start.72 = (bf16[344,768]{1,0:T(8,128)(2,1)S(1)}, bf16[344,768]{1,0:T(8,128)(2,1)S(1)}, u32[]{:S(2)}, u32[]{:S(2)}) collective-permute-start(bf16[344,768]{1,0:T(8,128)(2,1)S(1)} %fusion.1), channel_id=1, source_target_pairs={{0,2},{1,3},{2,0},{3,1},{4,6},{5,7},{6,4},{7,5},{8,10},{9,11},{10,... | collective-permute-start | bytes 1585160 | tf_op jit(solution)/shard_map/ppermute | solution.py:998
  (164 other events, 1142.3 us)
Sparse Core Ops, SparseCore 0:
  58.4 30.7 all-gather.1
  657.8 37.7 reduce-scatter.5
  698.0 40.5 reduce-scatter.3
  742.5 47.9 reduce-scatter.7
